TPU v7x, 32 devices: a whole 2x2x4 slice. The times are simulated.
32 devices in a mesh: seq: 2 (over x), head: 4 (over y, core), fsdp: 4 (over z).
Axes of the slice: x: 2, y: 2, z: 4, core: 2. Of those that a mesh axis runs over, the one named last changes fastest.
Arguments:
- block_input: bfloat16 [3, 4, 1024, 1024], P(None, 'fsdp', 'seq'), may hold values from -6 to 6
- cotangent: bfloat16 [3, 4, 1024, 1024], P(None, 'fsdp', 'seq'), may hold values from -6 to 6
- doc_lengths: int32 [3, 4, 8], P(None, 'fsdp'), may hold values from 1 to 512, as said below
- attn_gain: float32 [1024], replicated, may hold values from 0.25 to 1.75
- w_query: bfloat16 [1024, 1024], P('fsdp', 'head'), may hold values from -0.1875 to 0.1875
- w_key: bfloat16 [1024, 1024], P('fsdp', 'head'), may hold values from -0.1875 to 0.1875
- w_value: bfloat16 [1024, 2048], P('fsdp', 'head'), may hold values from -0.1875 to 0.1875
- w_gate: bfloat16 [1024, 2048], P('fsdp', 'head'), may hold values from -0.1875 to 0.1875
- w_alpha: bfloat16 [1024, 8], P('fsdp', 'head'), may hold values from -0.1875 to 0.1875
- w_beta: bfloat16 [1024, 8], P('fsdp', 'head'), may hold values from -0.1875 to 0.1875
- conv_query: float32 [4, 1024], replicated, may hold values from -3 to 3
- conv_key: float32 [4, 1024], replicated, may hold values from -3 to 3
- conv_value: float32 [4, 2048], replicated, may hold values from -3 to 3
- a_log: float32 [8], replicated, may hold values from -6 to 0
- dt_bias: float32 [8], replicated, may hold values from -3 to -1
- head_gain: float32 [256], replicated, may hold values from 0.25 to 1.75
- w_out: bfloat16 [2048, 1024], P('head', 'fsdp'), may hold values from -0.125 to 0.125
- mlp_gain: float32 [1024], replicated, may hold values from 0.25 to 1.75
- w_ffgate: bfloat16 [1024, 2816], P('fsdp', 'head'), may hold values from -0.1875 to 0.1875
- w_ffup: bfloat16 [1024, 2816], P('fsdp', 'head'), may hold values from -0.1875 to 0.1875
- w_down: bfloat16 [2816, 1024], P('head', 'fsdp'), may hold values from -0.109375 to 0.109375
Outputs:
- block_output: bfloat16 [3, 4, 1024, 1024], P(None, 'fsdp', ('seq', 'head'))
- input_grad: float32 [3, 4, 1024, 1024], P(None, 'fsdp', ('seq', 'head'))
- grad_w_query: float32 [1024, 1024], P(('seq', 'fsdp'), 'head')
- grad_w_key: float32 [1024, 1024], P(('seq', 'fsdp'), 'head')
- grad_w_value: float32 [1024, 2048], P(('seq', 'fsdp'), 'head')
- grad_w_gate: float32 [1024, 2048], P(('seq', 'fsdp'), 'head')
- grad_w_alpha: float32 [1024, 8], P(('seq', 'fsdp'), 'head')
- grad_w_beta: float32 [1024, 8], P(('seq', 'fsdp'), 'head')
- grad_w_out: float32 [2048, 1024], P('head', ('seq', 'fsdp'))
- grad_w_ffgate: float32 [1024, 2816], P(('seq', 'fsdp'), 'head')
- grad_w_ffup: float32 [1024, 2816], P(('seq', 'fsdp'), 'head')
- grad_w_down: float32 [2816, 1024], P('head', ('seq', 'fsdp'))
- grad_attn_gain: float32 [1024], replicated
- grad_mlp_gain: float32 [1024], replicated
- grad_head_gain: float32 [256], replicated
- grad_conv_query: float32 [4, 1024], replicated
- grad_conv_key: float32 [4, 1024], replicated
- grad_conv_value: float32 [4, 2048], replicated
- grad_a_log: float32 [8], replicated
- grad_dt_bias: float32 [8], replicated
Inputs may be any that keep to these rules, and one draw needn't show every extreme that they name: `doc_lengths`: each row holds the 8 document lengths of one sequence in order, summing to 1024. Exactly one document, never the first or the last, has 512 tokens; the others share 512 tokens.
All inputs are finite; a program needn't handle non-finite values.
Results may differ from a plain program's by a relative error of at most 0.014.
Values may be sent and summed in bfloat16 or wider, within the bound.
No kernel may reach another device: no remote copies, remote signals or barrier semaphores. Data moves between devices by JAX's collectives and lax.ppermute only.
A program may use at most 256 MiB of HBM per device.

v0:
```python
import math

import jax
import jax.numpy as jnp
from jax import lax
from jax.sharding import PartitionSpec as P

DK = 128
DV = 256
KCONV = 4
STRETCH = 64
MB = 3


BEST_PRECISION = lax.Precision.HIGHEST


def passed_along(block, axis, distance):
    devices = range(lax.axis_size(axis))
    route = [(i - distance, i) for i in devices if i - distance in devices]
    return lax.ppermute(block, axis, route)


def prefix(x, axis, combine, identity, reverse):
    devices, place = (lax.axis_size(axis), lax.axis_index(axis))
    everything = jax.tree.map(lambda part: lax.all_gather(part, axis), x)
    start = jax.tree.map(
        lambda part, zero: jnp.broadcast_to(jnp.asarray(zero, part.dtype), part.shape), x, identity
    )

    def turn(k, before):
        at = devices - 1 - k if reverse else k
        reached = at > place if reverse else at < place
        new = combine(before, jax.tree.map(lambda part: part[at], everything))
        return jax.tree.map(lambda a, b: jnp.where(reached, a, b), new, before)

    return lax.fori_loop(0, devices, turn, start)


def rms_rows(values, gain_vec):
    return values * lax.rsqrt(jnp.mean(values * values, axis=-1, keepdims=True) + 1e-05) * gain_vec


def l2_rows(values):
    return values * lax.rsqrt(jnp.sum(values * values, axis=-1, keepdims=True) + 1e-06)


def short_conv(padded, filters, doc_pad):
    tok_count = padded.shape[0] - KCONV + 1
    own_doc = doc_pad[KCONV - 1 :]
    total = jnp.zeros((tok_count, padded.shape[1]), jnp.float32)
    for offset in range(KCONV):
        window = padded[offset : offset + tok_count]
        keep_mask = (doc_pad[offset : offset + tok_count] == own_doc)[:, None]
        total = total + jnp.where(keep_mask, window, 0.0) * filters[offset]
    return jax.nn.silu(total)


def mixer_inputs(
    q_pad,
    k_pad,
    v_pad,
    alpha_logit,
    beta_logit,
    conv_q,
    conv_k,
    conv_v,
    alog_vec,
    bias_vec,
    doc_pad,
):
    tok_count = alpha_logit.shape[0]
    head_count = alpha_logit.shape[1]
    q_conv = short_conv(q_pad, conv_q, doc_pad).reshape(tok_count, head_count, DK)
    k_conv = short_conv(k_pad, conv_k, doc_pad).reshape(tok_count, head_count, DK)
    v_conv = short_conv(v_pad, conv_v, doc_pad).reshape(tok_count, head_count, DV)
    queries = l2_rows(q_conv) * (1.0 / math.sqrt(DK))
    key_vecs = l2_rows(k_conv)
    beta_rate = jax.nn.sigmoid(beta_logit)
    log_decay = -jnp.exp(alog_vec) * jax.nn.softplus(alpha_logit + bias_vec)
    return (queries, key_vecs, v_conv, beta_rate, log_decay)


def stretch_step(running, block_in):
    state_mat, prior_doc = running
    queries, key_vecs, value_vecs, beta_rate, log_decay, doc_ids = block_in
    block_len = queries.shape[0]
    cumulative = jnp.cumsum(log_decay)
    row_ids = jnp.arange(block_len)[:, None]
    col_ids = jnp.arange(block_len)[None, :]
    same_doc = doc_ids[:, None] == doc_ids[None, :]
    decay_mat = jnp.where(
        same_doc & (row_ids >= col_ids),
        jnp.exp(jnp.minimum(cumulative[:, None] - cumulative[None, :], 0.0)),
        0.0,
    )
    reach = jnp.where(doc_ids == prior_doc, jnp.exp(cumulative), 0.0)
    strict_mat = jnp.where(row_ids > col_ids, decay_mat, 0.0)
    key_gram = jnp.dot(key_vecs, key_vecs.T, precision=BEST_PRECISION)
    lower_mat = jnp.eye(block_len, dtype=jnp.float32) + beta_rate[:, None] * strict_mat * key_gram
    from_state = jnp.dot(key_vecs, state_mat, precision=BEST_PRECISION)
    pseudo = jax.scipy.linalg.solve_triangular(
        lower_mat,
        beta_rate[:, None] * (value_vecs - reach[:, None] * from_state),
        lower=True,
        unit_diagonal=True,
    )
    scores = jnp.dot(queries, key_vecs.T, precision=BEST_PRECISION)
    outputs = reach[:, None] * jnp.dot(queries, state_mat, precision=BEST_PRECISION) + jnp.dot(
        decay_mat * scores, pseudo, precision=BEST_PRECISION
    )
    tail = jnp.where(doc_ids == doc_ids[-1], jnp.exp(cumulative[-1] - cumulative), 0.0)
    new_state = reach[-1] * state_mat + jnp.dot(
        key_vecs.T, tail[:, None] * pseudo, precision=BEST_PRECISION
    )
    return ((new_state, doc_ids[-1]), outputs)


def run_head(queries, key_vecs, value_vecs, beta_rate, log_decay, doc_ids, state_mat, prior_doc):
    tok_count = queries.shape[0]
    n_blocks = tok_count // STRETCH

    def split_blocks(member):
        return member.reshape((n_blocks, STRETCH) + member.shape[1:])

    pieces = tuple(
        (
            split_blocks(member)
            for member in (queries, key_vecs, value_vecs, beta_rate, log_decay, doc_ids)
        )
    )
    (final_state, last_doc), outputs = lax.scan(
        jax.checkpoint(stretch_step), (state_mat, prior_doc), pieces
    )
    return (final_state, outputs.reshape(tok_count, value_vecs.shape[-1]))


def gate_out(o_heads, gate_vals, gain_vec):
    tok_count = o_heads.shape[0]
    head_count = o_heads.shape[1]
    normed = rms_rows(o_heads, gain_vec) * jax.nn.silu(gate_vals.reshape(tok_count, head_count, DV))
    return normed.reshape(tok_count, head_count * DV)


def swiglu(gate_vals, up_vals):
    return jax.nn.silu(gate_vals) * up_vals


def matmul(left, right):
    return jnp.dot(left, right, preferred_element_type=jnp.float32)


def matmul_bt(left, right):
    return lax.dot_general(
        left, right, (((1,), (1,)), ((), ())), preferred_element_type=jnp.float32
    )


def matmul_at(left, right):
    return lax.dot_general(
        left, right, (((0,), (0,)), ((), ())), preferred_element_type=jnp.float32
    )


def combine_forward(earlier, later):
    trans_early, offset_early = earlier
    trans_late, offset_late = later
    trans_new = jnp.einsum("hij,hjk->hik", trans_late, trans_early, precision=BEST_PRECISION)
    offset_new = (
        jnp.einsum("hij,hjv->hiv", trans_late, offset_early, precision=BEST_PRECISION) + offset_late
    )
    return (trans_new, offset_new)


def combine_backward(earlier, later):
    trans_early, grad_early = earlier
    trans_late, grad_late = later
    trans_new = jnp.einsum("hij,hjk->hik", trans_early, trans_late, precision=BEST_PRECISION)
    grad_new = (
        jnp.einsum("hji,hjv->hiv", trans_late, grad_early, precision=BEST_PRECISION) + grad_late
    )
    return (trans_new, grad_new)


def send_grads(parts):
    return (
        lax.psum_scatter(parts[0], ("seq", "fsdp"), scatter_dimension=0, tiled=True),
        lax.psum_scatter(parts[1], ("seq", "fsdp"), scatter_dimension=0, tiled=True),
        lax.psum_scatter(parts[2], ("seq", "fsdp"), scatter_dimension=0, tiled=True),
        lax.psum_scatter(parts[3], ("seq", "fsdp"), scatter_dimension=0, tiled=True),
        lax.psum_scatter(parts[4], ("seq", "fsdp"), scatter_dimension=0, tiled=True),
        lax.psum_scatter(parts[5], ("seq", "fsdp"), scatter_dimension=0, tiled=True),
        lax.psum_scatter(parts[6], ("seq", "fsdp"), scatter_dimension=1, tiled=True),
        lax.psum_scatter(parts[7], ("seq", "fsdp"), scatter_dimension=0, tiled=True),
        lax.psum_scatter(parts[8], ("seq", "fsdp"), scatter_dimension=0, tiled=True),
        lax.psum_scatter(parts[9], ("seq", "fsdp"), scatter_dimension=1, tiled=True),
    )


def add_tuples(first_tuple, second_tuple):
    return tuple((one_part + other_part for one_part, other_part in zip(first_tuple, second_tuple)))


def per_device(
    block_input,
    cotangent,
    doc_lengths,
    attn_gain,
    w_query,
    w_key,
    w_value,
    w_gate,
    w_alpha,
    w_beta,
    conv_query,
    conv_key,
    conv_value,
    a_log,
    dt_bias,
    head_gain,
    w_out,
    mlp_gain,
    w_ffgate,
    w_ffup,
    w_down,
):
    head_devices = lax.axis_size("head")
    seq_place = lax.axis_index("seq")
    head_place = lax.axis_index("head")
    tok_count = block_input.shape[2]
    row_count = tok_count // head_devices
    row_first = head_place * row_count
    heads_here = w_query.shape[1] // DK
    query_width = heads_here * DK
    value_width = heads_here * DV
    conv_q_here = lax.dynamic_slice_in_dim(conv_query, head_place * query_width, query_width, 1)
    conv_k_here = lax.dynamic_slice_in_dim(conv_key, head_place * query_width, query_width, 1)
    conv_v_here = lax.dynamic_slice_in_dim(conv_value, head_place * value_width, value_width, 1)
    alog_here = lax.dynamic_slice_in_dim(a_log, head_place * heads_here, heads_here, 0)
    bias_here = lax.dynamic_slice_in_dim(dt_bias, head_place * heads_here, heads_here, 0)
    eye_block = jnp.broadcast_to(jnp.eye(DK, dtype=jnp.float32), (heads_here, DK, DK))
    zero_offset = jnp.zeros((heads_here, DK, DV), jnp.float32)
    weight_sums = None
    small_sums = None
    y_blocks = []
    dx_blocks = []
    for micro in range(MB):
        gathered = (
            lax.all_gather(w_query, "fsdp", axis=0, tiled=True),
            lax.all_gather(w_key, "fsdp", axis=0, tiled=True),
            lax.all_gather(w_value, "fsdp", axis=0, tiled=True),
            lax.all_gather(w_gate, "fsdp", axis=0, tiled=True),
            lax.all_gather(w_alpha, "fsdp", axis=0, tiled=True),
            lax.all_gather(w_beta, "fsdp", axis=0, tiled=True),
            lax.all_gather(w_out, "fsdp", axis=1, tiled=True),
            lax.all_gather(w_ffgate, "fsdp", axis=0, tiled=True),
            lax.all_gather(w_ffup, "fsdp", axis=0, tiled=True),
            lax.all_gather(w_down, "fsdp", axis=1, tiled=True),
        )
        (
            wq_full,
            wk_full,
            wv_full,
            wg_full,
            wa_full,
            wb_full,
            wo_full,
            wfg_full,
            wfu_full,
            wd_full,
        ) = gathered
        x_here = block_input[micro, 0].astype(jnp.float32)
        cot_here = cotangent[micro, 0]
        doc_ends = jnp.cumsum(doc_lengths[micro, 0])
        positions = seq_place * tok_count + jnp.arange(1 - KCONV, tok_count, dtype=jnp.int32)
        doc_pad = jnp.sum((positions[:, None] >= doc_ends[None, :]).astype(jnp.int32), axis=1)
        doc_pad = jnp.where(positions < 0, -1, doc_pad)
        doc_ids = doc_pad[KCONV - 1 :]
        prior_doc = doc_pad[KCONV - 2]
        h_one = rms_rows(x_here, attn_gain).astype(jnp.bfloat16)
        q_pre = matmul(h_one, wq_full).astype(jnp.bfloat16)
        k_pre = matmul(h_one, wk_full).astype(jnp.bfloat16)
        v_pre = matmul(h_one, wv_full).astype(jnp.bfloat16)
        gate_vals = matmul(h_one, wg_full)
        alpha_logit = matmul(h_one, wa_full)
        beta_logit = matmul(h_one, wb_full)
        edge = tok_count - KCONV + 1
        rims = passed_along((q_pre[edge:], k_pre[edge:], v_pre[edge:]), "seq", 1)
        q_pad = jnp.concatenate([rims[0], q_pre]).astype(jnp.float32)
        k_pad = jnp.concatenate([rims[1], k_pre]).astype(jnp.float32)
        v_pad = jnp.concatenate([rims[2], v_pre]).astype(jnp.float32)

        def prepare(qp_in, kp_in, vp_in, al_in, be_in, cq_in, ck_in, cv_in, alog_in, bias_in):
            return mixer_inputs(
                qp_in, kp_in, vp_in, al_in, be_in, cq_in, ck_in, cv_in, alog_in, bias_in, doc_pad
            )

        mixed_in, prepare_back = jax.vjp(
            prepare,
            q_pad,
            k_pad,
            v_pad,
            alpha_logit,
            beta_logit,
            conv_q_here,
            conv_k_here,
            conv_v_here,
            alog_here,
            bias_here,
        )

        def local_pass(queries, key_vecs, value_vecs, beta_rate, log_decay):
            value_heads = jnp.swapaxes(value_vecs, 0, 1)
            widened = jnp.concatenate(
                [jnp.zeros((heads_here, tok_count, DK), jnp.float32), value_heads], axis=2
            )
            start_state = jnp.concatenate([eye_block, zero_offset], axis=2)
            final_state, head_out = jax.vmap(run_head, in_axes=(0, 0, 0, 0, 0, None, 0, None))(
                jnp.swapaxes(queries, 0, 1),
                jnp.swapaxes(key_vecs, 0, 1),
                widened,
                beta_rate.T,
                log_decay.T,
                doc_ids,
                start_state,
                prior_doc,
            )
            return (head_out, final_state)

        (wide_out, wide_state), pass_back = jax.vjp(local_pass, *mixed_in)
        trans_here = wide_state[:, :, :DK]
        offset_here = wide_state[:, :, DK:]
        trans_in, incoming_state = prefix(
            (trans_here, offset_here), "seq", combine_forward, (eye_block, zero_offset), False
        )
        passing_query = wide_out[:, :, :DK]
        o_heads = wide_out[:, :, DK:] + jnp.einsum(
            "xzy,xyq->xzq", passing_query, incoming_state, precision=BEST_PRECISION
        )
        gated_f, gate_back = jax.vjp(gate_out, jnp.swapaxes(o_heads, 0, 1), gate_vals, head_gain)
        gated = gated_f.astype(jnp.bfloat16)
        attn_part = lax.psum_scatter(
            matmul(gated, wo_full), "head", scatter_dimension=0, tiled=True
        )
        x_part = lax.dynamic_slice_in_dim(x_here, row_first, row_count, 0)
        x_one_part = x_part + attn_part
        h_two_f, norm_two_back = jax.vjp(rms_rows, x_one_part, mlp_gain)
        h_two = lax.all_gather(h_two_f.astype(jnp.bfloat16), "head", axis=0, tiled=True)
        ff_gate = matmul(h_two, wfg_full)
        ff_up = matmul(h_two, wfu_full)
        hidden_f, swiglu_back = jax.vjp(swiglu, ff_gate, ff_up)
        hidden = hidden_f.astype(jnp.bfloat16)
        mlp_part = lax.psum_scatter(
            matmul(hidden, wd_full).astype(jnp.bfloat16), "head", scatter_dimension=0, tiled=True
        ).astype(jnp.float32)
        y_blocks.append((x_one_part + mlp_part).astype(jnp.bfloat16))
        d_hidden = matmul_bt(cot_here, wd_full)
        grad_down = matmul_at(hidden, cot_here)
        d_ffgate, d_ffup = swiglu_back(d_hidden)
        d_ffgate = d_ffgate.astype(jnp.bfloat16)
        d_ffup = d_ffup.astype(jnp.bfloat16)
        grad_ffgate = matmul_at(h_two, d_ffgate)
        grad_ffup = matmul_at(h_two, d_ffup)
        d_h_two = lax.psum_scatter(
            matmul_bt(d_ffgate, wfg_full) + matmul_bt(d_ffup, wfu_full),
            "head",
            scatter_dimension=0,
            tiled=True,
        )
        d_x_norm, grad_mlp_gain = norm_two_back(d_h_two)
        cot_part = lax.dynamic_slice_in_dim(cot_here, row_first, row_count, 0).astype(jnp.float32)
        d_x_one = cot_part + d_x_norm
        d_attn = lax.all_gather(d_x_one.astype(jnp.bfloat16), "head", axis=0, tiled=True)
        d_gated = matmul_bt(d_attn, wo_full)
        grad_out = matmul_at(gated, d_attn)
        d_o_rows, d_gate, grad_head_gain = gate_back(d_gated)
        output_heads_grad = jnp.swapaxes(d_o_rows, 0, 1)
        segment_gradient = jnp.einsum(
            "dso,dsl->dol", passing_query, output_heads_grad, precision=BEST_PRECISION
        )
        trans_out, outgoing_state_grad = prefix(
            (trans_here, segment_gradient), "seq", combine_backward, (eye_block, zero_offset), True
        )
        passing_gradient = jnp.einsum(
            "wqi,wli->wql", output_heads_grad, incoming_state, precision=BEST_PRECISION
        )
        d_wide_out = jnp.concatenate([passing_gradient, output_heads_grad], axis=2)
        transfer_gradient = jnp.einsum(
            "zpd,zld->zpl", outgoing_state_grad, incoming_state, precision=BEST_PRECISION
        )
        d_wide_state = jnp.concatenate([transfer_gradient, outgoing_state_grad], axis=2)
        d_mixed = pass_back((d_wide_out, d_wide_state))
        (
            d_q_pad,
            d_k_pad,
            d_v_pad,
            d_alpha,
            d_beta,
            grad_cq,
            grad_ck,
            grad_cv,
            grad_alog,
            grad_bias,
        ) = prepare_back(d_mixed)
        back_rims = passed_along(
            (d_q_pad[: KCONV - 1], d_k_pad[: KCONV - 1], d_v_pad[: KCONV - 1]), "seq", -1
        )
        d_q_pre = jnp.concatenate(
            [d_q_pad[KCONV - 1 : tok_count], d_q_pad[tok_count:] + back_rims[0]]
        ).astype(jnp.bfloat16)
        d_k_pre = jnp.concatenate(
            [d_k_pad[KCONV - 1 : tok_count], d_k_pad[tok_count:] + back_rims[1]]
        ).astype(jnp.bfloat16)
        d_v_pre = jnp.concatenate(
            [d_v_pad[KCONV - 1 : tok_count], d_v_pad[tok_count:] + back_rims[2]]
        ).astype(jnp.bfloat16)
        d_gate_b = d_gate.astype(jnp.bfloat16)
        d_alpha_b = d_alpha.astype(jnp.bfloat16)
        d_beta_b = d_beta.astype(jnp.bfloat16)
        grad_query = matmul_at(h_one, d_q_pre)
        grad_key = matmul_at(h_one, d_k_pre)
        grad_value = matmul_at(h_one, d_v_pre)
        grad_gate = matmul_at(h_one, d_gate_b)
        grad_alpha = matmul_at(h_one, d_alpha_b)
        grad_beta = matmul_at(h_one, d_beta_b)
        total = matmul_bt(d_q_pre, wq_full) + matmul_bt(d_k_pre, wk_full)
        total = total + matmul_bt(d_v_pre, wv_full) + matmul_bt(d_gate_b, wg_full)
        d_h_one = lax.psum_scatter(
            (total + matmul_bt(d_alpha_b, wa_full) + matmul_bt(d_beta_b, wb_full)).astype(
                jnp.bfloat16
            ),
            "head",
            scatter_dimension=0,
            tiled=True,
        ).astype(jnp.float32)
        norm_one_out, norm_one_back = jax.vjp(rms_rows, x_part, attn_gain)
        d_x_first, grad_attn_gain = norm_one_back(d_h_one)
        dx_blocks.append(d_x_one + d_x_first)
        micro_grads = (
            grad_query,
            grad_key,
            grad_value,
            grad_gate,
            grad_alpha,
            grad_beta,
            grad_out,
            grad_ffgate,
            grad_ffup,
            grad_down,
        )
        micro_small = (
            grad_attn_gain,
            grad_mlp_gain,
            grad_head_gain,
            grad_cq,
            grad_ck,
            grad_cv,
            grad_alog,
            grad_bias,
        )
        small_sums = micro_small if small_sums is None else add_tuples(small_sums, micro_small)
        micro_shards = send_grads(micro_grads)
        weight_sums = micro_shards if weight_sums is None else add_tuples(weight_sums, micro_shards)
    sum_attn_gain, sum_mlp_gain, sum_head_gain, sum_cq, sum_ck, sum_cv, sum_alog, sum_bias = (
        small_sums
    )
    full_cq = lax.dynamic_update_slice_in_dim(
        jnp.zeros_like(conv_query), sum_cq, head_place * query_width, 1
    )
    full_ck = lax.dynamic_update_slice_in_dim(
        jnp.zeros_like(conv_key), sum_ck, head_place * query_width, 1
    )
    full_cv = lax.dynamic_update_slice_in_dim(
        jnp.zeros_like(conv_value), sum_cv, head_place * value_width, 1
    )
    full_alog = lax.dynamic_update_slice_in_dim(
        jnp.zeros_like(a_log), sum_alog, head_place * heads_here, 0
    )
    full_bias = lax.dynamic_update_slice_in_dim(
        jnp.zeros_like(dt_bias), sum_bias, head_place * heads_here, 0
    )
    small_total = lax.psum(
        (
            sum_attn_gain,
            sum_mlp_gain,
            sum_head_gain,
            full_cq,
            full_ck,
            full_cv,
            full_alog,
            full_bias,
        ),
        ("seq", "head", "fsdp"),
    )
    block_output = jnp.stack(y_blocks)[:, None]
    input_grad = jnp.stack(dx_blocks)[:, None]
    (
        shard_query,
        shard_key,
        shard_value,
        shard_gate,
        shard_alpha,
        shard_beta,
        shard_out,
        shard_ffgate,
        shard_ffup,
        shard_down,
    ) = weight_sums
    tot_attn_gain, tot_mlp_gain, tot_head_gain, tot_cq, tot_ck, tot_cv, tot_alog, tot_bias = (
        small_total
    )
    return (
        block_output,
        input_grad,
        shard_query,
        shard_key,
        shard_value,
        shard_gate,
        shard_alpha,
        shard_beta,
        shard_out,
        shard_ffgate,
        shard_ffup,
        shard_down,
        tot_attn_gain,
        tot_mlp_gain,
        tot_head_gain,
        tot_cq,
        tot_ck,
        tot_cv,
        tot_alog,
        tot_bias,
    )


def solution(mesh):
    return jax.shard_map(
        per_device,
        mesh=mesh,
        in_specs=(
            P(None, "fsdp", "seq", None),
            P(None, "fsdp", "seq", None),
            P(None, "fsdp", None),
            P(),
            P("fsdp", "head"),
            P("fsdp", "head"),
            P("fsdp", "head"),
            P("fsdp", "head"),
            P("fsdp", "head"),
            P("fsdp", "head"),
            P(),
            P(),
            P(),
            P(),
            P(),
            P(),
            P("head", "fsdp"),
            P(),
            P("fsdp", "head"),
            P("fsdp", "head"),
            P("head", "fsdp"),
        ),
        out_specs=(
            P(None, "fsdp", ("seq", "head"), None),
            P(None, "fsdp", ("seq", "head"), None),
            P(("seq", "fsdp"), "head"),
            P(("seq", "fsdp"), "head"),
            P(("seq", "fsdp"), "head"),
            P(("seq", "fsdp"), "head"),
            P(("seq", "fsdp"), "head"),
            P(("seq", "fsdp"), "head"),
            P("head", ("seq", "fsdp")),
            P(("seq", "fsdp"), "head"),
            P(("seq", "fsdp"), "head"),
            P("head", ("seq", "fsdp")),
            P(),
            P(),
            P(),
            P(),
            P(),
            P(),
            P(),
            P(),
        ),
        check_vma=False,
    )
```

profile of v0, /device:TPU:0, one launch (start us, length us, event | category | flops | bytes accessed | tf_op | source)
XLA Modules:
  0.0 3089.6 jit_solution(7304490776352217088)
XLA Ops:
  13.0 24.1 all_gather.129
  41.9 16.2 all_gather.132
  221.2 172.5 %while.230 = (s32[]{:T(128)}, f32[2,128,384]{2,1,0:T(8,128)S(1)}, s32[]{:T(128)}, f32[8,2,64,384]{3,2,1,0:T(8,128)}, f32[8,2,128,384]{3,2,1,0:T(8,128)}, /*index...) while((s32[]{:T(128)}, f32[2,128,384]{2,1,0:T(8,128)S(1)}, ...), condition=%wide.region_35.38_spmd.clone, body=%wide.region_33.37_spmd.clone.sunk | while | flops 327795136 | bytes 4807661 | solution.py:132
  401.8 174.2 %while.229 = (s32[]{:T(128)}, f32[2,128,384]{2,1,0:T(8,128)S(1)}, s32[]{:T(128)}, f32[8,2,64,384]{3,2,1,0:T(8,128)}, f32[8,2,128,384]{3,2,1,0:T(8,128)}, /*index...) while((s32[]{:T(128)}, f32[2,128,384]{2,1,0:T(8,128)S(1)}, ...), condition=%wide.region_21.24_spmd.clone, body=%wide.region_19.23_spmd.clone.sunk | while | flops 327795136 | bytes 4807661 | solution.py:132
  405.8 10.6 custom-call.40
  427.5 10.6 custom-call.40
  449.3 10.6 custom-call.40
  471.0 10.6 custom-call.40
  492.8 10.6 custom-call.40
  514.5 10.6 custom-call.40
  536.4 10.6 custom-call.40
  558.2 10.6 custom-call.40
  582.5 173.7 %while.228 = (s32[]{:T(128)}, f32[2,128,384]{2,1,0:T(8,128)S(1)}, s32[]{:T(128)}, f32[8,2,64,384]{3,2,1,0:T(8,128)}, f32[8,2,128,384]{3,2,1,0:T(8,128)}, /*index...) while((s32[]{:T(128)}, f32[2,128,384]{2,1,0:T(8,128)S(1)}, ...), condition=%wide.region_7.10_spmd.clone, body=%wide.region_5.9_spmd.clone.sunk | while | flops 327795136 | bytes 4807661 | solution.py:132
  586.8 10.6 custom-call.39
  608.5 10.6 custom-call.39
  630.2 10.6 custom-call.39
  651.8 10.6 custom-call.39
  673.5 10.6 custom-call.39
  716.8 10.6 custom-call.39
  829.7 27.0 reduce-scatter.27.cloned.1.call-done
  866.1 27.7 all-gather.30.cloned.1.call-done
  893.8 17.1 all-gather.28.cloned.1.call-done
  914.7 33.4 %all-gather.32.cloned.1.call-done = bf16[1024,704]{0,1:T(8,128)(2,1)} async-done(((bf16[256,704]{0,1:T(8,128)(2,1)}), bf16[1024,704]{0,1:T(8,128)(2,1)}) %all-gather.32.cloned.1.call-update) | async-done | bytes 1441808 | tf_op jit(solution)/shard_map/all_gather | solution.py:257
  951.6 32.0 %all-gather.34.cloned.1.call-done = bf16[704,1024]{1,0:T(8,128)(2,1)} async-done(((bf16[704,256]{1,0:T(8,128)(2,1)}), bf16[704,1024]{1,0:T(8,128)(2,1)}) %all-gather.34.cloned.1.call-update) | async-done | bytes 1441808 | tf_op jit(solution)/shard_map/all_gather | solution.py:258
  996.7 19.3 reduce-scatter.31.cloned.1.call-done
  1017.9 31.9 %reduce-scatter.35.cloned.1.call-done = f32[128,1024]{1,0:T(8,128)} async-done(((f32[512,1024]{1,0:T(8,128)}), f32[128,1024]{1,0:T(8,128)}) %reduce-scatter.35.cloned.1.call-update) | async-done | bytes 524304 | tf_op jit(solution)/shard_map/reduce_scatter | solution.py:342
  1051.7 32.2 %reduce-scatter.39.cloned.1.call-done = f32[128,1024]{1,0:T(8,128)} async-done(((f32[512,1024]{1,0:T(8,128)}), f32[128,1024]{1,0:T(8,128)}) %reduce-scatter.39.cloned.1.call-update) | async-done | bytes 524304 | tf_op jit(solution)/shard_map/reduce_scatter | solution.py:364
  1088.7 16.1 all-gather.38.cloned.1.call-done
  1136.5 21.0 reduce-scatter.47.cloned.1.call-done
  1157.5 34.0 %reduce-scatter.43.cloned.1.call-done = f32[128,1024]{1,0:T(8,128)} async-done(((f32[512,1024]{1,0:T(8,128)}), f32[128,1024]{1,0:T(8,128)}) %reduce-scatter.43.cloned.1.call-update) | async-done | bytes 524304 | tf_op jit(solution)/shard_map/reduce_scatter | solution.py:364
  1213.9 15.1 all-gather.42.cloned.1.call-done
  1232.3 15.5 all-gather.44.cloned.1.call-done
  1288.7 234.9 %while.226 = (s32[]{:T(128)}, f32[2,128,384]{2,1,0:T(8,128)S(1)}, f32[8,2,64,128]{3,2,0,1:T(8,128)}, f32[8,2,64,128]{3,2,0,1:T(8,128)}, f32[8,2,64,384]{3,2,0,1:...) while((s32[]{:T(128)}, f32[2,128,384]{2,1,0:T(8,128)S(1)}, ...), condition=%wide.region_82.86_spmd, body=%wide.region_70.85_spmd.sunk | while | flops 876917952 | bytes 13976245 | solution.py:132
  1539.3 234.9 %while.225 = (s32[]{:T(128)}, f32[2,128,384]{2,1,0:T(8,128)S(1)}, f32[8,2,64,128]{3,2,0,1:T(8,128)}, f32[8,2,64,128]{3,2,0,1:T(8,128)}, f32[8,2,64,384]{3,2,0,1:...) while((s32[]{:T(128)}, f32[2,128,384]{2,1,0:T(8,128)S(1)}, ...), condition=%wide.region_59.63_spmd, body=%wide.region_47.62_spmd.sunk | while | flops 876917952 | bytes 13976245 | solution.py:132
  1787.4 225.2 %while.227 = (s32[]{:T(128)}, f32[2,128,384]{2,1,0:T(8,128)S(1)}, f32[8,2,64,128]{3,2,0,1:T(8,128)S(1)}, f32[8,2,64,128]{3,2,0,1:T(8,128)S(1)}, f32[8,2,64,384]{...) while((s32[]{:T(128)}, f32[2,128,384]{2,1,0:T(8,128)S(1)}, ...), condition=%wide.region_105.109_spmd, body=%wide.region_93.108_spmd.sunk | while | flops 876917952 | bytes 13976245 | solution.py:132
  2202.5 44.7 %reduce-scatter.69.cloned.1.call-done = f32[128,2]{1,0:T(8,128)} async-done(((f32[1024,2]{1,0:T(8,128)}), f32[128,2]{1,0:T(8,128)}) %reduce-scatter.69.cloned.1.call-update) | async-done | bytes 1040
  2248.7 63.1 %reduce-scatter.67.cloned.1.call-done = f32[128,2]{1,0:T(8,128)} async-done(((f32[1024,2]{1,0:T(8,128)}), f32[128,2]{1,0:T(8,128)}) %reduce-scatter.67.cloned.1.call-update) | async-done | bytes 1040
  2313.3 24.9 reduce-scatter.33.cloned.1.call-done
  2340.3 25.3 reduce-scatter.37.cloned.1.call-done
  2369.4 72.5 %reduce-scatter.65.cloned.1.call-done = f32[704,128]{1,0:T(8,128)} async-done(((f32[704,1024]{1,0:T(8,128)}), f32[704,128]{1,0:T(8,128)}) %reduce-scatter.65.cloned.1.call-update) | async-done | bytes 360464 | tf_op jit(solution)/shard_map/reduce_scatter | solution.py:196
  2441.9 75.7 %reduce-scatter.63.cloned.1.call-done = f32[128,704]{0,1:T(8,128)} async-done(((f32[1024,704]{0,1:T(8,128)}), f32[128,704]{0,1:T(8,128)}) %reduce-scatter.63.cloned.1.call-update) | async-done | bytes 360464 | tf_op jit(solution)/shard_map/reduce_scatter | solution.py:195
  2517.6 75.7 %reduce-scatter.61.cloned.1.call-done = f32[128,704]{0,1:T(8,128)} async-done(((f32[1024,704]{0,1:T(8,128)}), f32[128,704]{0,1:T(8,128)}) %reduce-scatter.61.cloned.1.call-update) | async-done | bytes 360464 | tf_op jit(solution)/shard_map/reduce_scatter | solution.py:194
  2593.4 66.5 %reduce-scatter.53.cloned.1.call-done = f32[128,256]{1,0:T(8,128)} async-done(((f32[1024,256]{1,0:T(8,128)}), f32[128,256]{1,0:T(8,128)}) %reduce-scatter.53.cloned.1.call-update) | async-done | bytes 131088 | tf_op jit(solution)/shard_map/reduce_scatter | solution.py:188
  2659.8 66.7 %reduce-scatter.51.cloned.1.call-done = f32[128,256]{1,0:T(8,128)} async-done(((f32[1024,256]{1,0:T(8,128)}), f32[128,256]{1,0:T(8,128)}) %reduce-scatter.51.cloned.1.call-update) | async-done | bytes 131088 | tf_op jit(solution)/shard_map/reduce_scatter | solution.py:187
  2726.6 128.8 %all-reduce.85.cloned.1.call-done = (f32[1024]{0:T(1024)}, f32[1024]{0:T(1024)}, f32[256]{0:T(256)}, f32[4,1024]{1,0:T(4,128)}, f32[4,1024]{1,0:T(4,128)}, /*index=5*/f32[4,2048]{1,0:T(4,128)}, f32[8]{0:T(128)}, f32[8]{0:T(128)}) async-done(((f32[1024]{0:T(1024)}, f32[1024]{0:T(1024)}, f32[256]{0:T(256)}, f32[4,1024]{1,0:T(4,128)}, f32[4,1024]{1,0:T(4,128)}, /*index=5*/f32[4,2048]{1,0:T(4,128)}, ...) | async-done | bytes 74832 | tf_op jit(solution)/shard_map/psum | solution.py:482
  2855.3 74.7 %reduce-scatter.59.cloned.1.call-done = f32[512,128]{1,0:T(8,128)} async-done(((f32[512,1024]{1,0:T(8,128)}), f32[512,128]{1,0:T(8,128)}) %reduce-scatter.59.cloned.1.call-update) | async-done | bytes 262160 | tf_op jit(solution)/shard_map/reduce_scatter | solution.py:193
  2930.0 71.3 %reduce-scatter.57.cloned.1.call-done = f32[128,512]{1,0:T(8,128)} async-done(((f32[1024,512]{1,0:T(8,128)}), f32[128,512]{1,0:T(8,128)}) %reduce-scatter.57.cloned.1.call-update) | async-done | bytes 262160 | tf_op jit(solution)/shard_map/reduce_scatter | solution.py:190
  3001.4 71.4 %reduce-scatter.55.cloned.1.call-done = f32[128,512]{1,0:T(8,128)} async-done(((f32[1024,512]{1,0:T(8,128)}), f32[128,512]{1,0:T(8,128)}) %reduce-scatter.55.cloned.1.call-update) | async-done | bytes 262160 | tf_op jit(solution)/shard_map/reduce_scatter | solution.py:189
  (3091 shorter events, 1681.1 us)
Async XLA Ops:
  7.2 190.2 %all-gather.24.cloned.1.call-start = ((), (), s32[]{:S(2)}) async-start(), calls=%async_computation.23 | async-start | bytes 1310720 | tf_op jit(solution)/shard_map/all_gather | solution.py:252
  7.9 198.2 %all-gather.22.cloned.1.call-start = ((), (), s32[]{:S(2)}) async-start(), calls=%async_computation.22 | async-start | bytes 1310720 | tf_op jit(solution)/shard_map/all_gather | solution.py:251
  8.7 814.1 %all-gather.26.cloned.1.call-start = ((), (), s32[]{:S(2)}) async-start(), calls=%async_computation.24 | async-start | bytes 1310720 | tf_op jit(solution)/shard_map/all_gather | solution.py:255
  38.3 90.1 %collective-permute-start.6 = (bf16[3,256]{1,0:T(4,128)(2,1)}, bf16[3,256]{1,0:T(4,128)(2,1)}, u32[]{:S(2)}, u32[]{:S(2)}) collective-permute-start(bf16[3,256]{1,0:T(4,128)(2,1)} %slice.758), channel_id=1, source_target_pairs={{0,16},{1,17},{2,18},{3,19},{4,20},{5,21},{6,22},{7,23},{8,24},{9,... | collective-permute-start | bytes 4616 | tf_op jit(solution)/shard_map/ppermute | solution.py:21
  59.2 72.5 %collective-permute-start.8 = (bf16[3,256]{1,0:T(4,128)(2,1)}, bf16[3,256]{1,0:T(4,128)(2,1)}, u32[]{:S(2)}, u32[]{:S(2)}) collective-permute-start(bf16[3,256]{1,0:T(4,128)(2,1)} %slice.768), channel_id=1, source_target_pairs={{0,16},{1,17},{2,18},{3,19},{4,20},{5,21},{6,22},{7,23},{8,24},{9,... | collective-permute-start | bytes 4616 | tf_op jit(solution)/shard_map/ppermute | solution.py:21
  63.7 87.0 %collective-permute-start = (bf16[3,256]{1,0:T(4,128)(2,1)}, bf16[3,256]{1,0:T(4,128)(2,1)}, u32[]{:S(2)}, u32[]{:S(2)}) collective-permute-start(bf16[3,256]{1,0:T(4,128)(2,1)} %slice.724), channel_id=1, source_target_pairs={{0,16},{1,17},{2,18},{3,19},{4,20},{5,21},{6,22},{7,23},{8,24},{9,... | collective-permute-start | bytes 4616 | tf_op jit(solution)/shard_map/ppermute | solution.py:21
  66.6 85.1 %collective-permute-start.3 = (bf16[3,256]{1,0:T(4,128)(2,1)}, bf16[3,256]{1,0:T(4,128)(2,1)}, u32[]{:S(2)}, u32[]{:S(2)}) collective-permute-start(bf16[3,256]{1,0:T(4,128)(2,1)} %slice.741), channel_id=1, source_target_pairs={{0,16},{1,17},{2,18},{3,19},{4,20},{5,21},{6,22},{7,23},{8,24},{9,... | collective-permute-start | bytes 4616 | tf_op jit(solution)/shard_map/ppermute | solution.py:21
  70.2 95.3 %collective-permute-start.2 = (bf16[3,256]{1,0:T(4,128)(2,1)}, bf16[3,256]{1,0:T(4,128)(2,1)}, u32[]{:S(2)}, u32[]{:S(2)}) collective-permute-start(bf16[3,256]{1,0:T(4,128)(2,1)} %slice.734), channel_id=1, source_target_pairs={{0,16},{1,17},{2,18},{3,19},{4,20},{5,21},{6,22},{7,23},{8,24},{9,... | collective-permute-start | bytes 4616 | tf_op jit(solution)/shard_map/ppermute | solution.py:21
  72.1 784.6 %reduce-scatter.27.cloned.1.call-start = ((), (), s32[]{:S(2)}) async-start(), calls=%async_computation.25 | async-start | bytes 2621440 | tf_op jit(solution)/shard_map/reduce_scatter | solution.py:342
  128.3 40.7 %collective-permute-start.5 = (bf16[3,256]{1,0:T(4,128)(2,1)}, bf16[3,256]{1,0:T(4,128)(2,1)}, u32[]{:S(2)}, u32[]{:S(2)}) collective-permute-start(bf16[3,256]{1,0:T(4,128)(2,1)} %slice.751), channel_id=1, source_target_pairs={{0,16},{1,17},{2,18},{3,19},{4,20},{5,21},{6,22},{7,23},{8,24},{9,... | collective-permute-start | bytes 4616 | tf_op jit(solution)/shard_map/ppermute | solution.py:21
  210.6 183.1 %collective-permute-start.1 = (bf16[3,512]{1,0:T(4,128)(2,1)S(1)}, bf16[3,512]{1,0:T(4,128)(2,1)S(1)}, u32[]{:S(2)}, u32[]{:S(2)}) collective-permute-start(bf16[3,512]{1,0:T(4,128)(2,1)S(1)} %slice.729), channel_id=1, source_target_pairs={{0,16},{1,17},{2,18},{3,19},{4,20},{5,21},{6,22},{7,23},{8,24},{9,... | collective-permute-start | bytes 9224 | tf_op jit(solution)/shard_map/ppermute | solution.py:21
  213.0 181.7 %collective-permute-start.4 = (bf16[3,512]{1,0:T(4,128)(2,1)S(1)}, bf16[3,512]{1,0:T(4,128)(2,1)S(1)}, u32[]{:S(2)}, u32[]{:S(2)}) collective-permute-start(bf16[3,512]{1,0:T(4,128)(2,1)S(1)} %slice.746), channel_id=1, source_target_pairs={{0,16},{1,17},{2,18},{3,19},{4,20},{5,21},{6,22},{7,23},{8,24},{9,... | collective-permute-start | bytes 9224 | tf_op jit(solution)/shard_map/ppermute | solution.py:21
  826.2 67.6 %all-gather.30.cloned.1.call-start = ((), (), s32[]{:S(2)}) async-start(), calls=%async_computation.27 | async-start | bytes 1802240 | tf_op jit(solution)/shard_map/all_gather | solution.py:256
  826.8 84.1 %all-gather.28.cloned.1.call-start = ((), (), s32[]{:S(2)}) async-start(), calls=%async_computation.26 | async-start | bytes 1310720 | tf_op jit(solution)/shard_map/all_gather | solution.py:348
  859.6 88.5 %all-gather.32.cloned.1.call-start = ((), (), s32[]{:S(2)}) async-start(), calls=%async_computation.28 | async-start | bytes 1802240 | tf_op jit(solution)/shard_map/all_gather | solution.py:257
  860.3 123.2 %all-gather.34.cloned.1.call-start = ((), (), s32[]{:S(2)}) async-start(), calls=%async_computation.29 | async-start | bytes 1802240 | tf_op jit(solution)/shard_map/all_gather | solution.py:258
  861.1 154.9 %reduce-scatter.31.cloned.1.call-start = ((), (), s32[]{:S(2)}) async-start(), calls=%async_computation.31 | async-start | bytes 2621440 | tf_op jit(solution)/shard_map/reduce_scatter | solution.py:342
  863.5 186.3 %reduce-scatter.35.cloned.1.call-start = ((), (), s32[]{:S(2)}) async-start(), calls=%async_computation.34 | async-start | bytes 2621440 | tf_op jit(solution)/shard_map/reduce_scatter | solution.py:342
  866.0 217.9 %reduce-scatter.39.cloned.1.call-start = ((), (), s32[]{:S(2)}) async-start(), calls=%async_computation.37 | async-start | bytes 2621440 | tf_op jit(solution)/shard_map/reduce_scatter | solution.py:364
  993.0 111.8 %all-gather.38.cloned.1.call-start = ((), (), s32[]{:S(2)}) async-start(), calls=%async_computation.35 | async-start | bytes 1310720 | tf_op jit(solution)/shard_map/all_gather | solution.py:348
  1087.9 35.8 %all-gather.36.cloned.1.call-start = ((), (), s32[]{:S(2)}) async-start(), calls=%async_computation.32 | async-start | bytes 1310720 | tf_op jit(solution)/shard_map/all_gather | solution.py:348
  1088.7 68.9 %reduce-scatter.47.cloned.1.call-start = ((), (), s32[]{:S(2)}) async-start(), calls=%async_computation.43 | async-start | bytes 2621440 | tf_op jit(solution)/shard_map/reduce_scatter | solution.py:364
  1116.9 74.6 %reduce-scatter.43.cloned.1.call-start = ((), (), s32[]{:S(2)}) async-start(), calls=%async_computation.40 | async-start | bytes 2621440 | tf_op jit(solution)/shard_map/reduce_scatter | solution.py:364
  1135.9 74.4 %all-gather.40.cloned.1.call-start = ((), (), s32[]{:S(2)}) async-start(), calls=%async_computation.38 | async-start | bytes 1310720 | tf_op jit(solution)/shard_map/all_gather | solution.py:373
  1136.5 92.5 %all-gather.42.cloned.1.call-start = ((), (), s32[]{:S(2)}) async-start(), calls=%async_computation.41 | async-start | bytes 1310720 | tf_op jit(solution)/shard_map/all_gather | solution.py:373
  1196.0 51.8 %all-gather.44.cloned.1.call-start = ((), (), s32[]{:S(2)}) async-start(), calls=%async_computation.44 | async-start | bytes 1310720 | tf_op jit(solution)/shard_map/all_gather | solution.py:373
  1196.5 977.6 %reduce-scatter.41.cloned.1.call-start = ((), (), s32[]{:S(2)}) async-start(), calls=%async_computation.39 | async-start | bytes 1310720 | tf_op jit(solution)/shard_map/reduce_scatter | solution.py:428
  2072.6 103.0 %reduce-scatter.29.cloned.1.call-start = ((), (), s32[]{:S(2)}) async-start(), calls=%async_computation.30 | async-start | bytes 1310720 | tf_op jit(solution)/shard_map/reduce_scatter | solution.py:353
  2076.2 99.4 %reduce-scatter.45.cloned.1.call-start = ((), (), s32[]{:S(2)}) async-start(), calls=%async_computation.42 | async-start | bytes 1310720 | tf_op jit(solution)/shard_map/reduce_scatter | solution.py:428
  2083.9 27.2 collective-permute-start.14
  2085.9 22.1 collective-permute-start.13
  2087.3 22.2 collective-permute-start.12
  2094.8 24.6 collective-permute-start.17
  2096.8 21.0 collective-permute-start.16
  2115.3 66.6 %reduce-scatter.49.cloned.1.call-start = ((), (), s32[]{:S(2)}) async-start(), calls=%async_computation.45 | async-start | bytes 1310720 | tf_op jit(solution)/shard_map/reduce_scatter | solution.py:428
  2123.7 123.5 %reduce-scatter.69.cloned.1.call-start = ((), (), s32[]{:S(2)}) async-start(), calls=%async_computation.55 | async-start | bytes 589824
  2127.1 184.7 %reduce-scatter.67.cloned.1.call-start = ((), (), s32[]{:S(2)}) async-start(), calls=%async_computation.54 | async-start | bytes 589824
  2128.4 209.8 %reduce-scatter.33.cloned.1.call-start = ((), (), s32[]{:S(2)}) async-start(), calls=%async_computation.33 | async-start | bytes 1310720 | tf_op jit(solution)/shard_map/reduce_scatter | solution.py:353
  2132.1 233.6 %reduce-scatter.37.cloned.1.call-start = ((), (), s32[]{:S(2)}) async-start(), calls=%async_computation.36 | async-start | bytes 1310720 | tf_op jit(solution)/shard_map/reduce_scatter | solution.py:353
  2135.7 306.2 %reduce-scatter.65.cloned.1.call-start = ((), (), s32[]{:S(2)}) async-start(), calls=%async_computation.53 | async-start | bytes 3244032 | tf_op jit(solution)/shard_map/reduce_scatter | solution.py:196
  2142.6 375.1 %reduce-scatter.63.cloned.1.call-start = ((), (), s32[]{:S(2)}) async-start(), calls=%async_computation.52 | async-start | bytes 3244032 | tf_op jit(solution)/shard_map/reduce_scatter | solution.py:195
  2149.1 444.3 %reduce-scatter.61.cloned.1.call-start = ((), (), s32[]{:S(2)}) async-start(), calls=%async_computation.51 | async-start | bytes 3244032 | tf_op jit(solution)/shard_map/reduce_scatter | solution.py:194
  2155.7 504.1 %reduce-scatter.53.cloned.1.call-start = ((), (), s32[]{:S(2)}) async-start(), calls=%async_computation.47 | async-start | bytes 1179648 | tf_op jit(solution)/shard_map/reduce_scatter | solution.py:188
  2159.8 566.7 %reduce-scatter.51.cloned.1.call-start = ((), (), s32[]{:S(2)}) async-start(), calls=%async_computation.46 | async-start | bytes 1179648 | tf_op jit(solution)/shard_map/reduce_scatter | solution.py:187
  2169.1 686.2 %all-reduce.85.cloned.1.call-start = ((), (), s32[]{:S(2)}) async-start(), calls=%async_computation.56 | async-start | bytes 151552 | tf_op jit(solution)/shard_map/psum | solution.py:482
  2186.0 744.0 %reduce-scatter.59.cloned.1.call-start = ((), (), s32[]{:S(2)}) async-start(), calls=%async_computation.50 | async-start | bytes 2359296 | tf_op jit(solution)/shard_map/reduce_scatter | solution.py:193
  2190.8 810.5 %reduce-scatter.57.cloned.1.call-start = ((), (), s32[]{:S(2)}) async-start(), calls=%async_computation.49 | async-start | bytes 2359296 | tf_op jit(solution)/shard_map/reduce_scatter | solution.py:190
  2197.3 875.5 %reduce-scatter.55.cloned.1.call-start = ((), (), s32[]{:S(2)}) async-start(), calls=%async_computation.48 | async-start | bytes 2359296 | tf_op jit(solution)/shard_map/reduce_scatter | solution.py:189
  (432 other events, 5709.7 us)
Sparse Core Ops, SparseCore 0:
  9.6 37.1 all-gather.23
  48.4 30.7 all-gather.21
  80.7 30.3 all-gather.25
  826.3 30.3 reduce-scatter.26
  858.2 35.5 all-gather.29
  895.9 14.9 all-gather.27
  912.5 35.5 all-gather.31
  949.7 33.7 all-gather.33
  986.3 29.6 reduce-scatter.30
  1018.3 31.4 reduce-scatter.34
  1052.5 31.3 reduce-scatter.38
  1088.0 16.7 all-gather.37
  1106.9 16.7 all-gather.35
  1126.1 31.4 reduce-scatter.46
  1160.1 31.3 reduce-scatter.42
  1193.5 16.7 all-gather.39
  1212.3 16.7 all-gather.41
  1231.0 16.7 all-gather.43
  2072.7 26.0 reduce-scatter.40
  2101.3 24.8 reduce-scatter.28
  2128.8 24.8 reduce-scatter.44
  2157.0 24.8 reduce-scatter.48
  2185.2 61.9 reduce-scatter.68
  2250.8 60.9 reduce-scatter.66
  2314.3 23.8 reduce-scatter.32
  2340.7 24.8 reduce-scatter.36
  2369.6 72.2 reduce-scatter.64
  2446.1 71.5 reduce-scatter.62
  2521.8 71.5 reduce-scatter.60
  2597.2 62.6 reduce-scatter.52
  2664.2 62.3 reduce-scatter.50
  2734.2 121.1 all-reduce.84
  2859.7 70.2 reduce-scatter.58
  2934.6 66.7 reduce-scatter.56
  3005.9 66.8 reduce-scatter.54
where the time goes:
time: 3110 us; the launch traced here: 3090 us
  waiting for transfers between devices  1210 us (39%)
  other arithmetic  732 us (24%)
  matrix products  569 us (18%)
  local copies, waits for them, and re-layouts  374 us (12%)
  blocking collectives  126 us (4%)
  starting transfers between devices  33.8 us (1%)
    another operation x192, other arithmetic, stretch_step(): jax.scipy.linalg.solve_triangular(lower_mat, beta_rate[:, None] * (value_...  491 us
    psum x1, waiting for transfers between devices, per_device(): lax.psum((sum_attn_gain, sum_mlp_gain, sum_head_gain, full_cq, full_ck, f...  129 us
    squeeze x144, local copies, waits for them, and re-layouts, run_head(): lax.scan(jax.checkpoint(stretch_step), (state_mat, prior_doc), pieces)  120 us
    unnamed x37, waiting for transfers between devices  113 us
    reduce_scatter x3, waiting for transfers between devices, per_device(): lax.psum_scatter(matmul_bt(d_ffgate, wfg_full) + matmul_bt(d_ffup, wfu_fu...  87.2 us
    reduce_scatter x3, waiting for transfers between devices, per_device(): lax.psum_scatter(matmul(gated, wo_full), 'head', scatter_dimension=0, til...  78.2 us
    reduce_scatter x1, waiting for transfers between devices, send_grads(): lax.psum_scatter(parts[7], ('seq', 'fsdp'), scatter_dimension=0, tiled=True)  75.7 us
    reduce_scatter x1, waiting for transfers between devices, send_grads(): lax.psum_scatter(parts[8], ('seq', 'fsdp'), scatter_dimension=0, tiled=True)  75.7 us
  transfers between devices with their start and end apart: 53, of which 29 were waited for; matrix products, arithmetic and copies ran while one was open for 28% of the time, Pallas kernels for 0%

commit v1 on v0

v1 whole, which is shorter than its diff:
```python
import math

import jax
import jax.numpy as jnp
from jax import lax
from jax.experimental import pallas as pl
from jax.experimental.pallas import tpu as pltpu
from jax.sharding import PartitionSpec as P

DK = 128
DV = 256
KCONV = 4
CHUNK = 128
PAD = 16
LANES = 128
FAR = -(1 << 20)
VMEM_BYTES = 56 * 1024 * 1024

F32 = jnp.float32
BF16 = jnp.bfloat16
BEST = lax.Precision.HIGHEST
SEQ_FSDP = ("seq", "fsdp")


def dot(left, right, left_dim=1, right_dim=0):
    return lax.dot_general(
        left, right, (((left_dim,), (right_dim,)), ((), ())), preferred_element_type=F32
    )


def split_two(value):
    high = value.astype(BF16)
    return high, (value - high.astype(F32)).astype(BF16)


def sigmoid(value):
    return 1.0 / (1.0 + jnp.exp(-value))


def rounded(value):
    return value.astype(BF16).astype(F32)


def row_sum(value):
    return jnp.sum(value, axis=1, keepdims=True)


def twice(value):
    return jnp.concatenate([value, value], axis=1)


def taps_of(padded, since_start):
    taps = [padded[PAD:]]
    for shift in range(1, KCONV):
        moved = pltpu.roll(padded, shift, 0)[PAD:]
        taps.append(jnp.where(since_start >= shift, moved, 0.0))
    return taps


def filtered(taps, filters):
    total = taps[0] * filters[KCONV - 1 : KCONV]
    for shift in range(1, KCONV):
        total = total + taps[shift] * filters[KCONV - 1 - shift : KCONV - shift]
    return total


def unfiltered(grads, filters, since_start):
    zero_rows = jnp.zeros((PAD, grads.shape[1]), F32)
    total = jnp.concatenate([zero_rows, grads * filters[KCONV - 1 : KCONV]], axis=0)
    rows = total.shape[0]
    for shift in range(1, KCONV):
        part = jnp.where(since_start >= shift, grads, 0.0)
        part = part * filters[KCONV - 1 - shift : KCONV - shift]
        part = jnp.concatenate([zero_rows, part], axis=0)
        total = total + pltpu.roll(part, rows - shift, 0)
    return total


def row_of(table, row):
    rows = lax.broadcasted_iota(jnp.int32, table.shape, 0)
    return jnp.sum(jnp.where(rows == row, table, 0.0), axis=0, keepdims=True)


def softplus(value):
    return jnp.maximum(value, 0.0) + jnp.log(1.0 + jnp.exp(-jnp.abs(value)))


def three_parts(value):
    high = value.astype(BF16).astype(F32)
    middle = (value - high).astype(BF16).astype(F32)
    return high, middle, value - high - middle


def stack_rows(rows):
    height = -(-len(rows) // 16) * 16
    place = lax.broadcasted_iota(jnp.int32, (height, rows[0].shape[1]), 0)
    out = jnp.zeros((height, rows[0].shape[1]), F32)
    for at, row in enumerate(rows):
        out = jnp.where(place == at, row, out)
    return out.astype(BF16)


def spread(rows):
    parts = [part for row in rows for part in three_parts(row)]
    stacked = stack_rows(parts)
    shape = (stacked.shape[0], LANES * len(rows))
    place = lax.broadcasted_iota(jnp.int32, shape, 0)
    lane = lax.broadcasted_iota(jnp.int32, shape, 1)
    mine = (place >= (lane // LANES) * 3) & (place < (lane // LANES) * 3 + 3)
    wide = dot(stacked, jnp.where(mine, 1.0, 0.0).astype(BF16), 0, 0)
    return [wide[:, at * LANES : (at + 1) * LANES] for at in range(len(rows))]


def squares_iota():
    rows = lax.broadcasted_iota(jnp.int32, (CHUNK, CHUNK), 0)
    cols = lax.broadcasted_iota(jnp.int32, (CHUNK, CHUNK), 1)
    return rows, cols


def token_rows(ends_ref, logits_ref, params_ref, micro, head, heads, first):
    table = logits_ref[PAD + first : PAD + first + CHUNK, :].T[:8]
    params = params_ref[...]
    lanes = lax.broadcasted_iota(jnp.int32, params.shape, 1)
    params = row_sum(jnp.where(lanes == head, params, 0.0))
    scale = jnp.exp(params[0:1])
    argument = row_of(table, head) + params[1:2]
    beta = sigmoid(row_of(table, heads + head))
    log_decay = -scale * softplus(argument)
    slope = -scale * sigmoid(argument)
    rows, cols = squares_iota()
    upto = jnp.where(rows <= cols, 1.0, 0.0).astype(BF16)
    run = jnp.sum(dot(stack_rows(three_parts(log_decay)), upto), axis=0, keepdims=True)
    position = first + lax.broadcasted_iota(jnp.int32, (1, CHUNK), 1)
    start = jnp.full((1, CHUNK), FAR, jnp.int32)
    for at in range(ends_ref.shape[1]):
        edge = ends_ref[micro, at]
        start = jnp.where(position >= edge, edge, start)
    return beta, log_decay, slope, run, start.astype(F32)


def inverse_unit_lower(stricts):
    rows, cols = squares_iota()
    eye = jnp.where(rows == cols, 1.0, 0.0)

    def corner(width):
        inside = (rows // (2 * width)) == (cols // (2 * width))
        return inside & (rows % (2 * width) >= width) & (cols % (2 * width) < width)

    inverses = [eye - jnp.where(corner(1), strict, 0.0) for strict in stricts]
    width = 2
    while width < CHUNK:
        mask = corner(width)
        held = [inverse.astype(BF16) for inverse in inverses]
        edges = [jnp.where(mask, strict, 0.0).astype(BF16) for strict in stricts]
        lefts = [dot(one, edge).astype(BF16) for one, edge in zip(held, edges)]
        steps = [dot(left, one) for left, one in zip(lefts, held)]
        inverses = [inverse - step for inverse, step in zip(inverses, steps)]
        width *= 2
    out = []
    for strict, inverse in zip(stricts, inverses):
        strict_hi, strict_lo = split_two(strict)
        inv_hi, inv_lo = split_two(inverse)
        product = dot(strict_hi, inv_hi) + dot(strict_hi, inv_lo) + dot(strict_lo, inv_hi)
        out.append((inverse, (eye - inverse - product).astype(BF16), inv_hi))
    return [inverse + dot(inv_hi, miss) for inverse, miss, inv_hi in out]


def decay_terms(run_rows, run_cols, start, first):
    rows, cols = squares_iota()
    allowed = (cols <= rows) & ((cols + first).astype(F32) >= start)
    within = jnp.where(allowed, jnp.exp(jnp.minimum(run_rows - run_cols, 0.0)), 0.0)
    strict = jnp.where(cols < rows, within, 0.0)
    reach = jnp.where(start < first, jnp.exp(run_rows), 0.0)
    last = run_rows[CHUNK - 1 :]
    last_start = start[CHUNK - 1 :]
    tail = jnp.where((rows + first).astype(F32) >= last_start, jnp.exp(last - run_rows), 0.0)
    return within, strict, reach, tail, reach[CHUNK - 1 :]


def ages(starts):
    start = jnp.concatenate(starts, axis=0)
    return lax.broadcasted_iota(jnp.int32, start.shape, 0).astype(F32) - start


def normalized(conved):
    gate = sigmoid(conved)
    active = conved * gate
    inv = lax.rsqrt(row_sum(active * active) + 1e-06)
    return active * inv, inv, gate


def local_kernel(heads, with_trans):
    def body(
        ends_ref, q_ref, k_ref, v_ref, logits_ref, fq_ref, fk_ref, fv_ref, params_ref, *outs
    ):
        qe_ref, ol_ref, mt_ref, nn_ref, ti_ref, rl_ref, rr_ref, fin_ref = outs[:8]
        micro, head = pl.program_id(0), pl.program_id(1)
        rows = q_ref.shape[0] - PAD
        chunks = range(rows // CHUNK)
        parts = [slice(c * CHUNK, (c + 1) * CHUNK) for c in chunks]
        found = [
            token_rows(ends_ref, logits_ref, params_ref, micro, head, heads, c * CHUNK)
            for c in chunks
        ]
        for c in chunks:
            for at, row in enumerate(found[c]):
                rr_ref[at : at + 1, parts[c]] = row
        spreads = [spread([run, beta, start]) for beta, _, _, run, start in found]
        since = ages([one[2] for one in spreads])
        since_wide = twice(since)
        decays = [
            decay_terms(spreads[c][0], found[c][3], spreads[c][2], c * CHUNK) for c in chunks
        ]
        k_conv = filtered(taps_of(rounded(k_ref[...]), since), fk_ref[...])
        keys = normalized(k_conv)[0]
        keys_b = keys.astype(BF16)
        betas = [one[1] for one in spreads]
        grams = [dot(keys_b[part], keys_b[part], 1, 1) for part in parts]
        inverses = inverse_unit_lower(
            [b * decay[1] * gram for b, decay, gram in zip(betas, decays, grams)]
        )
        q_conv = filtered(taps_of(rounded(q_ref[...]), since), fq_ref[...])
        v_conv = filtered(taps_of(rounded(v_ref[...]), since_wide), fv_ref[...])
        queries = normalized(q_conv)[0] * (1.0 / math.sqrt(DK))
        queries_b = queries.astype(BF16)
        values = v_conv * sigmoid(v_conv)
        scores = [dot(queries_b[part], keys_b[part], 1, 1) for part in parts]
        solved = []
        for c, part in zip(chunks, parts):
            within, strict, reach, tail, through = decays[c]
            sides = jnp.concatenate(
                [betas[c] * reach * keys[part], twice(betas[c]) * values[part]], axis=1
            )
            inv_b = inverses[c].astype(BF16)
            ti_ref[part, :] = inv_b
            solved.append(dot(inv_b, sides.astype(BF16)).astype(BF16))
        shifts, adds = [], []
        for c, part in zip(chunks, parts):
            within, strict, reach, tail, through = decays[c]
            out_part = dot((within * scores[c]).astype(BF16), solved[c])
            state_part = dot((tail * keys[part]).astype(BF16), solved[c], 0, 0)
            qe_ref[part, :] = (reach * queries[part] - out_part[:, :DK]).astype(BF16)
            ol_ref[part, :] = out_part[:, DK:]
            shifts.append(state_part[:, :DK].astype(BF16))
            adds.append(state_part[:, DK:])
            mt_ref[part, :] = shifts[c]
            nn_ref[part, :] = adds[c]
            rl_ref[c : c + 1, :] = through
        state = adds[0]
        for c in chunks[1:]:
            moved = dot(shifts[c], state.astype(BF16))
            state = twice(decays[c][4]) * state - moved + adds[c]
        fin_ref[...] = state.astype(fin_ref.dtype)
        if with_trans:
            square_rows, square_cols = squares_iota()
            trans = jnp.where(square_rows == square_cols, 1.0, 0.0)
            for c in chunks:
                trans = decays[c][4] * trans - dot(shifts[c], trans.astype(BF16))
            outs[8][...] = trans

    return body


def slot_of(slots_ref, chunk, per_block):
    first = slots_ref[chunk // per_block] * per_block + chunk % per_block
    return pl.ds(pl.multiple_of(first * CHUNK, CHUNK), CHUNK)


def output_kernel(per_block):
    def body(
        slots_ref,
        inc_ref,
        qe_ref,
        ol_ref,
        mt_ref,
        nn_ref,
        rl_ref,
        gate_ref,
        gain_ref,
        wo_ref,
        og_ref,
        o_ref,
        st_ref,
        keep_ref,
        give_ref,
        sum_scr,
    ):
        rows = qe_ref.shape[0]
        head = pl.program_id(0)
        state = inc_ref[...].astype(F32)
        gain = gain_ref[0:1, :]
        for chunk in range(rows // CHUNK):
            first = chunk * CHUNK
            part = slice(first, first + CHUNK)
            state_b = state.astype(BF16)
            st_ref[part, :] = state_b
            pair = jnp.concatenate([qe_ref[part, :], mt_ref[part, :]], axis=0)
            both = dot(pair, state_b)
            out = both[:CHUNK] + ol_ref[part, :]
            o_ref[part, :] = out
            gate = gate_ref[PAD + first : PAD + first + CHUNK, :].astype(F32)
            norm = lax.rsqrt(jnp.mean(out * out, axis=1, keepdims=True) + 1e-05)
            gated = (out * norm * gain * (gate * sigmoid(gate))).astype(BF16)
            og_ref[slot_of(slots_ref, chunk, per_block), :] = gated
            through = twice(rl_ref[chunk : chunk + 1, :])
            state = through * state - both[CHUNK:] + nn_ref[part, :]
        product = dot(og_ref[...], wo_ref[...], 1, 1)

        @pl.when(head == 0)
        def _():
            sum_scr[...] = product

        @pl.when(head > 0)
        def _():
            sum_scr[...] += product

        @pl.when(head == pl.num_programs(0) - 1)
        def _():
            half = rows // 2
            keep_ref[...] = sum_scr[:half, :].astype(BF16)
            give_ref[...] = sum_scr[half:, :].astype(BF16)

    return body


def gate_back_kernel(per_block):
    def body(
        slots_ref,
        low_ref,
        high_ref,
        o_ref,
        gate_ref,
        gain_ref,
        qe_ref,
        mt_ref,
        rl_ref,
        wo_ref,
        do_ref,
        hg_ref,
        dgate_ref,
        dattn_ref,
        gf_ref,
        gg_ref,
        dog_scr,
    ):
        rows = qe_ref.shape[0]
        gain = gain_ref[0:1, :]
        grad_gain = jnp.zeros((1, DV), F32)
        dgate_ref[:PAD, :] = jnp.zeros((PAD, DV), BF16)
        half = rows // 2
        dog_scr[:half, :] = dot(low_ref[...], wo_ref[...])
        dog_scr[half:, :] = dot(high_ref[...], wo_ref[...])
        state = None
        for chunk in reversed(range(rows // CHUNK)):
            first = chunk * CHUNK
            part = slice(first, first + CHUNK)
            out = o_ref[part, :]
            gate = gate_ref[PAD + first : PAD + first + CHUNK, :].astype(F32)
            dog = dog_scr[slot_of(slots_ref, chunk, per_block), :]
            norm = lax.rsqrt(jnp.mean(out * out, axis=1, keepdims=True) + 1e-05)
            unit = out * norm
            sig = sigmoid(gate)
            swish = gate * sig
            grad_gain = grad_gain + jnp.sum(dog * unit * swish, axis=0, keepdims=True)
            d_gate = dog * unit * gain * (sig * (1.0 + gate * (1.0 - sig)))
            dgate_ref[PAD + first : PAD + first + CHUNK, :] = d_gate.astype(BF16)
            d_unit = dog * gain * swish
            d_out = norm * (d_unit - unit * jnp.mean(d_unit * unit, axis=1, keepdims=True))
            d_out_b = d_out.astype(BF16)
            do_ref[part, :] = d_out_b
            added = dot(qe_ref[part, :], d_out_b, 0, 0)
            hg_ref[part, :] = added
            if state is None:
                state = added
            else:
                moved = dot(mt_ref[part, :], state.astype(BF16), 0, 0)
                state = twice(rl_ref[chunk : chunk + 1, :]) * state - moved + added
        gf_ref[...] = state.astype(gf_ref.dtype)
        first_head = pl.program_id(0) == 0

        @pl.when(first_head)
        def _():
            dattn_ref[:half, :] = low_ref[...]
            dattn_ref[half:, :] = high_ref[...]
            gg_ref[...] = jnp.broadcast_to(grad_gain, gg_ref.shape)

        @pl.when(jnp.logical_not(first_head))
        def _():
            gg_ref[...] += jnp.broadcast_to(grad_gain, gg_ref.shape)

    return body


def feed_forward_kernel(
    low_ref, high_ref, cot_ref, w_ref, keep_ref, give_ref, h_ref, hid_ref, dg_ref, du_ref
):
    shards, shard = w_ref.shape[0], w_ref.shape[3]
    half = low_ref.shape[0]
    width = shards * shard
    h_ref[:half, :] = low_ref[...]
    h_ref[half:, :] = high_ref[...]

    def spans(at):
        return slice(at * shard, (at + 1) * shard)

    def entering(ref, which):
        total = None
        for at in range(shards):
            part = dot(ref[:, spans(at)], w_ref[at, which], 1, 1)
            total = part if total is None else total + part
        return total

    gate = entering(h_ref, 0)
    sig = sigmoid(gate)
    swish = gate * sig
    up = entering(h_ref, 1)
    hidden = (swish * up).astype(BF16)
    hid_ref[...] = hidden
    d_hidden = entering(cot_ref, 2)
    d_gate = (d_hidden * up * sig * (1.0 + gate * (1.0 - sig))).astype(BF16)
    d_up = (d_hidden * swish).astype(BF16)
    dg_ref[...] = d_gate
    du_ref[...] = d_up
    for at in range(shards):
        out = dot(hidden, w_ref[at, 2]).astype(BF16)
        d_h = (dot(d_gate, w_ref[at, 0]) + dot(d_up, w_ref[at, 1])).astype(BF16)
        shifted = slice(width + at * shard, width + (at + 1) * shard)
        keep_ref[:, spans(at)] = out[:half]
        give_ref[:, spans(at)] = out[half:]
        keep_ref[:, shifted] = d_h[:half]
        give_ref[:, shifted] = d_h[half:]


def back_kernel(heads):
    def body(
        q_ref,
        k_ref,
        v_ref,
        rr_ref,
        fq_ref,
        fk_ref,
        fv_ref,
        ti_ref,
        st_ref,
        mt_ref,
        rl_ref,
        hg_ref,
        gin_ref,
        do_ref,
        dext_ref,
        own_ref,
        small_ref,
        dq_scr,
        dk_scr,
        dv_scr,
    ):
        head = pl.program_id(0)
        rows = q_ref.shape[0] - PAD
        logits_at = dext_ref.shape[1] - LANES
        chunks = range(rows // CHUNK)
        parts = [slice(c * CHUNK, (c + 1) * CHUNK) for c in chunks]

        @pl.when(head == 0)
        def _():
            dext_ref[...] = jnp.zeros(dext_ref.shape, BF16)
            small_ref[...] = jnp.zeros(small_ref.shape, F32)

        grads = [None for _ in chunks]
        grad_state = gin_ref[...].astype(F32)
        for c in reversed(chunks):
            grads[c] = grad_state.astype(BF16)
            if c:
                moved = dot(mt_ref[parts[c], :], grads[c], 0, 0)
                through = twice(rl_ref[c : c + 1, :])
                grad_state = through * grad_state - moved + hg_ref[parts[c], :]
        found = [[rr_ref[at : at + 1, part] for at in range(5)] for part in parts]
        spreads = [
            spread([run, beta, start, log_decay, slope])
            for beta, log_decay, slope, run, start in found
        ]
        since = ages([one[2] for one in spreads])
        since_wide = twice(since)
        decays = [
            decay_terms(spreads[c][0], found[c][3], spreads[c][2], c * CHUNK) for c in chunks
        ]
        fq, fk, fv = fq_ref[...], fk_ref[...], fv_ref[...]
        q_taps = taps_of(rounded(q_ref[...]), since)
        k_taps = taps_of(rounded(k_ref[...]), since)
        v_taps = taps_of(rounded(v_ref[...]), since_wide)
        q_conv, k_conv, v_conv = filtered(q_taps, fq), filtered(k_taps, fk), filtered(v_taps, fv)
        q_unit, q_inv, q_gate = normalized(q_conv)
        keys, k_inv, k_gate = normalized(k_conv)
        q_scale = 1.0 / math.sqrt(DK)
        queries = q_unit * q_scale
        v_gate = sigmoid(v_conv)
        values = v_conv * v_gate
        keys_b, queries_b = keys.astype(BF16), queries.astype(BF16)
        square_rows, square_cols = squares_iota()
        later = jnp.where(square_cols >= square_rows, 1.0, 0.0).astype(BF16)
        lanes = lax.broadcasted_iota(jnp.int32, (CHUNK, LANES), 1)
        sums = [jnp.zeros((1, 1), F32), jnp.zeros((1, 1), F32)]
        for c in reversed(chunks):
            part = parts[c]
            within, strict, reach, tail, through = decays[c]
            run, b, start, log_decay, slope = spreads[c]
            k, q, v = keys[part], queries[part], values[part]
            k_b, q_b = keys_b[part], queries_b[part]
            inv_b = ti_ref[part, :]
            state_b = st_ref[part, :]
            grad_b = grads[c]
            d_out = do_ref[part, :]
            gram = dot(k_b, k_b, 1, 1)
            raw = dot(q_b, k_b, 1, 1)
            scores_b = (within * raw).astype(BF16)
            from_both = dot(k_b, jnp.concatenate([state_b, grad_b], axis=1))
            side = twice(b) * (v - twice(reach) * from_both[:, :DV])
            pseudo_b = dot(inv_b, side.astype(BF16)).astype(BF16)
            d_pseudo = dot(scores_b, d_out, 0, 0) + twice(tail) * from_both[:, DV:]
            d_side = dot(inv_b, d_pseudo.astype(BF16), 0, 0)
            d_side_b = d_side.astype(BF16)
            out_and_side = jnp.concatenate([d_out, d_side_b], axis=0)
            squares = dot(out_and_side, pseudo_b, 1, 1)
            by_state = dot(out_and_side, state_b, 1, 1)
            by_grad = dot(pseudo_b, grad_b, 1, 1)
            out_state, side_state = by_state[:CHUNK], by_state[CHUNK:]
            d_raw = within * squares[:CHUNK]
            solve_grad = squares[CHUNK:] * strict
            d_gram = -(b * solve_grad)
            d_raw_b, d_gram_b = d_raw.astype(BF16), d_gram.astype(BF16)
            d_q = reach * out_state + dot(d_raw_b, k_b)
            d_k = tail * by_grad - b * reach * side_state
            d_k = d_k + dot(d_raw_b, q_b, 0, 0) + dot(d_gram_b, k_b) + dot(d_gram_b, k_b, 0, 0)
            dv_scr[part, :] = twice(b) * d_side
            dq_scr[part, :] = d_q
            dk_scr[part, :] = d_k
            side_key = row_sum(k * side_state)
            d_beta = row_sum(d_side * v) - row_sum(solve_grad * gram) - reach * side_key
            weight = d_raw * raw + d_gram * gram
            reach_part = reach * (row_sum(q * out_state) - b * side_key)
            tail_part = tail * row_sum(k * by_grad)
            d_run = row_sum(weight - weight.T) + reach_part - tail_part
            kept = jnp.sum(grad_b.astype(F32) * state_b.astype(F32), axis=0, keepdims=True)
            kept = through * row_sum(kept)
            end_grad = jnp.sum(tail_part, axis=0, keepdims=True) + kept
            run_hi, run_lo = split_two(d_run)
            d_decay = dot(later, run_hi) + dot(later, run_lo) + end_grad
            d_alpha = d_decay * slope
            d_beta_logit = d_beta * b * (1.0 - b)
            sums[0] = sums[0] + jnp.sum((d_decay * log_decay)[:, :1], axis=0, keepdims=True)
            sums[1] = sums[1] + jnp.sum(d_alpha[:, :1], axis=0, keepdims=True)
            place = slice(PAD + c * CHUNK, PAD + (c + 1) * CHUNK)
            held = dext_ref[place, logits_at:].astype(F32)
            held = jnp.where(lanes == head, d_alpha, held)
            held = jnp.where(lanes == heads + head, d_beta_logit, held)
            dext_ref[place, logits_at:] = held.astype(BF16)

        def channel_back(d_conv, taps, filters, since_here, at, width):
            place = pl.ds(pl.multiple_of(at, LANES), width)
            dext_ref[:, place] = unfiltered(d_conv, filters, since_here).astype(BF16)
            for shift in range(KCONV):
                grad = jnp.sum(d_conv * taps[shift], axis=0, keepdims=True)
                small_ref[KCONV - 1 - shift : KCONV - shift, place] = grad

        def unit_back(d_unit, unit, inv, conv, gate):
            d_active = inv * (d_unit - unit * row_sum(d_unit * unit))
            return d_active * gate * (1.0 + conv * (1.0 - gate))

        d_q_conv = unit_back(dq_scr[...] * q_scale, q_unit, q_inv, q_conv, q_gate)
        d_k_conv = unit_back(dk_scr[...], keys, k_inv, k_conv, k_gate)
        d_v_conv = dv_scr[...] * v_gate * (1.0 + v_conv * (1.0 - v_gate))
        channel_back(d_q_conv, q_taps, fq, since, head * DK, DK)
        channel_back(d_k_conv, k_taps, fk, since, (heads + head) * DK, DK)
        channel_back(d_v_conv, v_taps, fv, since_wide, 2 * heads * DK + head * DV, DV)
        rate_rows = lax.broadcasted_iota(jnp.int32, (8, LANES), 0)
        rate_lanes = lax.broadcasted_iota(jnp.int32, (8, LANES), 1)
        rates = jnp.where(rate_rows == 0, sums[0], jnp.where(rate_rows == 1, sums[1], 0.0))
        small_ref[:, logits_at:] += jnp.where(rate_lanes == head, rates, 0.0)

        @pl.when(head == pl.num_programs(0) - 1)
        def _():
            own_ref[...] = dext_ref[...]

    return body


def whole(shape):
    return pl.BlockSpec((None,) + shape, lambda m, h, *_: (m, 0, 0))


def per_head(shape):
    return pl.BlockSpec((None, None) + shape, lambda m, h, *_: (m, h, 0, 0))


def columns(rows, width, skip=0):
    return pl.BlockSpec((None, rows, width), lambda m, h, *_: (m, 0, skip + h))


def filter_cols(width):
    return pl.BlockSpec((KCONV, width), lambda m, h, *_: (0, h))


def fixed(shape):
    return pl.BlockSpec(shape, lambda m, h, *_: (0, 0))


def kernel_params(axes=2):
    return pltpu.CompilerParams(
        dimension_semantics=("arbitrary",) * axes, vmem_limit_bytes=VMEM_BYTES
    )


def busy(microseconds):
    return pl.CostEstimate(
        flops=0, transcendentals=0, bytes_accessed=int(microseconds * 3.3e6)
    )


class Shared:
    def __init__(self, micros):
        self.micros = micros
        self.arrays = None

    def call(self, body, micro, grid, prefetch, operands, in_specs, out, scratch, name, cost):
        shared = [at for at, one in enumerate(out) if one[4]]
        held = [] if self.arrays is None else self.arrays
        skip = len(prefetch) + len(operands)

        def wrapped(*refs):
            body(*refs[:skip], *refs[skip + len(held) :])

        out_shape, out_specs = [], []
        for shape, dtype, block, index, is_shared in out:
            leading = (self.micros,) if is_shared else (1,)
            first = micro if is_shared else 0
            out_shape.append(jax.ShapeDtypeStruct(leading + shape, dtype))
            out_specs.append(
                pl.BlockSpec((None,) + block, lambda *g, i=index, f=first: (f,) + i(*g))
            )
        results = pl.pallas_call(
            wrapped,
            grid_spec=pltpu.PrefetchScalarGridSpec(
                num_scalar_prefetch=len(prefetch),
                grid=grid,
                in_specs=in_specs + [pl.BlockSpec(memory_space=pl.ANY)] * len(held),
                out_specs=out_specs,
                scratch_shapes=scratch,
            ),
            out_shape=out_shape,
            input_output_aliases={skip + at: shared[at] for at in range(len(held))},
            compiler_params=kernel_params(len(grid)),
            cost_estimate=busy(cost),
            name=name,
        )(*prefetch, *operands, *held)
        self.arrays = [results[at] for at in shared]
        return [one for at, one in enumerate(results) if at not in shared]


def by_head(h, *_):
    return (h, 0, 0)


def by_column(h, *_):
    return (0, h)


def at_origin(*_):
    return (0, 0)


def mixer_specs(heads, padded):
    return [
        columns(padded, DK),
        columns(padded, DK, heads),
        columns(padded, DV, heads * DK * 2 // DV),
    ]


def filter_specs():
    return [filter_cols(DK), filter_cols(DK), filter_cols(DV)]


def run_local(ends, pre, filters, params, heads, with_trans):
    micros, padded = pre.shape[0], pre.shape[1]
    rows = padded - PAD
    logits_at = pre.shape[2] // LANES - 1
    shapes = [
        ((rows, DK), BF16),
        ((rows, heads * DV), F32),
        ((rows, DK), BF16),
        ((rows, DV), F32),
        ((rows, CHUNK), BF16),
        ((8, LANES), F32),
        ((8, rows), F32),
        ((DK, DV), BF16),
    ]
    if with_trans:
        shapes.append(((DK, DK), F32))
    out_shape, out_specs = [], []
    for at, (shape, dtype) in enumerate(shapes):
        if at == 1:
            out_shape.append(jax.ShapeDtypeStruct((micros,) + shape, dtype))
            out_specs.append(columns(rows, DV))
        else:
            out_shape.append(jax.ShapeDtypeStruct((micros, heads) + shape, dtype))
            out_specs.append(per_head(shape))
    logits_spec = pl.BlockSpec((None, padded, LANES), lambda m, h, *_: (m, 0, logits_at))
    return pl.pallas_call(
        local_kernel(heads, with_trans),
        grid_spec=pltpu.PrefetchScalarGridSpec(
            num_scalar_prefetch=1,
            grid=(micros, heads),
            in_specs=mixer_specs(heads, padded)
            + [logits_spec]
            + filter_specs()
            + [fixed((8, LANES))],
            out_specs=out_specs,
        ),
        out_shape=out_shape,
        compiler_params=kernel_params(),
        cost_estimate=busy(10.0 * micros),
        name="mixer_local",
    )(ends, pre, pre, pre, pre, *filters, params)


def one_head(shape):
    return pl.BlockSpec((None, None) + shape, lambda h, *_: (0, h, 0, 0))


def one_column(rows, width, skip=0):
    return pl.BlockSpec((None, rows, width), lambda h, *_: (0, 0, skip + h))


def one_whole(shape, micro=0):
    return pl.BlockSpec((None,) + shape, lambda *_: (micro,) + (0,) * len(shape))


def gain_spec():
    return pl.BlockSpec((8, DV), at_origin)


def run_output(shared, micro, slots, incoming, saved, gate, gain, w_out):
    qe, ol, mt, nn, ti, rl, rr = saved
    heads, rows = qe.shape[1:3]
    width = w_out.shape[0]
    half = (rows // 2, width)
    return shared.call(
        output_kernel(rows // slots.shape[0] // CHUNK),
        micro,
        (heads,),
        [slots],
        [incoming, qe, ol, mt, nn, rl, gate, gain, w_out],
        [
            one_head((DK, DV)),
            one_head((rows, DK)),
            one_column(rows, DV),
            one_head((rows, DK)),
            one_head((rows, DV)),
            one_head((8, LANES)),
            one_column(rows + PAD, DV),
            gain_spec(),
            pl.BlockSpec((width, DV), lambda h, *_: (0, heads + h)),
        ],
        [
            ((rows, heads * DV), BF16, (rows, DV), by_column, True),
            ((rows, heads * DV), F32, (rows, DV), by_column, False),
            ((heads, rows, DV), BF16, (None, rows, DV), by_head, False),
            (half, BF16, half, at_origin, False),
            (half, BF16, half, at_origin, False),
        ],
        [pltpu.VMEM((rows, width), F32)],
        "mixer_output",
        6.0,
    )


def run_gate_back(shared, micro, slots, d_attn, out, gate, gain, saved, w_out):
    qe, ol, mt, nn, ti, rl, rr = saved
    heads, rows = qe.shape[1:3]
    width = w_out.shape[0]
    return shared.call(
        gate_back_kernel(rows // slots.shape[0] // CHUNK),
        micro,
        (heads,),
        [slots],
        [*d_attn, out, gate, gain, qe, mt, rl, w_out],
        [one_whole((rows // 2, width))] * 2
        + [
            one_column(rows, DV),
            one_column(rows + PAD, DV),
            gain_spec(),
            one_head((rows, DK)),
            one_head((rows, DK)),
            one_head((8, LANES)),
            pl.BlockSpec((width, DV), lambda h, *_: (0, heads + h)),
        ],
        [
            ((rows, heads * DV), BF16, (rows, DV), by_column, False),
            ((heads, rows, DV), F32, (None, rows, DV), by_head, False),
            ((rows + PAD, heads * DV), BF16, (rows + PAD, DV), by_column, True),
            ((rows, width), BF16, (rows, width), at_origin, True),
            ((heads, DK, DV), BF16, (None, DK, DV), by_head, False),
            ((8, DV), F32, (8, DV), at_origin, False),
        ],
        [pltpu.VMEM((rows, DV), F32)],
        "mixer_gate_back",
        6.0,
    )


def run_feed_forward(shared, micro, h_two, cot, weights):
    rows, width = cot.shape[1:]
    hidden = weights.shape[2]
    sums = (rows // 2, 2 * width)
    kept = (rows, hidden)
    return shared.call(
        feed_forward_kernel,
        micro,
        (1,),
        [],
        [*h_two, cot, weights],
        [one_whole((rows // 2, width))] * 2
        + [
            one_whole((rows, width), micro),
            pl.BlockSpec(weights.shape, lambda *_: (0, 0, 0, 0)),
        ],
        [
            (sums, BF16, sums, at_origin, False),
            (sums, BF16, sums, at_origin, False),
            ((rows, width), BF16, (rows, width), at_origin, True),
            (kept, BF16, kept, at_origin, True),
            (kept, BF16, kept, at_origin, True),
            (kept, BF16, kept, at_origin, True),
        ],
        [],
        "feed_forward",
        9.0,
    )


def run_back(shared, micro, pre, filters, saved, states, added, incoming, d_out):
    qe, ol, mt, nn, ti, rl, rr = saved
    heads, rows = qe.shape[1:3]
    padded = rows + PAD
    width = pre.shape[2]
    return shared.call(
        back_kernel(heads),
        micro,
        (heads,),
        [],
        [pre, pre, pre, rr, *filters, ti, states, mt, rl, added, incoming, d_out],
        [
            one_column(padded, DK),
            one_column(padded, DK, heads),
            one_column(padded, DV, heads * DK * 2 // DV),
            one_head((8, rows)),
            pl.BlockSpec((KCONV, DK), by_column),
            pl.BlockSpec((KCONV, DK), by_column),
            pl.BlockSpec((KCONV, DV), by_column),
            one_head((rows, CHUNK)),
            one_head((rows, DV)),
            one_head((rows, DK)),
            one_head((8, LANES)),
            one_head((rows, DV)),
            one_head((DK, DV)),
            one_column(rows, DV),
        ],
        [
            ((padded, width), BF16, (padded, width), at_origin, True),
            ((padded, width), BF16, (padded, width), at_origin, False),
            ((8, width), F32, (8, width), at_origin, False),
        ],
        [
            pltpu.VMEM((rows, DK), F32),
            pltpu.VMEM((rows, DK), F32),
            pltpu.VMEM((rows, DV), F32),
        ],
        "mixer_back",
        14.0,
    )


def passed_along(block, axis, distance):
    devices = range(lax.axis_size(axis))
    route = [(i - distance, i) for i in devices if i - distance in devices]
    return lax.ppermute(block, axis, route)


def swapped(block, axis, bit):
    return lax.ppermute(block, axis, [(i, i ^ bit) for i in range(lax.axis_size(axis))])


def reversed_bits(value, size):
    out, bit = 0, 1
    while bit < size:
        out = out * 2 + (value // bit) % 2
        bit *= 2
    return out


def to_slots(rows, axis):
    place = lax.axis_index(axis)
    size = lax.axis_size(axis)
    count = rows.shape[1] // size
    owners = [place ^ reversed_bits(slot, size) for slot in range(size)]
    return jnp.concatenate(
        [lax.dynamic_slice_in_dim(rows, owner * count, count, 1) for owner in owners], axis=1
    )


def slot_table(axis):
    size = lax.axis_size(axis)
    away = jnp.arange(size, dtype=jnp.int32) ^ lax.axis_index(axis)
    return reversed_bits(away, size).astype(jnp.int32)


class Scatter:
    def __init__(self, keep, give, axis):
        self.axis, self.bit, self.keep = axis, 1, keep.astype(F32)
        self.send(give)

    def send(self, give):
        self.sent = give.astype(BF16)
        self.got = swapped(self.sent, self.axis, self.bit)

    def advance(self, *waits):
        parts = self.keep + after(self.got, *waits).astype(F32)
        self.bit *= 2
        if self.bit >= lax.axis_size(self.axis):
            return parts
        half = parts.shape[1] // 2
        self.keep = parts[:, :half]
        self.send(parts[:, half:])
        return None

    def finish(self, *waits):
        result = None
        while result is None:
            result = self.advance(*waits)
        return result


class Gather:
    def __init__(self, part, axis):
        self.axis, self.bit = axis, lax.axis_size(axis) // 2
        self.send(part)

    def send(self, part):
        self.sent = part
        self.got = swapped(part, self.axis, self.bit)

    def advance(self, *waits):
        got = after(self.got, *waits)
        if self.bit == 1:
            return self.sent, got
        self.bit //= 2
        self.send(jnp.concatenate([self.sent, got], axis=1))
        return None

    def finish(self, *waits):
        result = None
        while result is None:
            result = self.advance(*waits)
        return result


def after(value, *others):
    return lax.optimization_barrier((value,) + others)[0] if others else value


class GatherWeights:
    def __init__(self, rows):
        devices = lax.axis_size("fsdp")
        self.rows = rows
        self.side = lax.axis_index("seq") % 2
        half = rows.shape[0] // 2
        self.mine = lax.dynamic_slice_in_dim(rows, self.side * half, half, 0)
        self.got = [
            lax.ppermute(self.mine, "fsdp", [(i, (i + away) % devices) for i in range(devices)])
            for away in range(1, devices)
        ]

    def swap(self, *waits):
        self.got = [after(one, *waits) for one in self.got]
        self.other = [swapped(one, "seq", 1) for one in self.got]

    def result(self, *waits):
        devices = lax.axis_size("fsdp")
        place, side = lax.axis_index("fsdp"), self.side
        count, width = self.rows.shape
        half = (count // 2, width)
        sources = [(place - away) % devices for away in range(devices)]
        where = jnp.stack(sources + [side]).astype(jnp.int32)
        pieces = self.got + [after(one, *waits) for one in self.other]

        def body(where_ref, own_ref, *refs):
            out_ref = refs[-1]
            side = where_ref[devices]
            out_ref[where_ref[0]] = own_ref[...]
            for at in range(1, devices):
                out_ref[where_ref[at], side] = refs[at - 1][...]
                out_ref[where_ref[at], 1 - side] = refs[devices + at - 2][...]

        out = pl.pallas_call(
            body,
            grid_spec=pltpu.PrefetchScalarGridSpec(
                num_scalar_prefetch=1,
                grid=(1,),
                in_specs=[pl.BlockSpec((2,) + half, lambda *_: (0, 0, 0))]
                + [pl.BlockSpec(half, at_origin)] * len(pieces),
                out_specs=pl.BlockSpec((devices, 2) + half, lambda *_: (0, 0, 0, 0)),
            ),
            out_shape=jax.ShapeDtypeStruct((devices, 2) + half, self.rows.dtype),
            compiler_params=kernel_params(1),
            cost_estimate=busy(2.0),
            name="place_weights",
        )(where, self.rows.reshape((2,) + half), *pieces)
        return out.reshape(devices * count, width)


class SmallSum:
    def __init__(self, value):
        self.value = value
        self.left = []
        for axis in ("head", "seq", "fsdp"):
            bit = 1
            while bit < lax.axis_size(axis):
                self.left.append((axis, bit))
                bit *= 2
        self.got = None

    def step(self, *waits):
        if self.got is not None:
            self.value = self.value + after(self.got, *waits)
            self.got = None
        if self.left:
            axis, bit = self.left.pop(0)
            self.got = swapped(self.value, axis, bit)
        return self.value

    def finish(self, *waits):
        while self.got is not None:
            self.step(*waits)
        return self.value


class Reduce:
    def __init__(self, grad):
        self.rows = grad.shape[0]
        self.bit = lax.axis_size("seq") // 2
        self.send(grad)

    def send(self, grad):
        half = grad.shape[0] // 2
        mine = (lax.axis_index("seq") // self.bit) % 2
        self.sent = lax.dynamic_slice_in_dim(grad, (1 - mine) * half, half, 0).astype(BF16)
        self.keep = lax.dynamic_slice_in_dim(grad, mine * half, half, 0)
        self.got = swapped(self.sent, "seq", self.bit)

    def spread(self, *waits):
        grad = self.keep.astype(F32) + after(self.got, *waits).astype(F32)
        while self.bit > 1:
            self.bit //= 2
            self.send(grad)
            grad = self.keep.astype(F32) + self.got.astype(F32)
        devices, place = lax.axis_size("fsdp"), lax.axis_index("fsdp")
        count = grad.shape[0] // devices
        self.total = lax.dynamic_slice_in_dim(grad, place * count, count, 0)
        self.gives, self.gots = [], []
        for away in range(1, devices):
            owner = (place + away) % devices
            give = lax.dynamic_slice_in_dim(grad, owner * count, count, 0).astype(BF16)
            route = [(i, (i + away) % devices) for i in range(devices)]
            self.gives.append(give)
            self.gots.append(lax.ppermute(give, "fsdp", route))

    def finish(self, *waits):
        total = self.total
        for got in self.gots:
            total = total + after(got, *waits).astype(F32)
        return total


def state_from_before(final, trans):
    state = None
    for _ in range(lax.axis_size("seq") - 1):
        sent = final
        if state is not None:
            moved = jnp.einsum("mhij,mhjv->mhiv", trans, state.astype(F32), precision=BEST)
            sent = (final.astype(F32) + moved).astype(BF16)
        state = passed_along(sent, "seq", 1)
    return state


def grad_from_after(first, trans):
    grad = None
    for _ in range(lax.axis_size("seq") - 1):
        sent = first
        if grad is not None:
            moved = jnp.einsum("mhji,mhjv->mhiv", trans, grad.astype(F32), precision=BEST)
            sent = (first.astype(F32) + moved).astype(BF16)
        grad = passed_along(sent, "seq", -1)
    return grad


def rms_unit(values):
    return values * lax.rsqrt(jnp.mean(values * values, axis=-1, keepdims=True) + 1e-05)


def rms_back(values, gain, d_out):
    inv = lax.rsqrt(jnp.mean(values * values, axis=-1, keepdims=True) + 1e-05)
    unit = values * inv
    d_unit = d_out * gain
    d_values = inv * (d_unit - unit * jnp.mean(d_unit * unit, axis=-1, keepdims=True))
    return d_values, d_out * unit


def mat(left, right):
    return lax.dot_general(left, right, (((2,), (0,)), ((), ())), preferred_element_type=F32)


def mat_t(left, right):
    return lax.dot_general(left, right, (((2,), (1,)), ((), ())), preferred_element_type=F32)


def grad_of(left, right):
    left = left.reshape(-1, left.shape[2])
    right = right.reshape(-1, right.shape[2])
    part = lax.dot_general(left, right, (((0,), (0,)), ((), ())), preferred_element_type=F32)
    return part.astype(BF16)


def scatter_grad(grad):
    return lax.psum_scatter(grad, SEQ_FSDP, scatter_dimension=0, tiled=True).astype(F32)


def per_device(
    block_input,
    cotangent,
    doc_lengths,
    attn_gain,
    w_query,
    w_key,
    w_value,
    w_gate,
    w_alpha,
    w_beta,
    conv_query,
    conv_key,
    conv_value,
    a_log,
    dt_bias,
    head_gain,
    w_out,
    mlp_gain,
    w_ffgate,
    w_ffup,
    w_down,
):
    head_devices = lax.axis_size("head")
    seq_devices = lax.axis_size("seq")
    owners = seq_devices * lax.axis_size("fsdp")
    seq_place = lax.axis_index("seq")
    head_place = lax.axis_index("head")
    tok_count, model = block_input.shape[2:]
    row_count = tok_count // head_devices
    row_first = head_place * row_count
    heads = w_query.shape[1] // DK
    hidden_width = w_ffgate.shape[1]
    qw, vw = heads * DK, heads * DV
    rates_at = 2 * qw + vw

    x_own = block_input[:, 0]
    halo = passed_along(x_own[:, tok_count - PAD :], "seq", 1)
    w_first = jnp.concatenate([w_query, w_key, w_value, w_alpha, w_beta], axis=1)
    w_first = jnp.pad(w_first, ((0, 0), (0, LANES - 2 * heads)))
    w_second = jnp.concatenate([w_gate, w_out.T], axis=1)
    w_third = jnp.stack([w_ffgate.T, w_ffup.T, w_down])
    x_pad = jnp.concatenate([halo, x_own], axis=1).astype(F32)
    h_one = (rms_unit(x_pad) * attn_gain).astype(BF16)
    cot = to_slots(cotangent[:, 0], "head")
    slots = slot_table("head")
    first = GatherWeights(w_first)
    first.swap()
    second = GatherWeights(after(w_second, *first.got))
    w_first, h_one, cot, w_third = lax.optimization_barrier(
        (first.result(), h_one, cot, w_third)
    )
    w_third = lax.all_gather(after(w_third, *second.got), "fsdp", axis=0)

    conv_q = lax.dynamic_slice_in_dim(conv_query, head_place * qw, qw, 1)
    conv_k = lax.dynamic_slice_in_dim(conv_key, head_place * qw, qw, 1)
    conv_v = lax.dynamic_slice_in_dim(conv_value, head_place * vw, vw, 1)
    filters = (conv_q, conv_k, conv_v)
    rates = jnp.stack(
        [
            lax.dynamic_slice_in_dim(a_log, head_place * heads, heads, 0),
            lax.dynamic_slice_in_dim(dt_bias, head_place * heads, heads, 0),
        ]
    )
    params = jnp.pad(rates, ((0, 6), (0, LANES - heads)))
    gain_rows = jnp.broadcast_to(head_gain[None], (8, DV))
    lengths = doc_lengths[:, 0]
    docs = lengths.shape[1]
    counted = jnp.arange(docs)[None, :] < jnp.arange(docs + 1)[:, None]
    ends = jnp.sum(jnp.where(counted[None], lengths[:, None, :], 0), axis=2)
    ends = (ends - seq_place * tok_count).astype(jnp.int32)

    micros = range(block_input.shape[0])
    count = len(micros)
    outputs, forwards, gate_backs, backs = (Shared(count) for _ in range(4))
    x_parts = [
        lax.dynamic_slice_in_dim(x_own[m : m + 1], row_first, row_count, 1).astype(F32)
        for m in micros
    ]
    pres, found, saves, transes = {}, {}, {}, {}
    states_in, gates, outs, statess = {}, {}, {}, {}
    attn, rows_two, x_ones, sums, back_sums, back_rows = {}, {}, {}, {}, {}, {}
    y_parts, mlp_terms, d_x_ones = {}, {}, {}
    backed, exts, smalls, gain_sums = {}, {}, {}, {}

    def project(m):
        pres[m] = mat(h_one[m : m + 1], w_first)
        return pres[m]

    def local(m, *waits):
        found[m] = run_local(
            ends[m : m + 1], after(pres[m], *waits), filters, params, heads, seq_devices > 2
        )
        saves[m] = tuple(found[m][:7])
        transes[m] = found[m][8] if seq_devices > 2 else None
        states_in[m] = state_from_before(found[m][7], transes[m])
        return found[m][5]

    def project_gate(m):
        gates[m] = mat(h_one[m : m + 1], w_g)
        return gates[m]

    def output(m, *waits):
        outs[m], statess[m], keep, give = run_output(
            outputs,
            m,
            slots,
            after(states_in[m], *waits),
            saves[m],
            gates[m],
            gain_rows,
            w_second,
        )
        attn[m] = Scatter(keep, give, "head")
        return keep

    def to_feed_forward(m, summed):
        x_ones[m] = x_parts[m] + summed
        rows_two[m] = Gather((rms_unit(x_ones[m]) * mlp_gain).astype(BF16), "head")

    def feed_forward(m, halves, *waits):
        low, high = halves
        keep, give = run_feed_forward(forwards, m, (after(low, *waits), high), cot, w_third)
        sums[m] = Scatter(keep, give, "head")
        return keep

    def to_gate_back(m, both):
        y_parts[m] = (x_ones[m] + both[..., :model]).astype(BF16)
        d_norm, terms = rms_back(x_ones[m], mlp_gain, both[..., model:])
        mlp_terms[m] = jnp.sum(terms, axis=(0, 1))
        d_x_ones[m] = cot[m : m + 1, :row_count].astype(F32) + d_norm
        back_rows[m] = Gather(d_x_ones[m].astype(BF16), "head")

    def gate_back(m, halves, *waits):
        low, high = halves
        d_out, added, grad_first, gain_sum = run_gate_back(
            gate_backs,
            m,
            slots,
            (after(low, *waits), high),
            outs[m],
            gates[m],
            gain_rows,
            saves[m],
            w_second,
        )
        gain_sums[m] = gain_sum
        backed[m] = (d_out, added, grad_from_after(grad_first, transes[m]))
        return gain_sum

    def back(m, *waits):
        d_out, added, grad_incoming = backed[m]
        exts[m], smalls[m] = run_back(
            backs,
            m,
            pres[m],
            filters,
            saves[m],
            statess[m],
            added,
            after(grad_incoming, *waits),
            d_out,
        )
        return smalls[m]

    project(0)
    done = local(0)
    project(1)
    second.swap(done)
    done = local(1, done, *second.got)
    w_second = second.result(done)
    w_g = w_second[:, :vw]
    project_gate(0)
    done = output(0, done)
    moved = project(2)
    attn[0].advance(moved)
    done = local(2, done, attn[0].sent)
    project_gate(1)
    to_feed_forward(0, attn[0].finish(done))
    done = output(1, done, rows_two[0].sent)
    moved = project_gate(2)
    attn[1].advance(moved)
    rows_two[0].advance(done)
    done = output(2, done, attn[1].sent, rows_two[0].sent)
    halves = rows_two[0].finish(done)
    to_feed_forward(1, attn[1].finish(halves[1]))
    attn[2].advance(halves[1])
    done = feed_forward(0, halves, attn[2].sent, rows_two[1].sent)
    rows_two[1].advance(done)
    to_feed_forward(2, attn[2].finish(done))
    halves = rows_two[1].finish(sums[0].sent, rows_two[2].sent)
    sums[0].advance(halves[1])
    done = feed_forward(1, halves, done, sums[0].sent)
    rows_two[2].advance(done)
    to_gate_back(0, sums[0].finish(done))
    halves = rows_two[2].finish(sums[1].sent, back_rows[0].sent)
    sums[1].advance(halves[1])
    back_rows[0].advance(halves[1])
    done = feed_forward(2, halves, done, sums[1].sent, back_rows[0].sent)

    h_two, hid, d_ffg, d_ffu = forwards.arrays
    halves = back_rows[0].finish(done)
    to_gate_back(1, sums[1].finish(done))
    sums[2].advance(done)
    done = gate_back(0, halves, back_rows[1].sent, sums[2].sent)
    back_rows[1].advance(done)
    to_gate_back(2, sums[2].finish(done))
    ff_grads = [
        grad_of(after(d_ffg, done, back_rows[1].sent, back_rows[2].sent), h_two),
        grad_of(d_ffu, h_two),
        grad_of(hid, cot),
    ]
    ff_grads = jnp.stack(ff_grads).reshape(3, hidden_width, owners, -1)
    ff_grads = jnp.transpose(ff_grads, (2, 0, 1, 3))
    halves = back_rows[1].finish(ff_grads)
    back_rows[2].advance(ff_grads)
    done = gate_back(1, halves, back_rows[2].sent, backed[0][2])
    ff_shard = scatter_grad(ff_grads)[0]
    done = back(0, done)
    done = gate_back(2, back_rows[2].finish(done), done, backed[1][2])
    d_gates, d_attn_rows = gate_backs.arrays
    side_grads = jnp.concatenate(
        [grad_of(h_one, d_gates), grad_of(d_attn_rows, outputs.arrays[0])], axis=1
    )
    side = Reduce(side_grads)
    done = back(1, done, side.sent, backed[2][2])
    side.spread(done)

    dx_parts, attn_terms, d_h_sums = {}, {}, {}

    def to_input(m, *waits):
        d_ext, d_gate = exts[m], d_gates[m : m + 1]
        rims = after(passed_along(d_ext[:, :PAD], "seq", -1), *waits)
        d_h_one = mat_t(d_ext[:, PAD:], w_first) + mat_t(d_gate[:, PAD:], w_g)
        d_rim = mat_t(rims, w_first)
        d_h_one = d_h_one + jnp.pad(d_rim, ((0, 0), (tok_count - PAD, 0), (0, 0)))
        unit_own = rms_unit(x_own[m : m + 1].astype(F32))
        attn_terms[m] = jnp.sum(d_h_one * unit_own, axis=(0, 1))
        d_h_one = to_slots(d_h_one.astype(BF16), "head")
        half = tok_count // 2
        d_h_sums[m] = Scatter(d_h_one[:, :half], d_h_one[:, half:], "head")

    def to_end(m, summed):
        d_first, _ = rms_back(x_parts[m], attn_gain, summed)
        dx_parts[m] = d_x_ones[m] + d_first

    to_input(0, done)
    done = back(2, done, *side.gives, d_h_sums[0].sent)
    mix_grad = grad_of(h_one, backs.arrays[0])
    mix = [Reduce(mix_grad[:, : 2 * qw]), Reduce(mix_grad[:, 2 * qw :])]
    to_input(2, mix[0].sent, mix[1].sent)
    to_input(1, mix[0].sent, mix[1].sent)

    small = sum(jnp.sum(one, axis=0) for one in smalls.values())
    rate_sums = small[:2, rates_at : rates_at + heads]
    taps = small[:KCONV]
    sizes = (conv_query.shape[1], conv_key.shape[1], conv_value.shape[1])
    widened = [
        lax.dynamic_update_slice_in_dim(
            jnp.zeros((KCONV, size), F32), taps[:, at : at + width], head_place * width, 1
        )
        for size, at, width in zip(sizes, (0, qw, 2 * qw), (qw, qw, vw))
    ]
    widened_rates = lax.dynamic_update_slice_in_dim(
        jnp.zeros((2, a_log.shape[0]), F32), rate_sums, head_place * heads, 1
    )
    gain_sum = sum(jnp.sum(one[:, 0], axis=0) for one in gain_sums.values())
    pieces = [sum(attn_terms.values()), sum(mlp_terms.values()), gain_sum] + widened + [widened_rates]
    packed = jnp.concatenate([piece.reshape(-1) for piece in pieces])
    length = packed.shape[0]
    packed = jnp.pad(packed, (0, -length % 1024)).reshape(-1, LANES)
    small_sum = SmallSum(packed)
    small_sum.step()
    d_h_sums[0].advance(small_sum.value)
    side_shard = side.finish(small_sum.value)
    ff_shard = [ff_shard[0].T, ff_shard[1].T, ff_shard[2]]
    block_output = jnp.concatenate([y_parts[m] for m in micros])
    mix[0].spread(side_shard, block_output, d_h_sums[0].sent)
    d_h_sums[2].advance(*mix[0].gives)
    d_h_sums[1].advance(*mix[0].gives)
    small_sum.step(*mix[0].gives)
    to_end(0, d_h_sums[0].finish(d_h_sums[1].sent))
    mix[1].spread(small_sum.value, *ff_shard, dx_parts[0])
    small_sum.step(*mix[1].gives)
    to_end(2, d_h_sums[2].finish(small_sum.value))
    to_end(1, d_h_sums[1].finish(small_sum.value))
    input_grad = jnp.concatenate([dx_parts[m] for m in micros])
    small_sum.step(input_grad)
    total = mix[0].finish(small_sum.value)
    small_sum.step(total)
    shard_mix = jnp.concatenate([total, mix[1].finish(small_sum.value)], axis=1)
    packed = small_sum.finish().reshape(-1)
    totals, at = [], 0
    for piece in pieces:
        totals.append(packed[at : at + piece.size].reshape(piece.shape))
        at += piece.size
    tot_attn, tot_mlp, tot_head, tot_cq, tot_ck, tot_cv, tot_rates = totals
    return (
        block_output[:, None],
        input_grad[:, None],
        shard_mix[:, :qw],
        shard_mix[:, qw : 2 * qw],
        shard_mix[:, 2 * qw : rates_at],
        side_shard[:, :vw],
        shard_mix[:, rates_at : rates_at + heads],
        shard_mix[:, rates_at + heads : rates_at + 2 * heads],
        side_shard[:, vw:].T,
        ff_shard[0],
        ff_shard[1],
        ff_shard[2],
        tot_attn,
        tot_mlp,
        tot_head,
        tot_cq,
        tot_ck,
        tot_cv,
        tot_rates[0],
        tot_rates[1],
    )


def solution(mesh):
    rows_by_fsdp = P("fsdp", "head")
    cols_by_fsdp = P("head", "fsdp")
    tokens = P(None, "fsdp", "seq", None)
    return jax.shard_map(
        per_device,
        mesh=mesh,
        in_specs=(
            (tokens, tokens, P(None, "fsdp", None), P())
            + (rows_by_fsdp,) * 6
            + (P(),) * 6
            + (cols_by_fsdp, P(), rows_by_fsdp, rows_by_fsdp, cols_by_fsdp)
        ),
        out_specs=(
            (P(None, "fsdp", ("seq", "head"), None),) * 2
            + (P(SEQ_FSDP, "head"),) * 6
            + (P("head", SEQ_FSDP), P(SEQ_FSDP, "head"), P(SEQ_FSDP, "head"))
            + (P("head", SEQ_FSDP),)
            + (P(),) * 8
        ),
        check_vma=False,
    )
```

time: 3110 us -> 514 us (0.17)
  waiting for transfers between devices: 1210 us -> 70.8 us
  other arithmetic: 732 us -> 56.3 us
  matrix products: 569 us -> 66.7 us
  local copies, waits for them, and re-layouts: 374 us -> 57.4 us
  Pallas kernels: 0 us -> 156 us
  blocking collectives: 126 us -> 0 us
  starting transfers between devices: 33.8 us -> 82 us
    reduce_scatter x20 -> x1, waiting for transfers between devices: 797 us -> 0.01 us  [scatter_grad(): lax.psum_scatter(grad, SEQ_FSDP, scatter_dimension=0, tiled=True)]
    another operation x303 -> x2, other arithmetic: 523 us -> 2.97 us  [the longest x1 2.38 us: per_device(): w_third = jnp.stack([w_ffgate.T, w_ffup.T, w_down])]
    dot_general x666 -> x21, matrix products: 521 us -> 66.7 us  [the longest x9 25.1 us: mat_t(): lax.dot_general(left, right, (((2,), (1,)), ((), ())), preferred_element_...]
    all_gather x12 -> x1, waiting for transfers between devices: 174 us -> 0.01 us  [per_device(): w_third = lax.all_gather(after(w_third, *second.got), 'fsdp', axis=0)]
    pallas_call x0 -> x17, Pallas kernels: none -> 156 us  [the longest x12 115 us: call(): pl.pallas_call(wrapped, grid_spec=pltpu.PrefetchScalarGridSpec(num_scalar...]
    psum x1 -> x0, waiting for transfers between devices: 129 us -> none  [per_device(): lax.psum((sum_attn_gain, sum_mlp_gain, sum_head_gain, full_cq, full_ck, f...]
    all_gather x13 -> x0, blocking collectives: 126 us -> none  [the longest x9 68 us: prefix(): everything = jax.tree.map(lambda part: lax.all_gather(part, axis), x)]
    squeeze x144 -> x1, local copies, waits for them, and re-layouts: 120 us -> 1 us  [per_device(): ff_shard = [ff_shard[0].T, ff_shard[1].T, ff_shard[2]]]
  transfers between devices with their start and end apart: 53 -> 71, of which waited for: 29 -> 17; matrix products, arithmetic and copies ran while one was open for 28% -> 31% of each run, Pallas kernels for 0% -> 31%
where the time goes in v1:
time: 514 us; the launch traced here: 506 us
  Pallas kernels  156 us (30%)
  starting transfers between devices  82 us (16%)
  waiting for transfers between devices  70.8 us (14%)
  matrix products  66.7 us (13%)
  local copies, waits for them, and re-layouts  57.4 us (11%)
  other arithmetic  56.3 us (11%)
  between operations  16.7 us (3%)
    pallas_call x12, Pallas kernels, call(): pl.pallas_call(wrapped, grid_spec=pltpu.PrefetchScalarGridSpec(num_scalar...  115 us
    ppermute x44, waiting for transfers between devices, swapped(): lax.ppermute(block, axis, [(i, i ^ bit) for i in range(lax.axis_size(axis...  54.4 us
    ppermute x44, starting transfers between devices, swapped(): lax.ppermute(block, axis, [(i, i ^ bit) for i in range(lax.axis_size(axis...  34 us
    pallas_call x3, Pallas kernels, run_local(): pl.pallas_call(local_kernel(heads, with_trans), grid_spec=pltpu.PrefetchS...  32.4 us
    dot_general x9, matrix products, mat_t(): lax.dot_general(left, right, (((2,), (1,)), ((), ())), preferred_element_...  25.1 us
    unnamed x255, local copies, waits for them, and re-layouts  22.1 us
    dot_general x6, matrix products, grad_of(): lax.dot_general(left, right, (((0,), (0,)), ((), ())), preferred_element_...  21.1 us
    dot_general x6, matrix products, mat(): lax.dot_general(left, right, (((2,), (0,)), ((), ())), preferred_element_...  20.6 us
  transfers between devices with their start and end apart: 71, of which 17 were waited for; matrix products, arithmetic and copies ran while one was open for 31% of the time, Pallas kernels for 31%

profile of v1, /device:TPU:0, one launch (start us, length us, event | category | flops | bytes accessed | tf_op | source)
XLA Modules:
  0.0 505.5 jit_solution(1916054624421636989)
XLA Ops:
  10.9 3.0 collective-permute-start
  13.9 2.6 collective-permute-start.1
  19.4 3.4 collective-permute-start.6
  36.1 7.9 %collective-permute-start.10 = (bf16[128,1024]{1,0:T(8,128)(2,1)S(1)}, bf16[128,1024]{1,0:T(8,128)(2,1)S(1)}, u32[]{:S(2)}, u32[]{:S(2)}) collective-permute-start(bf16[128,1024]{1,0:T(8,128)(2,1)S(1)} %constant_dynamic-slice_fusion.14), channel_id=1, source_target_pairs={{0,3},{1,0},{2,1},{3,2},{4,7},{5,4},{6,5},{7,6},{8,11},{9,8},{10,9... | collective-permute-start | bytes 786440 | tf_op jit(solution)/shard_map/ppermute | solution.py:978
  48.7 6.0 %collective-permute-done.4.refs_4_ = bf16[128,1152]{1,0:T(8,128)(2,1)S(1)} collective-permute-done((bf16[128,1152]{1,0:T(8,128)(2,1)}, bf16[128,1152]{1,0:T(8,128)(2,1)S(1)}, u32[]{:S(2)}, u32[]{:S(2)}) %collective-permute-start.4) | collective-permute-done | bytes 294944 | tf_op jit(solution)/shard_map/ppermute | solution.py:889
  54.7 4.5 collective-permute-done.5.refs_5_
  60.0 4.0 place_weights.2
  64.0 3.5 collective-permute-done.9.refs_1_
  72.2 5.3 %convolution_bitcast_fusion.2.q_ref.k_ref.v_ref.logits_ref.refs_0_.refs_1_.refs_2_ = f32[1,528,1152]{2,1,0:T(8,128)} fusion(bf16[1024,1152]{1,0:T(8,128)(2,1)} %bitcast.251, bf16[3,528,1024]{2,1,0:T(8,128)(2,1)} %fusion.2), kind=kOutput, calls=%fused_computation.9 | convolution fusion | flops 1245708288 | bytes 5873664 | tf_op jit(solution)/shard_map/dot_general | solution.py:1118
  77.5 10.9 %mixer_local.3 = (bf16[1,2,512,128]{3,2,1,0:T(8,128)(2,1)}, f32[1,512,512]{2,1,0:T(8,128)}, bf16[1,2,512,128]{3,2,1,0:T(8,128)(2,1)}, f32[1,2,512,256]{3,2,1,0:T...) custom-call(s32[1,9]{1,0:T(1,128)} %get-tuple-element.475.ends_ref, ...), custom_call_target="tpu_custom_call" | custom-call | bytes 33000000 | tf_op jit(solution)/shard_map/mixer_local/pallas_call | solution.py:707
  91.9 2.6 collective-permute-start.7
  94.6 4.3 convolution_bitcast_fusion.1.q_ref.k_ref.v_ref.logits_ref.refs_0_.refs_1_.refs_2_
  98.9 10.7 %mixer_local.4 = (bf16[1,2,512,128]{3,2,1,0:T(8,128)(2,1)}, f32[1,512,512]{2,1,0:T(8,128)}, bf16[1,2,512,128]{3,2,1,0:T(8,128)(2,1)}, f32[1,2,512,256]{3,2,1,0:T...) custom-call(s32[1,9]{1,0:T(1,128)} %get-tuple-element.473.ends_ref, ...), custom_call_target="tpu_custom_call" | custom-call | bytes 33000000 | tf_op jit(solution)/shard_map/mixer_local/pallas_call | solution.py:707
  110.5 3.7 place_weights.3
  114.2 3.3 convolution_bitcast_fusion.5.refs_7_.refs_4_
  118.1 6.7 %mixer_output.3 = (bf16[3,512,512]{2,1,0:T(8,128)(2,1)}, f32[1,512,512]{2,1,0:T(8,128)}, bf16[1,2,512,256]{3,2,1,0:T(8,128)(2,1)}, bf16[1,256,1024]{2,1,0:T(8,128)(2,1)}, bf16[1,256,1024]{2,1,0:T(8,128)(2,1)}) custom-call(s32[4]{0:T(128)} %fusion.80.refs_0_, bf16[1,2,128,256]{3,2,1,0:T(8,128)(2,1)} %copy-done.93, ...), custom_call_target="tpu_custom_call" | custom-call | bytes 19800000 | tf_op jit(solution)/shard_map/mixer_output/pallas_call | solution.py:639
  126.2 4.0 collective-permute-start.17
  130.2 3.0 convolution_bitcast_fusion.q_ref.k_ref.v_ref.logits_ref.refs_0_.refs_1_.refs_2_
  136.7 10.8 %mixer_local.5 = (bf16[1,2,512,128]{3,2,1,0:T(8,128)(2,1)}, f32[1,512,512]{2,1,0:T(8,128)}, bf16[1,2,512,128]{3,2,1,0:T(8,128)(2,1)}, f32[1,2,512,256]{3,2,1,0:T...) custom-call(s32[1,9]{1,0:T(1,128)} %get-tuple-element.474.ends_ref, ...), custom_call_target="tpu_custom_call" | custom-call | bytes 33000000 | tf_op jit(solution)/shard_map/mixer_local/pallas_call | solution.py:707
  148.6 6.8 %mixer_output.4 = (bf16[3,512,512]{2,1,0:T(8,128)(2,1)}, f32[1,512,512]{2,1,0:T(8,128)}, bf16[1,2,512,256]{3,2,1,0:T(8,128)(2,1)}, bf16[1,256,1024]{2,1,0:T(8,128)(2,1)}, bf16[1,256,1024]{2,1,0:T(8,128)(2,1)}) custom-call(s32[4]{0:T(128)} %fusion.80.refs_0_, bf16[1,2,128,256]{3,2,1,0:T(8,128)(2,1)} %copy-done.90, ...), custom_call_target="tpu_custom_call", output_to_operand_aliasing={{0}: (10, {})} | custom-call | bytes 19800000 | tf_op jit(solution)/shard_map/mixer_output/pallas_call | solution.py:639
  157.0 3.0 convolution_bitcast_fusion.3.refs_7_.refs_4_
  160.0 4.2 collective-permute-done.16
  167.3 3.3 collective-permute-done.18.refs_1_
  171.3 6.8 %mixer_output.5 = (bf16[3,512,512]{2,1,0:T(8,128)(2,1)}, f32[1,512,512]{2,1,0:T(8,128)}, bf16[1,2,512,256]{3,2,1,0:T(8,128)(2,1)}, bf16[1,256,1024]{2,1,0:T(8,128)(2,1)}, bf16[1,256,1024]{2,1,0:T(8,128)(2,1)}) custom-call(s32[4]{0:T(128)} %fusion.80.refs_0_, bf16[1,2,128,256]{3,2,1,0:T(8,128)(2,1)} %copy-done.92, ...), custom_call_target="tpu_custom_call", output_to_operand_aliasing={{0}: (10, {})} | custom-call | bytes 19800000 | tf_op jit(solution)/shard_map/mixer_output/pallas_call | solution.py:639
  182.3 10.1 %feed_forward.3 = (bf16[1,256,2048]{2,1,0:T(8,128)(2,1)}, bf16[1,256,2048]{2,1,0:T(8,128)(2,1)}, bf16[3,512,1024]{2,1,0:T(8,128)(2,1)}, bf16[3,512,704]{2,1,0:T(...) custom-call(bf16[1,256,1024]{2,1,0:T(8,128)(2,1)} %copy-done.62, ...), custom_call_target="tpu_custom_call" | custom-call | bytes 29700000 | tf_op jit(solution)/shard_map/feed_forward/pallas_call | solution.py:639
  194.9 6.2 %collective-permute-done.26 = bf16[1,128,1024]{2,1,0:T(8,128)(2,1)S(1)} collective-permute-done((bf16[1,128,1024]{2,1,0:T(8,128)(2,1)S(1)}, bf16[1,128,1024]{2,1,0:T(8,128)(2,1)S(1)}, u32[]{:S(2)}, u32[]{:S(2)}) %collective-permute-start.26) | collective-permute-done | bytes 262176 | tf_op jit(solution)/shard_map/ppermute | solution.py:889
  206.6 10.0 %feed_forward.4 = (bf16[1,256,2048]{2,1,0:T(8,128)(2,1)}, bf16[1,256,2048]{2,1,0:T(8,128)(2,1)}, bf16[3,512,1024]{2,1,0:T(8,128)(2,1)}, bf16[3,512,704]{2,1,0:T(...) custom-call(bf16[1,256,1024]{2,1,0:T(8,128)(2,1)} %copy-done.63, ...), custom_call_target="tpu_custom_call", output_to_operand_aliasing={{2}: (4, {}), {3}: (5, {}), {4}: (6, {}), {5}: (7, {})} | custom-call | bytes 29700000 | tf_op jit(solution)/shard_map/feed_forward/pallas_call | solution.py:639
  216.6 7.0 %collective-permute-done.29 = bf16[1,128,1024]{2,1,0:T(8,128)(2,1)S(1)} collective-permute-done((bf16[1,128,1024]{2,1,0:T(8,128)(2,1)S(1)}, bf16[1,128,1024]{2,1,0:T(8,128)(2,1)S(1)}, u32[]{:S(2)}, u32[]{:S(2)}) %collective-permute-start.29) | collective-permute-done | bytes 262176 | tf_op jit(solution)/shard_map/ppermute | solution.py:889
  228.9 6.1 %collective-permute-done.32 = bf16[1,128,1024]{2,1,0:T(8,128)(2,1)} collective-permute-done((bf16[1,128,1024]{2,1,0:T(8,128)(2,1)S(1)}, bf16[1,128,1024]{2,1,0:T(8,128)(2,1)}, u32[]{:S(2)}, u32[]{:S(2)}) %collective-permute-start.32) | collective-permute-done | bytes 262176 | tf_op jit(solution)/shard_map/ppermute | solution.py:889
  239.9 10.1 %feed_forward.5 = (bf16[1,256,2048]{2,1,0:T(8,128)(2,1)}, bf16[1,256,2048]{2,1,0:T(8,128)(2,1)}, bf16[3,512,1024]{2,1,0:T(8,128)(2,1)}, bf16[3,512,704]{2,1,0:T(...) custom-call(bf16[1,256,1024]{2,1,0:T(8,128)(2,1)} %pad_maximum_fusio, ...), custom_call_target="tpu_custom_call", output_to_operand_aliasing={{2}: (4, {}), {3}: (5, {}), {4}: (6, {}), {5}: (7, {})} | custom-call | bytes 29700000 | tf_op jit(solution)/shard_map/feed_forward/pallas_call | solution.py:639
  250.3 4.1 fusion.14
  267.0 7.1 %mixer_gate_back.3 = (bf16[1,512,512]{2,1,0:T(8,128)(2,1)}, f32[1,2,512,256]{3,2,1,0:T(8,128)}, bf16[3,528,512]{2,1,0:T(8,128)(2,1)}, bf16[3,512,1024]{2,1,0:T(8...) custom-call(s32[4]{0:T(128)} %fusion.80.refs_0_, bf16[1,256,1024]{2,1,0:T(8,128)(2,1)} %pad_maximum_fusion.9.refs_1_, ...), custom_call_target="tpu_custom_call" | custom-call | bytes 19800000 | tf_op jit(solution)/shard_map/mixer_gate_back/pallas_call | solution.py:639
  291.0 6.3 %collective-permute-done.36.refs_12_ = bf16[1,2,128,256]{3,2,1,0:T(8,128)(2,1)S(1)} collective-permute-done((bf16[1,2,128,256]{3,2,1,0:T(8,128)(2,1)}, bf16[1,2,128,256]{3,2,1,0:T(8,128)(2,1)S(1)}, u32[]{:S(2)}, u32[]{:S(2)}) %collective-permute-start.36) | collective-permute-done | bytes 131104 | tf_op jit(solution)/shard_map/ppermute | solution.py:885
  297.3 6.7 %mixer_gate_back.4 = (bf16[1,512,512]{2,1,0:T(8,128)(2,1)}, f32[1,2,512,256]{3,2,1,0:T(8,128)}, bf16[3,528,512]{2,1,0:T(8,128)(2,1)}, bf16[3,512,1024]{2,1,0:T(8...) custom-call(s32[4]{0:T(128)} %fusion.80.refs_0_, ...), custom_call_target="tpu_custom_call", output_to_operand_aliasing={{2}: (10, {}), {3}: (11, {})} | custom-call | bytes 19800000 | tf_op jit(solution)/shard_map/mixer_gate_back/pallas_call | solution.py:639
  305.9 14.6 %mixer_back.3 = (bf16[3,528,1152]{2,1,0:T(8,128)(2,1)}, bf16[1,528,1152]{2,1,0:T(8,128)(2,1)}, f32[1,8,1152]{2,1,0:T(8,128)}) custom-call(f32[1,528,1152]{2,1,0:T(8,128)} %convolution_bitcast_fusion.2.q_ref.k_ref.v_ref.logits_ref.refs_0_.refs_1_.refs_2_, f32[1,528,1152]{2,1,0:T(8,128)} %convolution_bitcast_fusion.2.q_ref.k_ref.v_ref.logits_ref.refs_0_.refs_1_.refs_2_, ...), custom_call_target="tpu_custom_call" | custom-call | bytes 46200000 | tf_op jit(solution)/shard_map/mixer_back/pallas_call | solution.py:639
  322.5 7.0 %mixer_gate_back.5 = (bf16[1,512,512]{2,1,0:T(8,128)(2,1)}, f32[1,2,512,256]{3,2,1,0:T(8,128)}, bf16[3,528,512]{2,1,0:T(8,128)(2,1)}, bf16[3,512,1024]{2,1,0:T(8...) custom-call(s32[4]{0:T(128)} %fusion.80.refs_0_, ...), custom_call_target="tpu_custom_call", output_to_operand_aliasing={{2}: (10, {}), {3}: (11, {})} | custom-call | bytes 19800000 | tf_op jit(solution)/shard_map/mixer_gate_back/pallas_call | solution.py:639
  329.6 3.2 fusion.62
  344.3 2.6 collective-permute-start.45
  347.7 14.8 %mixer_back.4 = (bf16[3,528,1152]{2,1,0:T(8,128)(2,1)}, bf16[1,528,1152]{2,1,0:T(8,128)(2,1)}, f32[1,8,1152]{2,1,0:T(8,128)}) custom-call(f32[1,528,1152]{2,1,0:T(8,128)} %convolution_bitcast_fusion.1.q_ref.k_ref.v_ref.logits_ref.refs_0_.refs_1_.refs_2_, ...), custom_call_target="tpu_custom_call", output_to_operand_aliasing={{0}: (14, {})} | custom-call | bytes 46200000 | tf_op jit(solution)/shard_map/mixer_back/pallas_call | solution.py:639
  365.7 4.2 fusion.95
  371.6 10.5 %collective-permute-done.45 = bf16[512,1024]{0,1:T(8,128)(2,1)} collective-permute-done((bf16[512,1024]{0,1:T(8,128)(2,1)}, bf16[512,1024]{0,1:T(8,128)(2,1)}, u32[]{:S(2)}, u32[]{:S(2)}) %collective-permute-start.45) | collective-permute-done | bytes 1048608 | tf_op jit(solution)/shard_map/ppermute | solution.py:889
  384.9 14.9 %mixer_back.5 = (bf16[3,528,1152]{2,1,0:T(8,128)(2,1)}, bf16[1,528,1152]{2,1,0:T(8,128)(2,1)}, f32[1,8,1152]{2,1,0:T(8,128)}) custom-call(f32[1,528,1152]{2,1,0:T(8,128)} %convolution_bitcast_fusion.q_ref.k_ref.v_ref.logits_ref.refs_0_.refs_1_.refs_2_, ...), custom_call_target="tpu_custom_call", output_to_operand_aliasing={{0}: (14, {})} | custom-call | bytes 46200000 | tf_op jit(solution)/shard_map/mixer_back/pallas_call | solution.py:639
  399.8 8.0 %bitcast_convert_fusion = bf16[1024,1152]{1,0:T(8,128)(2,1)S(1)} fusion(bf16[3,528,1024]{2,1,0:T(8,128)(2,1)} %fusion.2, bf16[3,528,1152]{2,1,0:T(8,128)(2,1)} %get-tuple-element.314), kind=kOutput, calls=%fused_computation.5 | convolution fusion | flops 3738304512 | bytes 9252864 | tf_op jit(solution)/shard_map/dot_general | solution.py:1128
  408.9 3.1 collective-permute-start.53
  425.3 4.9 fusion.8
  430.4 3.4 fusion.5
  483.2 5.5 %collective-permute-done.65 = f32[152,128]{1,0:T(8,128)S(1)} collective-permute-done((f32[152,128]{1,0:T(8,128)S(1)}, f32[152,128]{1,0:T(8,128)S(1)}, u32[]{:S(2)}, u32[]{:S(2)}) %collective-permute-start.65) | collective-permute-done | bytes 77856 | tf_op jit(solution)/shard_map/ppermute | solution.py:889
  491.2 3.4 collective-permute-done.68
  (538 shorter events, 190.7 us)
Async XLA Ops:
  7.2 175.1 %all-gather.3.cloned.1.call-start = ((), (), s32[]{:S(2)}) async-start(), calls=%async_computation.2 | async-start | bytes 5406720 | tf_op jit(solution)/shard_map/all_gather | solution.py:1188
  10.9 22.6 %collective-permute-start = (bf16[128,1152]{1,0:T(8,128)(2,1)}, bf16[128,1152]{1,0:T(8,128)(2,1)}, u32[]{:S(2)}, u32[]{:S(2)}) collective-permute-start(bf16[128,1152]{1,0:T(8,128)(2,1)} %constant_dynamic-slice_fusion.18), channel_id=1, source_target_pairs={{0,1},{1,2},{2,3},{3,0},{4,5},{5,6},{6,7},{7,4},{8,9},{9,10},{10,1... | collective-permute-start | bytes 884744 | tf_op jit(solution)/shard_map/ppermute | solution.py:978
  13.9 22.1 %collective-permute-start.1 = (bf16[128,1152]{1,0:T(8,128)(2,1)}, bf16[128,1152]{1,0:T(8,128)(2,1)}, u32[]{:S(2)}, u32[]{:S(2)}) collective-permute-start(bf16[128,1152]{1,0:T(8,128)(2,1)} %constant_dynamic-slice_fusion.18), channel_id=1, source_target_pairs={{0,2},{1,3},{2,0},{3,1},{4,6},{5,7},{6,4},{7,5},{8,10},{9,11},{10,... | collective-permute-start | bytes 884744 | tf_op jit(solution)/shard_map/ppermute | solution.py:978
  16.5 19.5 %collective-permute-start.2 = (bf16[128,1152]{1,0:T(8,128)(2,1)}, bf16[128,1152]{1,0:T(8,128)(2,1)}, u32[]{:S(2)}, u32[]{:S(2)}) collective-permute-start(bf16[128,1152]{1,0:T(8,128)(2,1)} %constant_dynamic-slice_fusion.18), channel_id=1, source_target_pairs={{0,3},{1,0},{2,1},{3,2},{4,7},{5,4},{6,5},{7,6},{8,11},{9,8},{10,9... | collective-permute-start | bytes 884744 | tf_op jit(solution)/shard_map/ppermute | solution.py:978
  19.4 13.4 %collective-permute-start.6 = (bf16[3,16,1024]{2,1,0:T(8,128)(2,1)}, bf16[3,16,1024]{2,1,0:T(8,128)(2,1)S(1)}, u32[]{:S(2)}, u32[]{:S(2)}) collective-permute-start(bf16[3,16,1024]{2,1,0:T(8,128)(2,1)} %slice.359), channel_id=1, source_target_pairs={{0,16},{1,17},{2,18},{3,19},{4,20},{5,21},{6,22},{7,23},{8,24},{9,... | collective-permute-start | bytes 294920 | tf_op jit(solution)/shard_map/ppermute | solution.py:885
  33.5 12.6 %collective-permute-start.3 = (bf16[128,1152]{1,0:T(8,128)(2,1)}, bf16[128,1152]{1,0:T(8,128)(2,1)S(1)}, u32[]{:S(2)}, u32[]{:S(2)}) collective-permute-start(bf16[128,1152]{1,0:T(8,128)(2,1)} %collective-permute-done.refs_0_), channel_id=1, source_target_pairs={{0,16},{16,0},{1,17},{17,1},{2,18},{18,2},{3,19},{19,3},{4,20},{20... | collective-permute-start | bytes 884744 | tf_op jit(solution)/shard_map/ppermute | solution.py:889
  36.1 27.9 %collective-permute-start.10 = (bf16[128,1024]{1,0:T(8,128)(2,1)S(1)}, bf16[128,1024]{1,0:T(8,128)(2,1)S(1)}, u32[]{:S(2)}, u32[]{:S(2)}) collective-permute-start(bf16[128,1024]{1,0:T(8,128)(2,1)S(1)} %constant_dynamic-slice_fusion.14), channel_id=1, source_target_pairs={{0,3},{1,0},{2,1},{3,2},{4,7},{5,4},{6,5},{7,6},{8,11},{9,8},{10,9... | collective-permute-start | bytes 786440 | tf_op jit(solution)/shard_map/ppermute | solution.py:978
  43.9 23.6 %collective-permute-start.9 = (bf16[128,1024]{1,0:T(8,128)(2,1)S(1)}, bf16[128,1024]{1,0:T(8,128)(2,1)}, u32[]{:S(2)}, u32[]{:S(2)}) collective-permute-start(bf16[128,1024]{1,0:T(8,128)(2,1)S(1)} %constant_dynamic-slice_fusion.14), channel_id=1, source_target_pairs={{0,2},{1,3},{2,0},{3,1},{4,6},{5,7},{6,4},{7,5},{8,10},{9,11},{10,... | collective-permute-start | bytes 786440 | tf_op jit(solution)/shard_map/ppermute | solution.py:978
  44.4 23.2 %collective-permute-start.8 = (bf16[128,1024]{1,0:T(8,128)(2,1)S(1)}, bf16[128,1024]{1,0:T(8,128)(2,1)}, u32[]{:S(2)}, u32[]{:S(2)}) collective-permute-start(bf16[128,1024]{1,0:T(8,128)(2,1)S(1)} %constant_dynamic-slice_fusion.14), channel_id=1, source_target_pairs={{0,1},{1,2},{2,3},{3,0},{4,5},{5,6},{6,7},{7,4},{8,9},{9,10},{10,1... | collective-permute-start | bytes 786440 | tf_op jit(solution)/shard_map/ppermute | solution.py:978
  46.1 13.2 %collective-permute-start.5 = (bf16[128,1152]{1,0:T(8,128)(2,1)}, bf16[128,1152]{1,0:T(8,128)(2,1)S(1)}, u32[]{:S(2)}, u32[]{:S(2)}) collective-permute-start(bf16[128,1152]{1,0:T(8,128)(2,1)} %collective-permute-done.2.refs_2_), channel_id=1, source_target_pairs={{0,16},{16,0},{1,17},{17,1},{2,18},{18,2},{3,19},{19,3},{4,20},{20... | collective-permute-start | bytes 884744 | tf_op jit(solution)/shard_map/ppermute | solution.py:889
  67.6 392.1 %reduce-scatter.2.cloned.1.call-start = ((), (), s32[]{:S(2)}) async-start(), calls=%async_computation.1 | async-start | bytes 4866048 | tf_op jit(solution)/shard_map/reduce_scatter | solution.py:1133
  88.4 21.2 %collective-permute-start.13 = (bf16[128,1024]{1,0:T(8,128)(2,1)S(1)}, bf16[128,1024]{1,0:T(8,128)(2,1)S(1)}, u32[]{:S(2)}, u32[]{:S(2)}) collective-permute-start(bf16[128,1024]{1,0:T(8,128)(2,1)S(1)} %collective-permute-done.10.refs_2_), channel_id=1, source_target_pairs={{0,16},{16,0},{1,17},{17,1},{2,18},{18,2},{3,19},{19,3},{4,20},{20... | collective-permute-start | bytes 786440 | tf_op jit(solution)/shard_map/ppermute | solution.py:889
  89.9 19.7 %collective-permute-start.12 = (bf16[128,1024]{1,0:T(8,128)(2,1)}, bf16[128,1024]{1,0:T(8,128)(2,1)S(1)}, u32[]{:S(2)}, u32[]{:S(2)}) collective-permute-start(bf16[128,1024]{1,0:T(8,128)(2,1)} %collective-permute-done.9.refs_1_), channel_id=1, source_target_pairs={{0,16},{16,0},{1,17},{17,1},{2,18},{18,2},{3,19},{19,3},{4,20},{20... | collective-permute-start | bytes 786440 | tf_op jit(solution)/shard_map/ppermute | solution.py:889
  90.5 19.2 %collective-permute-start.11 = (bf16[128,1024]{1,0:T(8,128)(2,1)}, bf16[128,1024]{1,0:T(8,128)(2,1)S(1)}, u32[]{:S(2)}, u32[]{:S(2)}) collective-permute-start(bf16[128,1024]{1,0:T(8,128)(2,1)} %collective-permute-done.8.refs_0_), channel_id=1, source_target_pairs={{0,16},{16,0},{1,17},{17,1},{2,18},{18,2},{3,19},{19,3},{4,20},{20... | collective-permute-start | bytes 786440 | tf_op jit(solution)/shard_map/ppermute | solution.py:889
  91.9 17.6 %collective-permute-start.7 = (bf16[1,2,128,256]{3,2,1,0:T(8,128)(2,1)}, bf16[1,2,128,256]{3,2,1,0:T(8,128)(2,1)S(1)}, u32[]{:S(2)}, u32[]{:S(2)}) collective-permute-start(bf16[1,2,128,256]{3,2,1,0:T(8,128)(2,1)} %get-tuple-element.182), channel_id=1, source_target_pairs={{0,16},{1,17},{2,18},{3,19},{4,20},{5,21},{6,22},{7,23},{8,24},{9,... | collective-permute-start | bytes 393224 | tf_op jit(solution)/shard_map/ppermute | solution.py:885
  126.2 21.8 %collective-permute-start.17 = (bf16[1,2,128,256]{3,2,1,0:T(8,128)(2,1)S(1)}, bf16[1,2,128,256]{3,2,1,0:T(8,128)(2,1)S(1)}, u32[]{:S(2)}, u32[]{:S(2)}) collective-permute-start(bf16[1,2,128,256]{3,2,1,0:T(8,128)(2,1)S(1)} %copy-done.113), channel_id=1, source_target_pairs={{0,16},{1,17},{2,18},{3,19},{4,20},{5,21},{6,22},{7,23},{8,24},{9,... | collective-permute-start | bytes 393224 | tf_op jit(solution)/shard_map/ppermute | solution.py:885
  133.4 14.2 %collective-permute-start.15 = (bf16[1,128,1024]{2,1,0:T(8,128)(2,1)S(1)}, bf16[1,128,1024]{2,1,0:T(8,128)(2,1)S(1)}, u32[]{:S(2)}, u32[]{:S(2)}) collective-permute-start(bf16[1,128,1024]{2,1,0:T(8,128)(2,1)S(1)} %slice.592), channel_id=1, source_target_pairs={{0,8},{4,12},{8,0},{12,4},{1,9},{5,13},{9,1},{13,5},{2,10},{6,14},... | collective-permute-start | bytes 786440 | tf_op jit(solution)/shard_map/ppermute | solution.py:889
  164.3 14.0 %collective-permute-start.21 = (bf16[1,256,1024]{2,1,0:T(8,128)(2,1)S(1)}, bf16[1,256,1024]{2,1,0:T(8,128)(2,1)S(1)}, u32[]{:S(2)}, u32[]{:S(2)}) collective-permute-start(bf16[1,256,1024]{2,1,0:T(8,128)(2,1)S(1)} %pad_maximum_fusion.6.refs_0_), channel_id=1, source_target_pairs={{0,4},{4,0},{8,12},{12,8},{1,5},{5,1},{9,13},{13,9},{2,6},{6,2},{1... | collective-permute-start | bytes 1572872 | tf_op jit(solution)/shard_map/ppermute | solution.py:889
  164.6 13.7 %collective-permute-start.22 = (bf16[1,128,1024]{2,1,0:T(8,128)(2,1)S(1)}, bf16[1,128,1024]{2,1,0:T(8,128)(2,1)S(1)}, u32[]{:S(2)}, u32[]{:S(2)}) collective-permute-start(bf16[1,128,1024]{2,1,0:T(8,128)(2,1)S(1)} %slice.591), channel_id=1, source_target_pairs={{0,8},{4,12},{8,0},{12,4},{1,9},{5,13},{9,1},{13,5},{2,10},{6,14},... | collective-permute-start | bytes 786440 | tf_op jit(solution)/shard_map/ppermute | solution.py:889
  179.5 14.4 %collective-permute-start.24 = (bf16[1,128,1024]{2,1,0:T(8,128)(2,1)S(1)}, bf16[1,128,1024]{2,1,0:T(8,128)(2,1)}, u32[]{:S(2)}, u32[]{:S(2)}) collective-permute-start(bf16[1,128,1024]{2,1,0:T(8,128)(2,1)S(1)} %multiply_convert_fusion.1), channel_id=1, source_target_pairs={{0,8},{4,12},{8,0},{12,4},{1,9},{5,13},{9,1},{13,5},{2,10},{6,14},... | collective-permute-start | bytes 786440 | tf_op jit(solution)/shard_map/ppermute | solution.py:889
  192.4 11.7 %collective-permute-start.23 = (bf16[1,256,2048]{2,1,0:T(8,128)(2,1)}, bf16[1,256,2048]{2,1,0:T(8,128)(2,1)S(1)}, u32[]{:S(2)}, u32[]{:S(2)}) collective-permute-start(bf16[1,256,2048]{2,1,0:T(8,128)(2,1)} %get-tuple-element.232), channel_id=1, source_target_pairs={{0,4},{4,0},{8,12},{12,8},{1,5},{5,1},{9,13},{13,9},{2,6},{6,2},{1... | collective-permute-start | bytes 3145736 | tf_op jit(solution)/shard_map/ppermute | solution.py:889
  204.5 20.4 %collective-permute-start.27 = (bf16[1,128,2048]{2,1,0:T(8,128)(2,1)S(1)}, bf16[1,128,2048]{2,1,0:T(8,128)(2,1)S(1)}, u32[]{:S(2)}, u32[]{:S(2)}) collective-permute-start(bf16[1,128,2048]{2,1,0:T(8,128)(2,1)S(1)} %slice.586), channel_id=1, source_target_pairs={{0,8},{4,12},{8,0},{12,4},{1,9},{5,13},{9,1},{13,5},{2,10},{6,14},... | collective-permute-start | bytes 1572872 | tf_op jit(solution)/shard_map/ppermute | solution.py:889
  205.8 17.8 %collective-permute-start.29 = (bf16[1,128,1024]{2,1,0:T(8,128)(2,1)S(1)}, bf16[1,128,1024]{2,1,0:T(8,128)(2,1)S(1)}, u32[]{:S(2)}, u32[]{:S(2)}) collective-permute-start(bf16[1,128,1024]{2,1,0:T(8,128)(2,1)S(1)} %multiply_convert_fusion), channel_id=1, source_target_pairs={{0,8},{4,12},{8,0},{12,4},{1,9},{5,13},{9,1},{13,5},{2,10},{6,14},... | collective-permute-start | bytes 786440 | tf_op jit(solution)/shard_map/ppermute | solution.py:889
  224.4 12.3 %collective-permute-start.28 = (bf16[1,256,2048]{2,1,0:T(8,128)(2,1)}, bf16[1,256,2048]{2,1,0:T(8,128)(2,1)}, u32[]{:S(2)}, u32[]{:S(2)}) collective-permute-start(bf16[1,256,2048]{2,1,0:T(8,128)(2,1)} %get-tuple-element.244), channel_id=1, source_target_pairs={{0,4},{4,0},{8,12},{12,8},{1,5},{5,1},{9,13},{13,9},{2,6},{6,2},{1... | collective-permute-start | bytes 3145736 | tf_op jit(solution)/shard_map/ppermute | solution.py:889
  236.7 30.3 %collective-permute-start.35 = (bf16[1,256,1024]{2,1,0:T(8,128)(2,1)}, bf16[1,256,1024]{2,1,0:T(8,128)(2,1)}, u32[]{:S(2)}, u32[]{:S(2)}) collective-permute-start(bf16[1,256,1024]{2,1,0:T(8,128)(2,1)} %pad_maximum_fusion.9.refs_1_), channel_id=1, source_target_pairs={{0,4},{4,0},{8,12},{12,8},{1,5},{5,1},{9,13},{13,9},{2,6},{6,2},{1... | collective-permute-start | bytes 1572872 | tf_op jit(solution)/shard_map/ppermute | solution.py:889
  238.7 15.6 %collective-permute-start.31 = (bf16[1,128,2048]{2,1,0:T(8,128)(2,1)S(1)}, bf16[1,128,2048]{2,1,0:T(8,128)(2,1)S(1)}, u32[]{:S(2)}, u32[]{:S(2)}) collective-permute-start(bf16[1,128,2048]{2,1,0:T(8,128)(2,1)S(1)} %slice.585), channel_id=1, source_target_pairs={{0,8},{4,12},{8,0},{12,4},{1,9},{5,13},{9,1},{13,5},{2,10},{6,14},... | collective-permute-start | bytes 1572872 | tf_op jit(solution)/shard_map/ppermute | solution.py:889
  256.4 17.7 %collective-permute-start.37 = (bf16[1,128,1024]{2,1,0:T(8,128)(2,1)S(1)}, bf16[1,128,1024]{2,1,0:T(8,128)(2,1)}, u32[]{:S(2)}, u32[]{:S(2)}) collective-permute-start(bf16[1,128,1024]{2,1,0:T(8,128)(2,1)S(1)} %fusion.85), channel_id=1, source_target_pairs={{0,8},{4,12},{8,0},{12,4},{1,9},{5,13},{9,1},{13,5},{2,10},{6,14},... | collective-permute-start | bytes 786440 | tf_op jit(solution)/shard_map/ppermute | solution.py:889
  259.8 16.4 %collective-permute-start.34 = (bf16[1,128,2048]{2,1,0:T(8,128)(2,1)}, bf16[1,128,2048]{2,1,0:T(8,128)(2,1)}, u32[]{:S(2)}, u32[]{:S(2)}) collective-permute-start(bf16[1,128,2048]{2,1,0:T(8,128)(2,1)} %slice.584), channel_id=1, source_target_pairs={{0,8},{4,12},{8,0},{12,4},{1,9},{5,13},{9,1},{13,5},{2,10},{6,14},... | collective-permute-start | bytes 1572872 | tf_op jit(solution)/shard_map/ppermute | solution.py:889
  276.0 15.0 %collective-permute-start.39 = (bf16[1,256,1024]{2,1,0:T(8,128)(2,1)}, bf16[1,256,1024]{2,1,0:T(8,128)(2,1)}, u32[]{:S(2)}, u32[]{:S(2)}) collective-permute-start(bf16[1,256,1024]{2,1,0:T(8,128)(2,1)} %pad_maximum_fusion.10.refs_1_), channel_id=1, source_target_pairs={{0,4},{4,0},{8,12},{12,8},{1,5},{5,1},{9,13},{13,9},{2,6},{6,2},{1... | collective-permute-start | bytes 1572872 | tf_op jit(solution)/shard_map/ppermute | solution.py:889
  288.7 33.8 %collective-permute-start.41 = (bf16[1,256,1024]{2,1,0:T(8,128)(2,1)}, bf16[1,256,1024]{2,1,0:T(8,128)(2,1)}, u32[]{:S(2)}, u32[]{:S(2)}) collective-permute-start(bf16[1,256,1024]{2,1,0:T(8,128)(2,1)} %pad_maximum_fusion.11.refs_1_), channel_id=1, source_target_pairs={{0,4},{4,0},{8,12},{12,8},{1,5},{5,1},{9,13},{13,9},{2,6},{6,2},{1... | collective-permute-start | bytes 1572872 | tf_op jit(solution)/shard_map/ppermute | solution.py:889
  304.0 18.5 %collective-permute-start.40 = (bf16[1,2,128,256]{3,2,1,0:T(8,128)(2,1)}, bf16[1,2,128,256]{3,2,1,0:T(8,128)(2,1)S(1)}, u32[]{:S(2)}, u32[]{:S(2)}) collective-permute-start(bf16[1,2,128,256]{3,2,1,0:T(8,128)(2,1)} %get-tuple-element.285), channel_id=1, source_target_pairs={{16,0},{17,1},{18,2},{19,3},{20,4},{21,5},{22,6},{23,7},{24,8},{25... | collective-permute-start | bytes 393224 | tf_op jit(solution)/shard_map/ppermute | solution.py:885
  321.2 41.3 %collective-permute-start.42 = (bf16[1,16,1152]{2,1,0:T(8,128)(2,1)S(1)}, bf16[1,16,1152]{2,1,0:T(8,128)(2,1)S(1)}, u32[]{:S(2)}, u32[]{:S(2)}) collective-permute-start(bf16[1,16,1152]{2,1,0:T(8,128)(2,1)S(1)} %slice.316), channel_id=1, source_target_pairs={{16,0},{17,1},{18,2},{19,3},{20,4},{21,5},{22,6},{23,7},{24,8},{25... | collective-permute-start | bytes 110600 | tf_op jit(solution)/shard_map/ppermute | solution.py:885
  344.3 37.7 %collective-permute-start.45 = (bf16[512,1024]{0,1:T(8,128)(2,1)}, bf16[512,1024]{0,1:T(8,128)(2,1)}, u32[]{:S(2)}, u32[]{:S(2)}) collective-permute-start(bf16[512,1024]{0,1:T(8,128)(2,1)} %fusion.28), channel_id=1, source_target_pairs={{0,16},{16,0},{1,17},{17,1},{2,18},{18,2},{3,19},{19,3},{4,20},{20... | collective-permute-start | bytes 3145736 | tf_op jit(solution)/shard_map/ppermute | solution.py:889
  363.5 50.3 %collective-permute-start.47 = (bf16[1,16,1152]{2,1,0:T(8,128)(2,1)S(1)}, bf16[1,16,1152]{2,1,0:T(8,128)(2,1)S(1)}, u32[]{:S(2)}, u32[]{:S(2)}) collective-permute-start(bf16[1,16,1152]{2,1,0:T(8,128)(2,1)S(1)} %slice.324), channel_id=1, source_target_pairs={{16,0},{17,1},{18,2},{19,3},{20,4},{21,5},{22,6},{23,7},{24,8},{25... | collective-permute-start | bytes 110600 | tf_op jit(solution)/shard_map/ppermute | solution.py:885
  371.5 63.0 %collective-permute-start.44 = (bf16[1,256,1024]{2,1,0:T(8,128)(2,1)}, bf16[1,256,1024]{2,1,0:T(8,128)(2,1)}, u32[]{:S(2)}, u32[]{:S(2)}) collective-permute-start(bf16[1,256,1024]{2,1,0:T(8,128)(2,1)} %pad_maximum_fusion.12), channel_id=1, source_target_pairs={{0,4},{4,0},{8,12},{12,8},{1,5},{5,1},{9,13},{13,9},{2,6},{6,2},{1... | collective-permute-start | bytes 1572872 | tf_op jit(solution)/shard_map/ppermute | solution.py:889
  408.1 31.5 %collective-permute-start.51 = (bf16[128,1024]{0,1:T(8,128)(2,1)}, bf16[128,1024]{0,1:T(8,128)(2,1)}, u32[]{:S(2)}, u32[]{:S(2)}) collective-permute-start(bf16[128,1024]{0,1:T(8,128)(2,1)} %get-tuple-element.430), channel_id=1, source_target_pairs={{0,1},{1,2},{2,3},{3,0},{4,5},{5,6},{6,7},{7,4},{8,9},{9,10},{10,1... | collective-permute-start | bytes 786440 | tf_op jit(solution)/shard_map/ppermute | solution.py:1074
  408.2 31.4 %collective-permute-start.52 = (bf16[128,1024]{0,1:T(8,128)(2,1)}, bf16[128,1024]{0,1:T(8,128)(2,1)}, u32[]{:S(2)}, u32[]{:S(2)}) collective-permute-start(bf16[128,1024]{0,1:T(8,128)(2,1)} %get-tuple-element.429), channel_id=1, source_target_pairs={{0,2},{1,3},{2,0},{3,1},{4,6},{5,7},{6,4},{7,5},{8,10},{9,11},{10,... | collective-permute-start | bytes 786440 | tf_op jit(solution)/shard_map/ppermute | solution.py:1074
  408.9 31.2 %collective-permute-start.53 = (bf16[128,1024]{0,1:T(8,128)(2,1)}, bf16[128,1024]{0,1:T(8,128)(2,1)}, u32[]{:S(2)}, u32[]{:S(2)}) collective-permute-start(bf16[128,1024]{0,1:T(8,128)(2,1)} %get-tuple-element.428), channel_id=1, source_target_pairs={{0,3},{1,0},{2,1},{3,2},{4,7},{5,4},{6,5},{7,6},{8,11},{9,8},{10,9... | collective-permute-start | bytes 786440 | tf_op jit(solution)/shard_map/ppermute | solution.py:1074
  420.5 24.4 %collective-permute-start.50 = (bf16[512,512]{1,0:T(8,128)(2,1)}, bf16[512,512]{1,0:T(8,128)(2,1)}, u32[]{:S(2)}, u32[]{:S(2)}) collective-permute-start(bf16[512,512]{1,0:T(8,128)(2,1)} %constant_dynamic-slice_fusion.9), channel_id=1, source_target_pairs={{0,16},{16,0},{1,17},{17,1},{2,18},{18,2},{3,19},{19,3},{4,20},{20... | collective-permute-start | bytes 1572872 | tf_op jit(solution)/shard_map/ppermute | solution.py:889
  434.5 27.4 %collective-permute-start.57 = (bf16[512,640]{1,0:T(8,128)(2,1)}, bf16[512,640]{1,0:T(8,128)(2,1)}, u32[]{:S(2)}, u32[]{:S(2)}) collective-permute-start(bf16[512,640]{1,0:T(8,128)(2,1)} %constant_dynamic-slice_fusion.8), channel_id=1, source_target_pairs={{0,16},{16,0},{1,17},{17,1},{2,18},{18,2},{3,19},{19,3},{4,20},{20... | collective-permute-start | bytes 1966088 | tf_op jit(solution)/shard_map/ppermute | solution.py:889
  440.1 14.0 %collective-permute-start.48 = (bf16[1,128,1024]{2,1,0:T(8,128)(2,1)}, bf16[1,128,1024]{2,1,0:T(8,128)(2,1)S(1)}, u32[]{:S(2)}, u32[]{:S(2)}) collective-permute-start(bf16[1,128,1024]{2,1,0:T(8,128)(2,1)} %slice.589), channel_id=1, source_target_pairs={{0,8},{4,12},{8,0},{12,4},{1,9},{5,13},{9,1},{13,5},{2,10},{6,14},... | collective-permute-start | bytes 786440 | tf_op jit(solution)/shard_map/ppermute | solution.py:889
  444.9 10.6 %collective-permute-start.58 = (bf16[1,256,1024]{2,1,0:T(8,128)(2,1)}, bf16[1,256,1024]{2,1,0:T(8,128)(2,1)S(1)}, u32[]{:S(2)}, u32[]{:S(2)}) collective-permute-start(bf16[1,256,1024]{2,1,0:T(8,128)(2,1)} %pad_maximum_fusion.14), channel_id=1, source_target_pairs={{0,4},{4,0},{8,12},{12,8},{1,5},{5,1},{9,13},{13,9},{2,6},{6,2},{1... | collective-permute-start | bytes 1572872 | tf_op jit(solution)/shard_map/ppermute | solution.py:889
  447.2 32.1 %collective-permute-start.60 = (bf16[128,512]{1,0:T(8,128)(2,1)}, bf16[128,512]{1,0:T(8,128)(2,1)}, u32[]{:S(2)}, u32[]{:S(2)}) collective-permute-start(bf16[128,512]{1,0:T(8,128)(2,1)} %get-tuple-element.456), channel_id=1, source_target_pairs={{0,1},{1,2},{2,3},{3,0},{4,5},{5,6},{6,7},{7,4},{8,9},{9,10},{10,1... | collective-permute-start | bytes 393224 | tf_op jit(solution)/shard_map/ppermute | solution.py:1074
  449.3 31.3 %collective-permute-start.62 = (bf16[128,512]{1,0:T(8,128)(2,1)}, bf16[128,512]{1,0:T(8,128)(2,1)}, u32[]{:S(2)}, u32[]{:S(2)}) collective-permute-start(bf16[128,512]{1,0:T(8,128)(2,1)} %get-tuple-element.455), channel_id=1, source_target_pairs={{0,2},{1,3},{2,0},{3,1},{4,6},{5,7},{6,4},{7,5},{8,10},{9,11},{10,... | collective-permute-start | bytes 393224 | tf_op jit(solution)/shard_map/ppermute | solution.py:1074
  455.5 12.7 %collective-permute-start.54 = (bf16[1,128,1024]{2,1,0:T(8,128)(2,1)}, bf16[1,128,1024]{2,1,0:T(8,128)(2,1)}, u32[]{:S(2)}, u32[]{:S(2)}) collective-permute-start(bf16[1,128,1024]{2,1,0:T(8,128)(2,1)} %slice.588), channel_id=1, source_target_pairs={{0,8},{4,12},{8,0},{12,4},{1,9},{5,13},{9,1},{13,5},{2,10},{6,14},... | collective-permute-start | bytes 786440 | tf_op jit(solution)/shard_map/ppermute | solution.py:889
  464.7 16.7 %collective-permute-start.63 = (bf16[128,512]{1,0:T(8,128)(2,1)S(1)}, bf16[128,512]{1,0:T(8,128)(2,1)S(1)}, u32[]{:S(2)}, u32[]{:S(2)}) collective-permute-start(bf16[128,512]{1,0:T(8,128)(2,1)S(1)} %copy-done.95), channel_id=1, source_target_pairs={{0,3},{1,0},{2,1},{3,2},{4,7},{5,4},{6,5},{7,6},{8,11},{9,8},{10,9... | collective-permute-start | bytes 393224 | tf_op jit(solution)/shard_map/ppermute | solution.py:1074
  470.1 18.9 %collective-permute-start.64 = (bf16[128,640]{1,0:T(8,128)(2,1)S(1)}, bf16[128,640]{1,0:T(8,128)(2,1)S(1)}, u32[]{:S(2)}, u32[]{:S(2)}) collective-permute-start(bf16[128,640]{1,0:T(8,128)(2,1)S(1)} %get-tuple-element.439), channel_id=1, source_target_pairs={{0,1},{1,2},{2,3},{3,0},{4,5},{5,6},{6,7},{7,4},{8,9},{9,10},{10,1... | collective-permute-start | bytes 491528 | tf_op jit(solution)/shard_map/ppermute | solution.py:1074
  478.1 10.9 %collective-permute-start.66 = (bf16[128,640]{1,0:T(8,128)(2,1)S(1)}, bf16[128,640]{1,0:T(8,128)(2,1)S(1)}, u32[]{:S(2)}, u32[]{:S(2)}) collective-permute-start(bf16[128,640]{1,0:T(8,128)(2,1)S(1)} %get-tuple-element.438), channel_id=1, source_target_pairs={{0,2},{1,3},{2,0},{3,1},{4,6},{5,7},{6,4},{7,5},{8,10},{9,11},{10,... | collective-permute-start | bytes 491528 | tf_op jit(solution)/shard_map/ppermute | solution.py:1074
  (143 other events, 1030.2 us)
Sparse Core Ops, SparseCore 0:
  67.7 81.3 all-gather.2
  306.0 100.9 reduce-scatter.1

commit v2 on v1

--- a/solution.py
+++ b/solution.py
@@ -14,7 +14,6 @@
 PAD = 16
 LANES = 128
 FAR = -(1 << 20)
-VMEM_BYTES = 56 * 1024 * 1024
 
 F32 = jnp.float32
 BF16 = jnp.bfloat16
@@ -392,11 +391,21 @@
 
 
 def feed_forward_kernel(
-    low_ref, high_ref, cot_ref, w_ref, keep_ref, give_ref, h_ref, hid_ref, dg_ref, du_ref
+    low_ref,
+    high_ref,
+    cot_ref,
+    w_ref,
+    keep_ref,
+    give_ref,
+    out_keep_ref,
+    out_give_ref,
+    h_ref,
+    hid_ref,
+    dg_ref,
+    du_ref,
 ):
     shards, shard = w_ref.shape[0], w_ref.shape[3]
     half = low_ref.shape[0]
-    width = shards * shard
     h_ref[:half, :] = low_ref[...]
     h_ref[half:, :] = high_ref[...]
 
@@ -424,11 +433,10 @@
     for at in range(shards):
         out = dot(hidden, w_ref[at, 2]).astype(BF16)
         d_h = (dot(d_gate, w_ref[at, 0]) + dot(d_up, w_ref[at, 1])).astype(BF16)
-        shifted = slice(width + at * shard, width + (at + 1) * shard)
-        keep_ref[:, spans(at)] = out[:half]
-        give_ref[:, spans(at)] = out[half:]
-        keep_ref[:, shifted] = d_h[:half]
-        give_ref[:, shifted] = d_h[half:]
+        out_keep_ref[:, spans(at)] = out[:half]
+        out_give_ref[:, spans(at)] = out[half:]
+        keep_ref[:, spans(at)] = d_h[:half]
+        give_ref[:, spans(at)] = d_h[half:]
 
 
 def back_kernel(heads):
@@ -603,15 +611,15 @@
     return pl.BlockSpec(shape, lambda m, h, *_: (0, 0))
 
 
-def kernel_params(axes=2):
+def kernel_params(axes, mebibytes):
     return pltpu.CompilerParams(
-        dimension_semantics=("arbitrary",) * axes, vmem_limit_bytes=VMEM_BYTES
+        dimension_semantics=("arbitrary",) * axes, vmem_limit_bytes=mebibytes * 1024 * 1024
     )
 
 
 def busy(microseconds):
     return pl.CostEstimate(
-        flops=0, transcendentals=0, bytes_accessed=int(microseconds * 3.3e6)
+        flops=0, transcendentals=0, bytes_accessed=int(microseconds * 3.3e5)
     )
 
 
@@ -620,7 +628,9 @@
         self.micros = micros
         self.arrays = None
 
-    def call(self, body, micro, grid, prefetch, operands, in_specs, out, scratch, name, cost):
+    def call(
+        self, body, micro, grid, prefetch, operands, in_specs, out, scratch, name, cost, mebibytes
+    ):
         shared = [at for at, one in enumerate(out) if one[4]]
         held = [] if self.arrays is None else self.arrays
         skip = len(prefetch) + len(operands)
@@ -632,7 +642,8 @@
         for shape, dtype, block, index, is_shared in out:
             leading = (self.micros,) if is_shared else (1,)
             first = micro if is_shared else 0
-            out_shape.append(jax.ShapeDtypeStruct(leading + shape, dtype))
+            place = pltpu.HBM if is_shared else jax.ShapeDtypeStruct
+            out_shape.append(place(leading + shape, dtype))
             out_specs.append(
                 pl.BlockSpec((None,) + block, lambda *g, i=index, f=first: (f,) + i(*g))
             )
@@ -647,7 +658,7 @@
             ),
             out_shape=out_shape,
             input_output_aliases={skip + at: shared[at] for at in range(len(held))},
-            compiler_params=kernel_params(len(grid)),
+            compiler_params=kernel_params(len(grid), mebibytes),
             cost_estimate=busy(cost),
             name=name,
         )(*prefetch, *operands, *held)
@@ -716,7 +727,7 @@
             out_specs=out_specs,
         ),
         out_shape=out_shape,
-        compiler_params=kernel_params(),
+        compiler_params=kernel_params(2, 12),
         cost_estimate=busy(10.0 * micros),
         name="mixer_local",
     )(ends, pre, pre, pre, pre, *filters, params)
@@ -770,6 +781,7 @@
         [pltpu.VMEM((rows, width), F32)],
         "mixer_output",
         6.0,
+        14,
     )
 
 
@@ -804,13 +816,14 @@
         [pltpu.VMEM((rows, DV), F32)],
         "mixer_gate_back",
         6.0,
+        14,
     )
 
 
 def run_feed_forward(shared, micro, h_two, cot, weights):
     rows, width = cot.shape[1:]
     hidden = weights.shape[2]
-    sums = (rows // 2, 2 * width)
+    sums = (rows // 2, width)
     kept = (rows, hidden)
     return shared.call(
         feed_forward_kernel,
@@ -826,6 +839,8 @@
         [
             (sums, BF16, sums, at_origin, False),
             (sums, BF16, sums, at_origin, False),
+            (sums, BF16, sums, at_origin, True),
+            (sums, BF16, sums, at_origin, True),
             ((rows, width), BF16, (rows, width), at_origin, True),
             (kept, BF16, kept, at_origin, True),
             (kept, BF16, kept, at_origin, True),
@@ -834,6 +849,7 @@
         [],
         "feed_forward",
         9.0,
+        20,
     )
 
 
@@ -876,6 +892,7 @@
         ],
         "mixer_back",
         14.0,
+        16,
     )
 
 
@@ -1010,7 +1027,7 @@
                 out_specs=pl.BlockSpec((devices, 2) + half, lambda *_: (0, 0, 0, 0)),
             ),
             out_shape=jax.ShapeDtypeStruct((devices, 2) + half, self.rows.dtype),
-            compiler_params=kernel_params(1),
+            compiler_params=kernel_params(1, 12),
             cost_estimate=busy(2.0),
             name="place_weights",
         )(where, self.rows.reshape((2,) + half), *pieces)
@@ -1181,11 +1198,8 @@
     slots = slot_table("head")
     first = GatherWeights(w_first)
     first.swap()
-    second = GatherWeights(after(w_second, *first.got))
-    w_first, h_one, cot, w_third = lax.optimization_barrier(
-        (first.result(), h_one, cot, w_third)
-    )
-    w_third = lax.all_gather(after(w_third, *second.got), "fsdp", axis=0)
+    second = GatherWeights(after(w_second, first.other[0]))
+    w_first, h_one, cot = lax.optimization_barrier((first.result(), h_one, cot))
 
     conv_q = lax.dynamic_slice_in_dim(conv_query, head_place * qw, qw, 1)
     conv_k = lax.dynamic_slice_in_dim(conv_key, head_place * qw, qw, 1)
@@ -1215,7 +1229,7 @@
     pres, found, saves, transes = {}, {}, {}, {}
     states_in, gates, outs, statess = {}, {}, {}, {}
     attn, rows_two, x_ones, sums, back_sums, back_rows = {}, {}, {}, {}, {}, {}
-    y_parts, mlp_terms, d_x_ones = {}, {}, {}
+    mlp_terms, d_x_ones = {}, {}
     backed, exts, smalls, gain_sums = {}, {}, {}, {}
 
     def project(m):
@@ -1259,9 +1273,8 @@
         sums[m] = Scatter(keep, give, "head")
         return keep
 
-    def to_gate_back(m, both):
-        y_parts[m] = (x_ones[m] + both[..., :model]).astype(BF16)
-        d_norm, terms = rms_back(x_ones[m], mlp_gain, both[..., model:])
+    def to_gate_back(m, summed):
+        d_norm, terms = rms_back(x_ones[m], mlp_gain, summed)
         mlp_terms[m] = jnp.sum(terms, axis=(0, 1))
         d_x_ones[m] = cot[m : m + 1, :row_count].astype(F32) + d_norm
         back_rows[m] = Gather(d_x_ones[m].astype(BF16), "head")
@@ -1300,67 +1313,59 @@
 
     project(0)
     done = local(0)
+    second.swap(done)
+    w_third = lax.all_gather(after(w_third, *second.got), "fsdp", axis=0)
     project(1)
-    second.swap(done)
-    done = local(1, done, *second.got)
+    done = local(1, done)
     w_second = second.result(done)
     w_g = w_second[:, :vw]
     project_gate(0)
     done = output(0, done)
-    moved = project(2)
-    attn[0].advance(moved)
-    done = local(2, done, attn[0].sent)
+    project(2)
+    done = local(2, done)
+    attn[0].advance(done)
     project_gate(1)
+    done = output(1, done, attn[0].sent)
     to_feed_forward(0, attn[0].finish(done))
-    done = output(1, done, rows_two[0].sent)
-    moved = project_gate(2)
-    attn[1].advance(moved)
-    rows_two[0].advance(done)
-    done = output(2, done, attn[1].sent, rows_two[0].sent)
-    halves = rows_two[0].finish(done)
-    to_feed_forward(1, attn[1].finish(halves[1]))
-    attn[2].advance(halves[1])
-    done = feed_forward(0, halves, attn[2].sent, rows_two[1].sent)
-    rows_two[1].advance(done)
-    to_feed_forward(2, attn[2].finish(done))
-    halves = rows_two[1].finish(sums[0].sent, rows_two[2].sent)
-    sums[0].advance(halves[1])
-    done = feed_forward(1, halves, done, sums[0].sent)
+    project_gate(2)
+    done = output(2, done, rows_two[0].sent)
+    attn[1].advance(done)
+    rows_two[0].advance(attn[1].sent)
+    attn[2].advance(rows_two[0].sent)
+    done = feed_forward(0, rows_two[0].finish(attn[2].sent))
+    to_feed_forward(1, attn[1].finish(done))
+    to_feed_forward(2, attn[2].finish(rows_two[1].sent))
+    sums[0].advance(rows_two[2].sent)
+    rows_two[1].advance(sums[0].sent)
+    done = feed_forward(1, rows_two[1].finish(rows_two[1].sent))
     rows_two[2].advance(done)
-    to_gate_back(0, sums[0].finish(done))
-    halves = rows_two[2].finish(sums[1].sent, back_rows[0].sent)
-    sums[1].advance(halves[1])
-    back_rows[0].advance(halves[1])
-    done = feed_forward(2, halves, done, sums[1].sent, back_rows[0].sent)
-
-    h_two, hid, d_ffg, d_ffu = forwards.arrays
-    halves = back_rows[0].finish(done)
-    to_gate_back(1, sums[1].finish(done))
-    sums[2].advance(done)
-    done = gate_back(0, halves, back_rows[1].sent, sums[2].sent)
+    sums[1].advance(rows_two[2].sent)
+    to_gate_back(0, sums[0].finish(sums[1].sent))
+    done = feed_forward(2, rows_two[2].finish(back_rows[0].sent))
+    out_keep, out_give, h_two, hid, d_ffg, d_ffu = forwards.arrays
+    grad_gate = grad_of(after(d_ffg, done), h_two)
+    sums[2].advance(grad_gate)
+    back_rows[0].advance(sums[2].sent)
+    grad_up = grad_of(after(d_ffu, back_rows[0].sent), h_two)
+    to_gate_back(1, sums[1].finish(grad_up))
+    grad_down = grad_of(after(hid, back_rows[1].sent), cot)
+    done = gate_back(0, back_rows[0].finish(grad_down))
     back_rows[1].advance(done)
-    to_gate_back(2, sums[2].finish(done))
-    ff_grads = [
-        grad_of(after(d_ffg, done, back_rows[1].sent, back_rows[2].sent), h_two),
-        grad_of(d_ffu, h_two),
-        grad_of(hid, cot),
-    ]
-    ff_grads = jnp.stack(ff_grads).reshape(3, hidden_width, owners, -1)
+    to_gate_back(2, sums[2].finish(back_rows[1].sent))
+    ff_grads = jnp.stack([after(grad_gate, back_rows[2].sent), grad_up, grad_down])
+    ff_grads = ff_grads.reshape(3, hidden_width, owners, -1)
     ff_grads = jnp.transpose(ff_grads, (2, 0, 1, 3))
-    halves = back_rows[1].finish(ff_grads)
-    back_rows[2].advance(ff_grads)
-    done = gate_back(1, halves, back_rows[2].sent, backed[0][2])
     ff_shard = scatter_grad(ff_grads)[0]
-    done = back(0, done)
-    done = gate_back(2, back_rows[2].finish(done), done, backed[1][2])
+    done = gate_back(1, back_rows[1].finish(ff_grads))
+    back_rows[2].advance(done)
+    done = back(0, back_rows[2].sent)
+    done = gate_back(2, back_rows[2].finish(done), backed[1][2])
+    out_sum = Scatter(after(out_keep, done), out_give, "head")
     d_gates, d_attn_rows = gate_backs.arrays
     side_grads = jnp.concatenate(
         [grad_of(h_one, d_gates), grad_of(d_attn_rows, outputs.arrays[0])], axis=1
     )
     side = Reduce(side_grads)
-    done = back(1, done, side.sent, backed[2][2])
-    side.spread(done)
-
     dx_parts, attn_terms, d_h_sums = {}, {}, {}
 
     def to_input(m, *waits):
@@ -1379,12 +1384,19 @@
         d_first, _ = rms_back(x_parts[m], attn_gain, summed)
         dx_parts[m] = d_x_ones[m] + d_first
 
+    done = back(1, done, side.sent, backed[2][2], out_sum.sent)
     to_input(0, done)
-    done = back(2, done, *side.gives, d_h_sums[0].sent)
+    to_input(1, d_h_sums[0].sent)
+    out_sum.advance(d_h_sums[1].sent)
+    side.spread(out_sum.sent)
+    d_h_sums[0].advance(*side.gives)
+    done = back(2, done, *side.gives, d_h_sums[0].sent, ff_shard)
+    x_all = jnp.concatenate([x_ones[m] for m in micros])
+    block_output = (x_all + out_sum.finish(done)).astype(BF16)
     mix_grad = grad_of(h_one, backs.arrays[0])
     mix = [Reduce(mix_grad[:, : 2 * qw]), Reduce(mix_grad[:, 2 * qw :])]
     to_input(2, mix[0].sent, mix[1].sent)
-    to_input(1, mix[0].sent, mix[1].sent)
+    d_h_sums[1].advance(d_h_sums[2].sent)
 
     small = sum(jnp.sum(one, axis=0) for one in smalls.values())
     rate_sums = small[:2, rates_at : rates_at + heads]
@@ -1406,24 +1418,20 @@
     packed = jnp.pad(packed, (0, -length % 1024)).reshape(-1, LANES)
     small_sum = SmallSum(packed)
     small_sum.step()
-    d_h_sums[0].advance(small_sum.value)
     side_shard = side.finish(small_sum.value)
+    small_sum.step(side_shard)
+    to_end(0, d_h_sums[0].finish(small_sum.value))
     ff_shard = [ff_shard[0].T, ff_shard[1].T, ff_shard[2]]
-    block_output = jnp.concatenate([y_parts[m] for m in micros])
-    mix[0].spread(side_shard, block_output, d_h_sums[0].sent)
+    mix[0].spread(side_shard, block_output, dx_parts[0])
     d_h_sums[2].advance(*mix[0].gives)
-    d_h_sums[1].advance(*mix[0].gives)
     small_sum.step(*mix[0].gives)
-    to_end(0, d_h_sums[0].finish(d_h_sums[1].sent))
-    mix[1].spread(small_sum.value, *ff_shard, dx_parts[0])
+    to_end(1, d_h_sums[1].finish(small_sum.value))
+    mix[1].spread(small_sum.value, *ff_shard, dx_parts[1])
     small_sum.step(*mix[1].gives)
     to_end(2, d_h_sums[2].finish(small_sum.value))
-    to_end(1, d_h_sums[1].finish(small_sum.value))
     input_grad = jnp.concatenate([dx_parts[m] for m in micros])
-    small_sum.step(input_grad)
-    total = mix[0].finish(small_sum.value)
-    small_sum.step(total)
-    shard_mix = jnp.concatenate([total, mix[1].finish(small_sum.value)], axis=1)
+    total = mix[0].finish(input_grad)
+    shard_mix = jnp.concatenate([total, mix[1].finish(total)], axis=1)
     packed = small_sum.finish().reshape(-1)
     totals, at = [], 0
     for piece in pieces:

time: 514 us -> 470 us (0.914)
  Pallas kernels: 156 us -> 126 us
  matrix products: 66.7 us -> 47.3 us
  local copies, waits for them, and re-layouts: 57.4 us -> 70.3 us
  waiting for transfers between devices: 70.8 us -> 60.8 us
    ppermute x44 -> x46, waiting for transfers between devices: 54.4 us -> 32.1 us  [swapped(): lax.ppermute(block, axis, [(i, i ^ bit) for i in range(lax.axis_size(axis...]
    unnamed x255 -> x317, local copies, waits for them, and re-layouts: 22.1 us -> 42.1 us
    pallas_call x12, Pallas kernels: 115 us -> 96.8 us  [call(): pl.pallas_call(wrapped, grid_spec=pltpu.PrefetchScalarGridSpec(num_scalar...]
    dot_general x6, matrix products: 20.6 us -> 6.93 us  [mat(): lax.dot_general(left, right, (((2,), (0,)), ((), ())), preferred_element_...]
    ppermute x10, waiting for transfers between devices: 10.4 us -> 20.5 us  [passed_along(): return lax.ppermute(block, axis, route)]
    dot_general x9, matrix products: 25.1 us -> 18.1 us  [mat_t(): lax.dot_general(left, right, (((2,), (1,)), ((), ())), preferred_element_...]
    all_gather x1, waiting for transfers between devices: 0.01 us -> 6.67 us  [per_device(): w_third = lax.all_gather(after(w_third, *second.got), 'fsdp', axis=0)]
    reduce_sum x5, other arithmetic: 2.82 us -> 8.87 us  [rms_unit(): jnp.mean(values * values, axis=-1, keepdims=True) + 1e-05]
  transfers between devices with their start and end apart: 71 -> 73, of which waited for: 17 -> 16; matrix products, arithmetic and copies ran while one was open for 31% -> 28% of each run, Pallas kernels for 31% -> 27%
where the time goes in v2:
time: 470 us; the launch traced here: 461 us
  Pallas kernels  126 us (27%)
  starting transfers between devices  82.5 us (18%)
  local copies, waits for them, and re-layouts  70.3 us (15%)
  waiting for transfers between devices  60.8 us (13%)
  other arithmetic  57.4 us (12%)
  matrix products  47.3 us (10%)
  between operations  16.9 us (4%)
    pallas_call x12, Pallas kernels, call(): pl.pallas_call(wrapped, grid_spec=pltpu.PrefetchScalarGridSpec(num_scalar...  96.8 us
    unnamed x317, local copies, waits for them, and re-layouts  42.1 us
    ppermute x46, waiting for transfers between devices, swapped(): lax.ppermute(block, axis, [(i, i ^ bit) for i in range(lax.axis_size(axis...  32.1 us
    ppermute x46, starting transfers between devices, swapped(): lax.ppermute(block, axis, [(i, i ^ bit) for i in range(lax.axis_size(axis...  31.7 us
    pallas_call x3, Pallas kernels, run_local(): pl.pallas_call(local_kernel(heads, with_trans), grid_spec=pltpu.PrefetchS...  26.9 us
    dot_general x6, matrix products, grad_of(): lax.dot_general(left, right, (((0,), (0,)), ((), ())), preferred_element_...  22.2 us
    ppermute x10, starting transfers between devices, passed_along(): return lax.ppermute(block, axis, route)  21.8 us
    ppermute x10, waiting for transfers between devices, passed_along(): return lax.ppermute(block, axis, route)  20.5 us
  transfers between devices with their start and end apart: 73, of which 16 were waited for; matrix products, arithmetic and copies ran while one was open for 28% of the time, Pallas kernels for 27%

profile of v2, /device:TPU:0, one launch (start us, length us, event | category | flops | bytes accessed | tf_op | source)
XLA Modules:
  0.0 461.4 jit_solution(11755797563100555826)
XLA Ops:
  11.0 3.0 collective-permute-start
  14.0 2.6 collective-permute-start.1
  19.5 3.4 collective-permute-start.6
  31.6 2.8 fusion
  39.1 5.4 %collective-permute-done.3.refs_3_ = bf16[128,1152]{1,0:T(8,128)(2,1)S(1)} collective-permute-done((bf16[128,1152]{1,0:T(8,128)(2,1)S(1)}, bf16[128,1152]{1,0:T(8,128)(2,1)S(1)}, u32[]{:S(2)}, u32[]{:S(2)}) %collective-permute-start.3) | collective-permute-done | bytes 294944 | tf_op jit(solution)/shard_map/ppermute | solution.py:906
  47.5 2.2 collective-permute-start.10
  50.8 4.0 collective-permute-done.5.refs_5_
  60.0 9.4 %mixer_local.3 = (bf16[1,2,512,128]{3,2,1,0:T(8,128)(2,1)S(1)}, f32[1,512,512]{2,1,0:T(8,128)S(1)}, bf16[1,2,512,128]{3,2,1,0:T(8,128)(2,1)S(1)}, f32[1,2,512,25...) custom-call(s32[1,9]{1,0:T(1,128)S(1)} %get-tuple-element.483.ends_r, ...), custom_call_target="tpu_custom_call" | custom-call | bytes 3300000 | tf_op jit(solution)/shard_map/mixer_local/pallas_call | solution.py:718
  74.2 3.6 fusion.84
  77.8 2.4 collective-permute-start.7
  84.1 8.8 %mixer_local.4 = (bf16[1,2,512,128]{3,2,1,0:T(8,128)(2,1)S(1)}, f32[1,512,512]{2,1,0:T(8,128)S(1)}, bf16[1,2,512,128]{3,2,1,0:T(8,128)(2,1)S(1)}, f32[1,2,512,25...) custom-call(s32[1,9]{1,0:T(1,128)S(1)} %get-tuple-element.481.ends_r, ...), custom_call_target="tpu_custom_call" | custom-call | bytes 3300000 | tf_op jit(solution)/shard_map/mixer_local/pallas_call | solution.py:718
  92.9 3.9 collective-permute-start.16
  96.8 2.8 collective-permute-done.11.refs_3_
  102.9 4.5 mixer_output.3
  109.1 8.8 %mixer_local.5 = (bf16[1,2,512,128]{3,2,1,0:T(8,128)(2,1)S(1)}, f32[1,512,512]{2,1,0:T(8,128)S(1)}, bf16[1,2,512,128]{3,2,1,0:T(8,128)(2,1)S(1)}, f32[1,2,512,25...) custom-call(s32[1,9]{1,0:T(1,128)S(1)} %get-tuple-element.482.ends_r, ...), custom_call_target="tpu_custom_call" | custom-call | bytes 3300000 | tf_op jit(solution)/shard_map/mixer_local/pallas_call | solution.py:718
  121.3 4.4 collective-permute-start.18
  125.7 4.5 mixer_output.4
  132.0 13.0 %mixer_output.5 = (bf16[3,512,512]{2,1,0:T(8,128)(2,1)}, f32[1,512,512]{2,1,0:T(8,128)S(1)}, bf16[1,2,512,256]{3,2,1,0:T(8,128)(2,1)S(1)}, bf16[1,256,1024]{2,1,0:T(8,128)(2,1)S(1)}, bf16[1,256,1024]{2,1,0:T(8,128)(2,1)S(1)}) custom-call(s32[4]{0:T(128)S(1)} %fusion.76.refs_0_, ...), custom_call_target="tpu_custom_call", output_to_operand_aliasing={{0}: (10, {})} | custom-call | bytes 1980000 | tf_op jit(solution)/shard_map/mixer_output/pallas_call | solution.py:650
  151.4 6.7 %all-gather.3.cloned.1.call-done = bf16[12,704,256]{2,1,0:T(8,128)(2,1)} async-done(((bf16[3,704,256]{2,1,0:T(8,128)(2,1)}), bf16[12,704,256]{2,1,0:T(8,128)(2,1)}) %all-gather.3.cloned.1.call-update) | async-done | bytes 4325392 | tf_op jit(solution)/shard_map/all_gather | solution.py:1317
  160.0 2.2 copy-done.11
  164.3 6.6 %feed_forward.3 = (bf16[1,256,1024]{2,1,0:T(8,128)(2,1)S(1)}, bf16[1,256,1024]{2,1,0:T(8,128)(2,1)S(1)}, bf16[3,256,1024]{2,1,0:T(8,128)(2,1)}, bf16[3,256,1024]...) custom-call(bf16[1,256,1024]{2,1,0:T(8,128)(2,1)S(1)} %copy-done.27,, ...), custom_call_target="tpu_custom_call" | custom-call | bytes 2970000 | tf_op jit(solution)/shard_map/feed_forward/pallas_call | solution.py:650
  178.1 3.0 collective-permute-done.25
  183.2 6.4 %feed_forward.4 = (bf16[1,256,1024]{2,1,0:T(8,128)(2,1)S(1)}, bf16[1,256,1024]{2,1,0:T(8,128)(2,1)}, bf16[3,256,1024]{2,1,0:T(8,128)(2,1)}, bf16[3,256,1024]{2,1...) custom-call(bf16[1,256,1024]{2,1,0:T(8,128)(2,1)S(1)} %pad_maximum_f, ...), custom_call_target="tpu_custom_call", output_to_operand_aliasing={{2}: (4, {}), {3}: (5, {}), {4}: (6, {}), {5}: (7, {}), {6}... | custom-call | bytes 2970000 | tf_op jit(solution)/shard_map/feed_forward/pallas_call | solution.py:650
  197.7 4.2 collective-permute-done.29
  204.7 2.2 copy-done.13
  206.9 6.6 %feed_forward.5 = (bf16[1,256,1024]{2,1,0:T(8,128)(2,1)S(1)}, bf16[1,256,1024]{2,1,0:T(8,128)(2,1)S(1)}, bf16[3,256,1024]{2,1,0:T(8,128)(2,1)}, bf16[3,256,1024]...) custom-call(bf16[1,256,1024]{2,1,0:T(8,128)(2,1)S(1)} %pad_maximum_f, ...), custom_call_target="tpu_custom_call", output_to_operand_aliasing={{2}: (4, {}), {3}: (5, {}), {4}: (6, {}), {5}: (7, {}), {6}... | custom-call | bytes 2970000 | tf_op jit(solution)/shard_map/feed_forward/pallas_call | solution.py:650
  213.6 5.2 %bitcast_convert_fusion.3 = bf16[704,1024]{1,0:T(8,128)(2,1)S(1)} fusion(bf16[3,512,704]{2,1,0:T(8,128)(2,1)} %get-tuple-element.262, bf16[3,512,1024]{2,1,0:T(8,128)(2,1)} %get-tuple-element.263), kind=kOutput, calls=%fused_computation.15 | convolution fusion | flops 2215313408 | bytes 6750208 | tf_op jit(solution)/shard_map/dot_general | solution.py:1145
  220.7 2.4 bitcast_convert_fusion.2
  225.7 3.0 bitcast_convert_fusion.1
  231.0 4.6 mixer_gate_back.3
  240.4 2.3 maximum_bitcast_fusion
  245.9 5.6 %mixer_gate_back.4 = (bf16[1,512,512]{2,1,0:T(8,128)(2,1)S(1)}, f32[1,2,512,256]{3,2,1,0:T(8,128)S(1)}, bf16[3,528,512]{2,1,0:T(8,128)(2,1)}, bf16[3,512,1024]{2...) custom-call(s32[4]{0:T(128)S(1)} %fusion.76.refs_0_, ...), custom_call_target="tpu_custom_call", output_to_operand_aliasing={{2}: (10, {}), {3}: (11, {})} | custom-call | bytes 1980000 | tf_op jit(solution)/shard_map/mixer_gate_back/pallas_call | solution.py:650
  259.1 4.7 %collective-permute-done.41.refs_12_ = bf16[1,2,128,256]{3,2,1,0:T(8,128)(2,1)S(1)} collective-permute-done((bf16[1,2,128,256]{3,2,1,0:T(8,128)(2,1)}, bf16[1,2,128,256]{3,2,1,0:T(8,128)(2,1)S(1)}, u32[]{:S(2)}, u32[]{:S(2)}) %collective-permute-start.41) | collective-permute-done | bytes 131104 | tf_op jit(solution)/shard_map/ppermute | solution.py:902
  270.7 12.9 %mixer_back.3 = (bf16[3,528,1152]{2,1,0:T(8,128)(2,1)}, bf16[1,528,1152]{2,1,0:T(8,128)(2,1)S(1)}, f32[1,8,1152]{2,1,0:T(8,128)S(1)}) custom-call(f32[1,528,1152]{2,1,0:T(8,128)S(1)} %copy-done.7, f32[1,528,1152]{2,1,0:T(8,128)S(1)} %copy-done.7, f32[1,528,1152]{2,1,0:T(8,128)S(1)} %copy-done.7, f32[1,2,8,512]{3,2,1,0:T(8,128)S(1)} %copy-done.81, ...), custom_call_target="tpu_custom_call" | custom-call | bytes 4620000 | tf_op jit(solution)/shard_map/mixer_back/pallas_call | solution.py:650
  285.0 5.7 %mixer_gate_back.5 = (bf16[1,512,512]{2,1,0:T(8,128)(2,1)S(1)}, f32[1,2,512,256]{3,2,1,0:T(8,128)S(1)}, bf16[3,528,512]{2,1,0:T(8,128)(2,1)}, bf16[3,512,1024]{2...) custom-call(s32[4]{0:T(128)S(1)} %fusion.76.refs_0_, ...), custom_call_target="tpu_custom_call", output_to_operand_aliasing={{2}: (10, {}), {3}: (11, {})} | custom-call | bytes 1980000 | tf_op jit(solution)/shard_map/mixer_gate_back/pallas_call | solution.py:650
  302.7 2.7 collective-permute-start.47
  305.4 4.4 collective-permute-done.43.refs_12_
  309.9 13.7 %mixer_back.4 = (bf16[3,528,1152]{2,1,0:T(8,128)(2,1)}, bf16[1,528,1152]{2,1,0:T(8,128)(2,1)S(1)}, f32[1,8,1152]{2,1,0:T(8,128)S(1)}) custom-call(f32[1,528,1152]{2,1,0:T(8,128)S(1)} %copy-done.5, f32[1,528,1152]{2,1,0:T(8,128)S(1)} %copy-done.5, f32[1,528,1152]{2,1,0:T(8,128)S(1)} %copy-done.5, ...), custom_call_target="tpu_custom_call", output_to_operand_aliasing={{0}: (14, {})} | custom-call | bytes 4620000 | tf_op jit(solution)/shard_map/mixer_back/pallas_call | solution.py:650
  325.5 3.0 fusion.90
  328.8 10.6 %collective-permute-done.44 = bf16[1,16,1152]{2,1,0:T(8,128)(2,1)S(1)} collective-permute-done((bf16[1,16,1152]{2,1,0:T(8,128)(2,1)S(1)}, bf16[1,16,1152]{2,1,0:T(8,128)(2,1)S(1)}, u32[]{:S(2)}, u32[]{:S(2)}) %collective-permute-start.44) | collective-permute-done | bytes 36896 | tf_op jit(solution)/shard_map/ppermute | solution.py:902
  340.1 4.3 fusion.8
  353.2 12.8 %mixer_back.5 = (bf16[3,528,1152]{2,1,0:T(8,128)(2,1)}, bf16[1,528,1152]{2,1,0:T(8,128)(2,1)S(1)}, f32[1,8,1152]{2,1,0:T(8,128)S(1)}) custom-call(f32[1,528,1152]{2,1,0:T(8,128)S(1)} %copy-done.3, f32[1,528,1152]{2,1,0:T(8,128)S(1)} %copy-done.3, f32[1,528,1152]{2,1,0:T(8,128)S(1)} %copy-done.3, ...), custom_call_target="tpu_custom_call", output_to_operand_aliasing={{0}: (14, {})} | custom-call | bytes 4620000 | tf_op jit(solution)/shard_map/mixer_back/pallas_call | solution.py:650
  366.0 7.7 %bitcast_convert_fusion = bf16[1024,1152]{1,0:T(8,128)(2,1)S(1)} fusion(bf16[3,528,1024]{2,1,0:T(8,128)(2,1)S(1)} %copy-done.113, bf16[3,528,1152]{2,1,0:T(8,128)(2,1)} %get-tuple-element.329), kind=kOutput, calls=%fused_computation.5 | convolution fusion | flops 3738304512 | bytes 9252864 | tf_op jit(solution)/shard_map/dot_general | solution.py:1145
  386.1 4.0 fusion.5
  409.2 4.3 collective-permute-start.63
  427.9 2.6 collective-permute-done.60
  431.2 2.2 collective-permute-start.67
  438.8 8.5 %collective-permute-done.70 = f32[152,128]{1,0:T(8,128)S(1)} collective-permute-done((f32[152,128]{1,0:T(8,128)S(1)}, f32[152,128]{1,0:T(8,128)S(1)}, u32[]{:S(2)}, u32[]{:S(2)}) %collective-permute-start.70) | collective-permute-done | bytes 77856 | tf_op jit(solution)/shard_map/ppermute | solution.py:906
  (603 shorter events, 190.0 us)
Async XLA Ops:
  7.2 150.9 %all-gather.3.cloned.1.call-start = ((), (), s32[]{:S(2)}) async-start(), calls=%async_computation.2 | async-start | bytes 5406720 | tf_op jit(solution)/shard_map/all_gather | solution.py:1317
  11.0 23.4 %collective-permute-start = (bf16[128,1152]{1,0:T(8,128)(2,1)}, bf16[128,1152]{1,0:T(8,128)(2,1)S(1)}, u32[]{:S(2)}, u32[]{:S(2)}) collective-permute-start(bf16[128,1152]{1,0:T(8,128)(2,1)} %constant_dynamic-slice_fusion.18), channel_id=1, source_target_pairs={{0,1},{1,2},{2,3},{3,0},{4,5},{5,6},{6,7},{7,4},{8,9},{9,10},{10,1... | collective-permute-start | bytes 884744 | tf_op jit(solution)/shard_map/ppermute | solution.py:995
  14.0 22.0 %collective-permute-start.1 = (bf16[128,1152]{1,0:T(8,128)(2,1)}, bf16[128,1152]{1,0:T(8,128)(2,1)S(1)}, u32[]{:S(2)}, u32[]{:S(2)}) collective-permute-start(bf16[128,1152]{1,0:T(8,128)(2,1)} %constant_dynamic-slice_fusion.18), channel_id=1, source_target_pairs={{0,2},{1,3},{2,0},{3,1},{4,6},{5,7},{6,4},{7,5},{8,10},{9,11},{10,... | collective-permute-start | bytes 884744 | tf_op jit(solution)/shard_map/ppermute | solution.py:995
  16.6 20.9 %collective-permute-start.2 = (bf16[128,1152]{1,0:T(8,128)(2,1)}, bf16[128,1152]{1,0:T(8,128)(2,1)S(1)}, u32[]{:S(2)}, u32[]{:S(2)}) collective-permute-start(bf16[128,1152]{1,0:T(8,128)(2,1)} %constant_dynamic-slice_fusion.18), channel_id=1, source_target_pairs={{0,3},{1,0},{2,1},{3,2},{4,7},{5,4},{6,5},{7,6},{8,11},{9,8},{10,9... | collective-permute-start | bytes 884744 | tf_op jit(solution)/shard_map/ppermute | solution.py:995
  36.0 14.7 %collective-permute-start.4 = (bf16[128,1152]{1,0:T(8,128)(2,1)S(1)}, bf16[128,1152]{1,0:T(8,128)(2,1)S(1)}, u32[]{:S(2)}, u32[]{:S(2)}) collective-permute-start(bf16[128,1152]{1,0:T(8,128)(2,1)S(1)} %collective-permute-done.1.refs_1_), channel_id=1, source_target_pairs={{0,16},{16,0},{1,17},{17,1},{2,18},{18,2},{3,19},{19,3},{4,20},{20... | collective-permute-start | bytes 884744 | tf_op jit(solution)/shard_map/ppermute | solution.py:906
  37.5 17.2 %collective-permute-start.5 = (bf16[128,1152]{1,0:T(8,128)(2,1)S(1)}, bf16[128,1152]{1,0:T(8,128)(2,1)S(1)}, u32[]{:S(2)}, u32[]{:S(2)}) collective-permute-start(bf16[128,1152]{1,0:T(8,128)(2,1)S(1)} %collective-permute-done.2.refs_2_), channel_id=1, source_target_pairs={{0,16},{16,0},{1,17},{17,1},{2,18},{18,2},{3,19},{19,3},{4,20},{20... | collective-permute-start | bytes 884744 | tf_op jit(solution)/shard_map/ppermute | solution.py:906
  44.5 28.9 %collective-permute-start.8 = (bf16[128,1024]{1,0:T(8,128)(2,1)S(1)}, bf16[128,1024]{1,0:T(8,128)(2,1)S(1)}, u32[]{:S(2)}, u32[]{:S(2)}) collective-permute-start(bf16[128,1024]{1,0:T(8,128)(2,1)S(1)} %constant_dynamic-slice_fusion.14), channel_id=1, source_target_pairs={{0,1},{1,2},{2,3},{3,0},{4,5},{5,6},{6,7},{7,4},{8,9},{9,10},{10,1... | collective-permute-start | bytes 786440 | tf_op jit(solution)/shard_map/ppermute | solution.py:995
  45.4 28.6 %collective-permute-start.9 = (bf16[128,1024]{1,0:T(8,128)(2,1)S(1)}, bf16[128,1024]{1,0:T(8,128)(2,1)}, u32[]{:S(2)}, u32[]{:S(2)}) collective-permute-start(bf16[128,1024]{1,0:T(8,128)(2,1)S(1)} %constant_dynamic-slice_fusion.14), channel_id=1, source_target_pairs={{0,2},{1,3},{2,0},{3,1},{4,6},{5,7},{6,4},{7,5},{8,10},{9,11},{10,... | collective-permute-start | bytes 786440 | tf_op jit(solution)/shard_map/ppermute | solution.py:995
  47.5 26.5 %collective-permute-start.10 = (bf16[128,1024]{1,0:T(8,128)(2,1)S(1)}, bf16[128,1024]{1,0:T(8,128)(2,1)}, u32[]{:S(2)}, u32[]{:S(2)}) collective-permute-start(bf16[128,1024]{1,0:T(8,128)(2,1)S(1)} %constant_dynamic-slice_fusion.14), channel_id=1, source_target_pairs={{0,3},{1,0},{2,1},{3,2},{4,7},{5,4},{6,5},{7,6},{8,11},{9,8},{10,9... | collective-permute-start | bytes 786440 | tf_op jit(solution)/shard_map/ppermute | solution.py:995
  74.1 346.6 %reduce-scatter.2.cloned.1.call-start = ((), (), s32[]{:S(2)}) async-start(), calls=%async_computation.1 | async-start | bytes 4866048 | tf_op jit(solution)/shard_map/reduce_scatter | solution.py:1150
  77.8 18.9 %collective-permute-start.7 = (bf16[1,2,128,256]{3,2,1,0:T(8,128)(2,1)}, bf16[1,2,128,256]{3,2,1,0:T(8,128)(2,1)S(1)}, u32[]{:S(2)}, u32[]{:S(2)}) collective-permute-start(bf16[1,2,128,256]{3,2,1,0:T(8,128)(2,1)} %get-tuple-element.187), channel_id=1, source_target_pairs={{0,16},{1,17},{2,18},{3,19},{4,20},{5,21},{6,22},{7,23},{8,24},{9,... | collective-permute-start | bytes 393224 | tf_op jit(solution)/shard_map/ppermute | solution.py:902
  80.3 16.5 %collective-permute-start.13 = (bf16[128,1024]{1,0:T(8,128)(2,1)}, bf16[128,1024]{1,0:T(8,128)(2,1)S(1)}, u32[]{:S(2)}, u32[]{:S(2)}) collective-permute-start(bf16[128,1024]{1,0:T(8,128)(2,1)} %collective-permute-done.10.refs_2_), channel_id=1, source_target_pairs={{0,16},{16,0},{1,17},{17,1},{2,18},{18,2},{3,19},{19,3},{4,20},{20... | collective-permute-start | bytes 786440 | tf_op jit(solution)/shard_map/ppermute | solution.py:906
  80.4 16.4 %collective-permute-start.12 = (bf16[128,1024]{1,0:T(8,128)(2,1)}, bf16[128,1024]{1,0:T(8,128)(2,1)S(1)}, u32[]{:S(2)}, u32[]{:S(2)}) collective-permute-start(bf16[128,1024]{1,0:T(8,128)(2,1)} %collective-permute-done.9.refs_1_), channel_id=1, source_target_pairs={{0,16},{16,0},{1,17},{17,1},{2,18},{18,2},{3,19},{19,3},{4,20},{20... | collective-permute-start | bytes 786440 | tf_op jit(solution)/shard_map/ppermute | solution.py:906
  82.4 17.2 %collective-permute-start.11 = (bf16[128,1024]{1,0:T(8,128)(2,1)S(1)}, bf16[128,1024]{1,0:T(8,128)(2,1)S(1)}, u32[]{:S(2)}, u32[]{:S(2)}) collective-permute-start(bf16[128,1024]{1,0:T(8,128)(2,1)S(1)} %copy-done.75), channel_id=1, source_target_pairs={{0,16},{16,0},{1,17},{17,1},{2,18},{18,2},{3,19},{19,3},{4,20},{20... | collective-permute-start | bytes 786440 | tf_op jit(solution)/shard_map/ppermute | solution.py:906
  92.9 32.8 %collective-permute-start.16 = (bf16[1,2,128,256]{3,2,1,0:T(8,128)(2,1)S(1)}, bf16[1,2,128,256]{3,2,1,0:T(8,128)(2,1)S(1)}, u32[]{:S(2)}, u32[]{:S(2)}) collective-permute-start(bf16[1,2,128,256]{3,2,1,0:T(8,128)(2,1)S(1)} %get-tuple-element.208), channel_id=1, source_target_pairs={{0,16},{1,17},{2,18},{3,19},{4,20},{5,21},{6,22},{7,23},{8,24},{9,... | collective-permute-start | bytes 393224 | tf_op jit(solution)/shard_map/ppermute | solution.py:902
  130.3 15.2 %collective-permute-start.17 = (bf16[1,256,1024]{2,1,0:T(8,128)(2,1)S(1)}, bf16[1,256,1024]{2,1,0:T(8,128)(2,1)S(1)}, u32[]{:S(2)}, u32[]{:S(2)}) collective-permute-start(bf16[1,256,1024]{2,1,0:T(8,128)(2,1)S(1)} %get-tuple-element.217), channel_id=1, source_target_pairs={{0,4},{4,0},{8,12},{12,8},{1,5},{5,1},{9,13},{13,9},{2,6},{6,2},{1... | collective-permute-start | bytes 1572872 | tf_op jit(solution)/shard_map/ppermute | solution.py:906
  131.3 15.1 %collective-permute-start.20 = (bf16[1,128,1024]{2,1,0:T(8,128)(2,1)S(1)}, bf16[1,128,1024]{2,1,0:T(8,128)(2,1)S(1)}, u32[]{:S(2)}, u32[]{:S(2)}) collective-permute-start(bf16[1,128,1024]{2,1,0:T(8,128)(2,1)S(1)} %multiply_convert_fusion.2), channel_id=1, source_target_pairs={{0,8},{4,12},{8,0},{12,4},{1,9},{5,13},{9,1},{13,5},{2,10},{6,14},... | collective-permute-start | bytes 786440 | tf_op jit(solution)/shard_map/ppermute | solution.py:906
  147.6 23.3 %collective-permute-start.19 = (bf16[1,128,1024]{2,1,0:T(8,128)(2,1)}, bf16[1,128,1024]{2,1,0:T(8,128)(2,1)}, u32[]{:S(2)}, u32[]{:S(2)}) collective-permute-start(bf16[1,128,1024]{2,1,0:T(8,128)(2,1)} %slice.546), channel_id=1, source_target_pairs={{0,8},{4,12},{8,0},{12,4},{1,9},{5,13},{9,1},{13,5},{2,10},{6,14},... | collective-permute-start | bytes 786440 | tf_op jit(solution)/shard_map/ppermute | solution.py:906
  150.0 24.5 %collective-permute-start.23 = (bf16[1,128,1024]{2,1,0:T(8,128)(2,1)}, bf16[1,128,1024]{2,1,0:T(8,128)(2,1)}, u32[]{:S(2)}, u32[]{:S(2)}) collective-permute-start(bf16[1,128,1024]{2,1,0:T(8,128)(2,1)} %slice.545), channel_id=1, source_target_pairs={{0,8},{4,12},{8,0},{12,4},{1,9},{5,13},{9,1},{13,5},{2,10},{6,14},... | collective-permute-start | bytes 786440 | tf_op jit(solution)/shard_map/ppermute | solution.py:906
  181.3 12.8 %collective-permute-start.24 = (bf16[1,128,1024]{2,1,0:T(8,128)(2,1)}, bf16[1,128,1024]{2,1,0:T(8,128)(2,1)}, u32[]{:S(2)}, u32[]{:S(2)}) collective-permute-start(bf16[1,128,1024]{2,1,0:T(8,128)(2,1)} %multiply_convert_fusion), channel_id=1, source_target_pairs={{0,8},{4,12},{8,0},{12,4},{1,9},{5,13},{9,1},{13,5},{2,10},{6,14},... | collective-permute-start | bytes 786440 | tf_op jit(solution)/shard_map/ppermute | solution.py:906
  197.1 26.0 %collective-permute-start.33 = (bf16[1,128,1024]{2,1,0:T(8,128)(2,1)S(1)}, bf16[1,128,1024]{2,1,0:T(8,128)(2,1)S(1)}, u32[]{:S(2)}, u32[]{:S(2)}) collective-permute-start(bf16[1,128,1024]{2,1,0:T(8,128)(2,1)S(1)} %slice.543), channel_id=1, source_target_pairs={{0,8},{4,12},{8,0},{12,4},{1,9},{5,13},{9,1},{13,5},{2,10},{6,14},... | collective-permute-start | bytes 786440 | tf_op jit(solution)/shard_map/ppermute | solution.py:906
  203.2 16.4 %collective-permute-start.34 = (bf16[1,128,1024]{2,1,0:T(8,128)(2,1)S(1)}, bf16[1,128,1024]{2,1,0:T(8,128)(2,1)S(1)}, u32[]{:S(2)}, u32[]{:S(2)}) collective-permute-start(bf16[1,128,1024]{2,1,0:T(8,128)(2,1)S(1)} %get-tuple-element.425), channel_id=1, source_target_pairs={{0,8},{4,12},{8,0},{12,4},{1,9},{5,13},{9,1},{13,5},{2,10},{6,14},... | collective-permute-start | bytes 786440 | tf_op jit(solution)/shard_map/ppermute | solution.py:906
  219.0 17.5 %collective-permute-start.32 = (bf16[1,128,1024]{2,1,0:T(8,128)(2,1)S(1)}, bf16[1,128,1024]{2,1,0:T(8,128)(2,1)S(1)}, u32[]{:S(2)}, u32[]{:S(2)}) collective-permute-start(bf16[1,128,1024]{2,1,0:T(8,128)(2,1)S(1)} %slice.542), channel_id=1, source_target_pairs={{0,8},{4,12},{8,0},{12,4},{1,9},{5,13},{9,1},{13,5},{2,10},{6,14},... | collective-permute-start | bytes 786440 | tf_op jit(solution)/shard_map/ppermute | solution.py:906
  238.4 14.9 %collective-permute-start.37 = (bf16[1,128,1024]{2,1,0:T(8,128)(2,1)}, bf16[1,128,1024]{2,1,0:T(8,128)(2,1)}, u32[]{:S(2)}, u32[]{:S(2)}) collective-permute-start(bf16[1,128,1024]{2,1,0:T(8,128)(2,1)} %get-tuple-element.421), channel_id=1, source_target_pairs={{0,8},{4,12},{8,0},{12,4},{1,9},{5,13},{9,1},{13,5},{2,10},{6,14},... | collective-permute-start | bytes 786440 | tf_op jit(solution)/shard_map/ppermute | solution.py:906
  254.3 30.6 %collective-permute-start.40 = (bf16[1,256,1024]{2,1,0:T(8,128)(2,1)S(1)}, bf16[1,256,1024]{2,1,0:T(8,128)(2,1)}, u32[]{:S(2)}, u32[]{:S(2)}) collective-permute-start(bf16[1,256,1024]{2,1,0:T(8,128)(2,1)S(1)} %pad_maximum_fusion.10.refs_1_), channel_id=1, source_target_pairs={{0,4},{4,0},{8,12},{12,8},{1,5},{5,1},{9,13},{13,9},{2,6},{6,2},{1... | collective-permute-start | bytes 1572872 | tf_op jit(solution)/shard_map/ppermute | solution.py:906
  256.7 28.2 %collective-permute-start.39 = (bf16[1,2,128,256]{3,2,1,0:T(8,128)(2,1)}, bf16[1,2,128,256]{3,2,1,0:T(8,128)(2,1)}, u32[]{:S(2)}, u32[]{:S(2)}) collective-permute-start(bf16[1,2,128,256]{3,2,1,0:T(8,128)(2,1)} %get-tuple-element.283), channel_id=1, source_target_pairs={{16,0},{17,1},{18,2},{19,3},{20,4},{21,5},{22,6},{23,7},{24,8},{25... | collective-permute-start | bytes 393224 | tf_op jit(solution)/shard_map/ppermute | solution.py:902
  258.6 87.6 %collective-permute-start.42 = (bf16[3,256,1024]{2,1,0:T(8,128)(2,1)}, bf16[3,256,1024]{2,1,0:T(8,128)(2,1)}, u32[]{:S(2)}, u32[]{:S(2)}) collective-permute-start(bf16[3,256,1024]{2,1,0:T(8,128)(2,1)} %get-tuple-element.299), channel_id=1, source_target_pairs={{0,4},{4,0},{8,12},{12,8},{1,5},{5,1},{9,13},{13,9},{2,6},{6,2},{1... | collective-permute-start | bytes 4718600 | tf_op jit(solution)/shard_map/ppermute | solution.py:906
  283.6 39.9 %collective-permute-start.45 = (bf16[1,16,1152]{2,1,0:T(8,128)(2,1)S(1)}, bf16[1,16,1152]{2,1,0:T(8,128)(2,1)S(1)}, u32[]{:S(2)}, u32[]{:S(2)}) collective-permute-start(bf16[1,16,1152]{2,1,0:T(8,128)(2,1)S(1)} %slice.302), channel_id=1, source_target_pairs={{16,0},{17,1},{18,2},{19,3},{20,4},{21,5},{22,6},{23,7},{24,8},{25... | collective-permute-start | bytes 110600 | tf_op jit(solution)/shard_map/ppermute | solution.py:902
  302.7 46.7 %collective-permute-start.47 = (bf16[512,1024]{0,1:T(8,128)(2,1)S(1)}, bf16[512,1024]{0,1:T(8,128)(2,1)S(1)}, u32[]{:S(2)}, u32[]{:S(2)}) collective-permute-start(bf16[512,1024]{0,1:T(8,128)(2,1)S(1)} %fusion.27), channel_id=1, source_target_pairs={{0,16},{16,0},{1,17},{17,1},{2,18},{18,2},{3,19},{19,3},{4,20},{20... | collective-permute-start | bytes 3145736 | tf_op jit(solution)/shard_map/ppermute | solution.py:906
  324.2 15.1 %collective-permute-start.44 = (bf16[1,16,1152]{2,1,0:T(8,128)(2,1)S(1)}, bf16[1,16,1152]{2,1,0:T(8,128)(2,1)S(1)}, u32[]{:S(2)}, u32[]{:S(2)}) collective-permute-start(bf16[1,16,1152]{2,1,0:T(8,128)(2,1)S(1)} %slice.299), channel_id=1, source_target_pairs={{16,0},{17,1},{18,2},{19,3},{20,4},{21,5},{22,6},{23,7},{24,8},{25... | collective-permute-start | bytes 110600 | tf_op jit(solution)/shard_map/ppermute | solution.py:902
  328.7 22.2 %collective-permute-start.48 = (bf16[1,256,1024]{2,1,0:T(8,128)(2,1)S(1)}, bf16[1,256,1024]{2,1,0:T(8,128)(2,1)S(1)}, u32[]{:S(2)}, u32[]{:S(2)}) collective-permute-start(bf16[1,256,1024]{2,1,0:T(8,128)(2,1)S(1)} %pad_maximum_fusion.11), channel_id=1, source_target_pairs={{0,4},{4,0},{8,12},{12,8},{1,5},{5,1},{9,13},{13,9},{2,6},{6,2},{1... | collective-permute-start | bytes 1572872 | tf_op jit(solution)/shard_map/ppermute | solution.py:906
  346.1 45.7 %collective-permute-start.55 = (bf16[1,256,1024]{2,1,0:T(8,128)(2,1)}, bf16[1,256,1024]{2,1,0:T(8,128)(2,1)}, u32[]{:S(2)}, u32[]{:S(2)}) collective-permute-start(bf16[1,256,1024]{2,1,0:T(8,128)(2,1)} %pad_maximum_fusion.12), channel_id=1, source_target_pairs={{0,4},{4,0},{8,12},{12,8},{1,5},{5,1},{9,13},{13,9},{2,6},{6,2},{1... | collective-permute-start | bytes 1572872 | tf_op jit(solution)/shard_map/ppermute | solution.py:906
  348.3 29.5 %collective-permute-start.46 = (bf16[3,128,1024]{2,1,0:T(8,128)(2,1)S(1)}, bf16[3,128,1024]{2,1,0:T(8,128)(2,1)S(1)}, u32[]{:S(2)}, u32[]{:S(2)}) collective-permute-start(bf16[3,128,1024]{2,1,0:T(8,128)(2,1)S(1)} %slice.538), channel_id=1, source_target_pairs={{0,8},{4,12},{8,0},{12,4},{1,9},{5,13},{9,1},{13,5},{2,10},{6,14},... | collective-permute-start | bytes 2359304 | tf_op jit(solution)/shard_map/ppermute | solution.py:906
  373.9 22.1 %collective-permute-start.52 = (bf16[128,1024]{0,1:T(8,128)(2,1)}, bf16[128,1024]{0,1:T(8,128)(2,1)}, u32[]{:S(2)}, u32[]{:S(2)}) collective-permute-start(bf16[128,1024]{0,1:T(8,128)(2,1)} %get-tuple-element.444), channel_id=1, source_target_pairs={{0,1},{1,2},{2,3},{3,0},{4,5},{5,6},{6,7},{7,4},{8,9},{9,10},{10,1... | collective-permute-start | bytes 786440 | tf_op jit(solution)/shard_map/ppermute | solution.py:1091
  374.0 22.2 %collective-permute-start.53 = (bf16[128,1024]{0,1:T(8,128)(2,1)}, bf16[128,1024]{0,1:T(8,128)(2,1)}, u32[]{:S(2)}, u32[]{:S(2)}) collective-permute-start(bf16[128,1024]{0,1:T(8,128)(2,1)} %get-tuple-element.443), channel_id=1, source_target_pairs={{0,2},{1,3},{2,0},{3,1},{4,6},{5,7},{6,4},{7,5},{8,10},{9,11},{10,... | collective-permute-start | bytes 786440 | tf_op jit(solution)/shard_map/ppermute | solution.py:1091
  375.6 20.6 %collective-permute-start.54 = (bf16[128,1024]{0,1:T(8,128)(2,1)}, bf16[128,1024]{0,1:T(8,128)(2,1)}, u32[]{:S(2)}, u32[]{:S(2)}) collective-permute-start(bf16[128,1024]{0,1:T(8,128)(2,1)} %get-tuple-element.442), channel_id=1, source_target_pairs={{0,3},{1,0},{2,1},{3,2},{4,7},{5,4},{6,5},{7,6},{8,11},{9,8},{10,9... | collective-permute-start | bytes 786440 | tf_op jit(solution)/shard_map/ppermute | solution.py:1091
  383.7 15.7 %collective-permute-start.49 = (bf16[1,128,1024]{2,1,0:T(8,128)(2,1)S(1)}, bf16[1,128,1024]{2,1,0:T(8,128)(2,1)S(1)}, u32[]{:S(2)}, u32[]{:S(2)}) collective-permute-start(bf16[1,128,1024]{2,1,0:T(8,128)(2,1)S(1)} %copy-done.134), channel_id=1, source_target_pairs={{0,8},{4,12},{8,0},{12,4},{1,9},{5,13},{9,1},{13,5},{2,10},{6,14},... | collective-permute-start | bytes 786440 | tf_op jit(solution)/shard_map/ppermute | solution.py:906
  391.9 15.2 %collective-permute-start.58 = (bf16[512,512]{1,0:T(8,128)(2,1)}, bf16[512,512]{1,0:T(8,128)(2,1)}, u32[]{:S(2)}, u32[]{:S(2)}) collective-permute-start(bf16[512,512]{1,0:T(8,128)(2,1)} %constant_dynamic-slice_fusion.7), channel_id=1, source_target_pairs={{0,16},{16,0},{1,17},{17,1},{2,18},{18,2},{3,19},{19,3},{4,20},{20... | collective-permute-start | bytes 1572872 | tf_op jit(solution)/shard_map/ppermute | solution.py:906
  396.1 26.8 %collective-permute-start.62 = (bf16[512,640]{1,0:T(8,128)(2,1)}, bf16[512,640]{1,0:T(8,128)(2,1)}, u32[]{:S(2)}, u32[]{:S(2)}) collective-permute-start(bf16[512,640]{1,0:T(8,128)(2,1)} %constant_dynamic-slice_fusion.6), channel_id=1, source_target_pairs={{0,16},{16,0},{1,17},{17,1},{2,18},{18,2},{3,19},{19,3},{4,20},{20... | collective-permute-start | bytes 1966088 | tf_op jit(solution)/shard_map/ppermute | solution.py:906
  396.2 22.0 %collective-permute-start.59 = (bf16[1,256,1024]{2,1,0:T(8,128)(2,1)}, bf16[1,256,1024]{2,1,0:T(8,128)(2,1)}, u32[]{:S(2)}, u32[]{:S(2)}) collective-permute-start(bf16[1,256,1024]{2,1,0:T(8,128)(2,1)} %pad_maximum_fusion.13), channel_id=1, source_target_pairs={{0,4},{4,0},{8,12},{12,8},{1,5},{5,1},{9,13},{13,9},{2,6},{6,2},{1... | collective-permute-start | bytes 1572872 | tf_op jit(solution)/shard_map/ppermute | solution.py:906
  398.1 17.6 %collective-permute-start.56 = (bf16[1,128,1024]{2,1,0:T(8,128)(2,1)}, bf16[1,128,1024]{2,1,0:T(8,128)(2,1)}, u32[]{:S(2)}, u32[]{:S(2)}) collective-permute-start(bf16[1,128,1024]{2,1,0:T(8,128)(2,1)} %slice.540), channel_id=1, source_target_pairs={{0,8},{4,12},{8,0},{12,4},{1,9},{5,13},{9,1},{13,5},{2,10},{6,14},... | collective-permute-start | bytes 786440 | tf_op jit(solution)/shard_map/ppermute | solution.py:906
  399.3 14.2 %collective-permute-start.57 = (f32[152,128]{1,0:T(8,128)}, f32[152,128]{1,0:T(8,128)}, u32[]{:S(2)}, u32[]{:S(2)}) collective-permute-start(f32[152,128]{1,0:T(8,128)} %fusion.79), channel_id=1, source_target_pairs={{0,8},{4,12},{8,0},{12,4},{1,9},{5,13},{9,1},{13,5},{2,10},{6,14},... | collective-permute-start | bytes 233480 | tf_op jit(solution)/shard_map/ppermute | solution.py:906
  409.2 22.1 %collective-permute-start.63 = (bf16[128,512]{1,0:T(8,128)(2,1)}, bf16[128,512]{1,0:T(8,128)(2,1)}, u32[]{:S(2)}, u32[]{:S(2)}) collective-permute-start(bf16[128,512]{1,0:T(8,128)(2,1)} %get-tuple-element.463), channel_id=1, source_target_pairs={{0,1},{1,2},{2,3},{3,0},{4,5},{5,6},{6,7},{7,4},{8,9},{9,10},{10,1... | collective-permute-start | bytes 393224 | tf_op jit(solution)/shard_map/ppermute | solution.py:1091
  413.5 19.9 %collective-permute-start.64 = (bf16[128,512]{1,0:T(8,128)(2,1)}, bf16[128,512]{1,0:T(8,128)(2,1)}, u32[]{:S(2)}, u32[]{:S(2)}) collective-permute-start(bf16[128,512]{1,0:T(8,128)(2,1)} %get-tuple-element.462), channel_id=1, source_target_pairs={{0,2},{1,3},{2,0},{3,1},{4,6},{5,7},{6,4},{7,5},{8,10},{9,11},{10,... | collective-permute-start | bytes 393224 | tf_op jit(solution)/shard_map/ppermute | solution.py:1091
  418.2 17.3 %collective-permute-start.65 = (bf16[128,512]{1,0:T(8,128)(2,1)}, bf16[128,512]{1,0:T(8,128)(2,1)S(1)}, u32[]{:S(2)}, u32[]{:S(2)}) collective-permute-start(bf16[128,512]{1,0:T(8,128)(2,1)} %get-tuple-element.461), channel_id=1, source_target_pairs={{0,3},{1,0},{2,1},{3,2},{4,7},{5,4},{6,5},{7,6},{8,11},{9,8},{10,9... | collective-permute-start | bytes 393224 | tf_op jit(solution)/shard_map/ppermute | solution.py:1091
  425.3 25.6 %collective-permute-start.66 = (bf16[128,640]{1,0:T(8,128)(2,1)S(1)}, bf16[128,640]{1,0:T(8,128)(2,1)}, u32[]{:S(2)}, u32[]{:S(2)}) collective-permute-start(bf16[128,640]{1,0:T(8,128)(2,1)S(1)} %get-tuple-element.447), channel_id=1, source_target_pairs={{0,1},{1,2},{2,3},{3,0},{4,5},{5,6},{6,7},{7,4},{8,9},{9,10},{10,1... | collective-permute-start | bytes 491528 | tf_op jit(solution)/shard_map/ppermute | solution.py:1091
  431.2 19.7 %collective-permute-start.67 = (bf16[128,640]{1,0:T(8,128)(2,1)S(1)}, bf16[128,640]{1,0:T(8,128)(2,1)S(1)}, u32[]{:S(2)}, u32[]{:S(2)}) collective-permute-start(bf16[128,640]{1,0:T(8,128)(2,1)S(1)} %get-tuple-element.446), channel_id=1, source_target_pairs={{0,2},{1,3},{2,0},{3,1},{4,6},{5,7},{6,4},{7,5},{8,10},{9,11},{10,... | collective-permute-start | bytes 491528 | tf_op jit(solution)/shard_map/ppermute | solution.py:1091
  433.4 17.5 %collective-permute-start.68 = (bf16[128,640]{1,0:T(8,128)(2,1)S(1)}, bf16[128,640]{1,0:T(8,128)(2,1)S(1)}, u32[]{:S(2)}, u32[]{:S(2)}) collective-permute-start(bf16[128,640]{1,0:T(8,128)(2,1)S(1)} %get-tuple-element.445), channel_id=1, source_target_pairs={{0,3},{1,0},{2,1},{3,2},{4,7},{5,4},{6,5},{7,6},{8,11},{9,8},{10,9... | collective-permute-start | bytes 491528 | tf_op jit(solution)/shard_map/ppermute | solution.py:1091
  (176 other events, 1192.7 us)
Sparse Core Ops, SparseCore 0:
  74.2 83.8 all-gather.2
  259.2 101.1 reduce-scatter.1

commit v3 on v2

--- a/solution.py
+++ b/solution.py
@@ -727,7 +727,7 @@
             out_specs=out_specs,
         ),
         out_shape=out_shape,
-        compiler_params=kernel_params(2, 12),
+        compiler_params=kernel_params(2, 10),
         cost_estimate=busy(10.0 * micros),
         name="mixer_local",
     )(ends, pre, pre, pre, pre, *filters, params)
@@ -849,7 +849,7 @@
         [],
         "feed_forward",
         9.0,
-        20,
+        17,
     )
 
 
@@ -1037,25 +1037,24 @@
 class SmallSum:
     def __init__(self, value):
         self.value = value
-        self.left = []
-        for axis in ("head", "seq", "fsdp"):
-            bit = 1
-            while bit < lax.axis_size(axis):
-                self.left.append((axis, bit))
-                bit *= 2
-        self.got = None
+        self.left = ["head", "seq", "fsdp"]
+        self.got = []
 
     def step(self, *waits):
-        if self.got is not None:
-            self.value = self.value + after(self.got, *waits)
-            self.got = None
+        for got in self.got:
+            self.value = self.value + after(got, *waits)
+        self.got = []
         if self.left:
-            axis, bit = self.left.pop(0)
-            self.got = swapped(self.value, axis, bit)
+            axis = self.left.pop(0)
+            devices = lax.axis_size(axis)
+            self.got = [
+                lax.ppermute(self.value, axis, [(i, (i + away) % devices) for i in range(devices)])
+                for away in range(1, devices)
+            ]
         return self.value
 
     def finish(self, *waits):
-        while self.got is not None:
+        while self.got:
             self.step(*waits)
         return self.value
 
@@ -1419,7 +1418,6 @@
     small_sum = SmallSum(packed)
     small_sum.step()
     side_shard = side.finish(small_sum.value)
-    small_sum.step(side_shard)
     to_end(0, d_h_sums[0].finish(small_sum.value))
     ff_shard = [ff_shard[0].T, ff_shard[1].T, ff_shard[2]]
     mix[0].spread(side_shard, block_output, dx_parts[0])

time: 470 us -> 468 us (level)
    ppermute x46 -> x41, waiting for transfers between devices: 32.1 us -> 25.3 us  [swapped(): lax.ppermute(block, axis, [(i, i ^ bit) for i in range(lax.axis_size(axis...]
    ppermute x46 -> x41, starting transfers between devices: 31.7 us -> 29.5 us  [swapped(): lax.ppermute(block, axis, [(i, i ^ bit) for i in range(lax.axis_size(axis...]
    unnamed x317 -> x327, local copies, waits for them, and re-layouts: 42.1 us -> 42.7 us
  transfers between devices with their start and end apart: 73 -> 75, of which waited for: 16 -> 17; matrix products, arithmetic and copies ran while one was open for 28% -> 28% of each run, Pallas kernels for 27% -> 27%
where the time goes in v3:
time: 468 us; the launch traced here: 459 us
  Pallas kernels  126 us (27%)
  starting transfers between devices  84.4 us (18%)
  local copies, waits for them, and re-layouts  72.3 us (15%)
  waiting for transfers between devices  59.1 us (13%)
  other arithmetic  53.9 us (12%)
  matrix products  47.3 us (10%)
  between operations  16.9 us (4%)
    pallas_call x12, Pallas kernels, call(): pl.pallas_call(wrapped, grid_spec=pltpu.PrefetchScalarGridSpec(num_scalar...  96.8 us
    unnamed x327, local copies, waits for them, and re-layouts  42.7 us
    ppermute x41, starting transfers between devices, swapped(): lax.ppermute(block, axis, [(i, i ^ bit) for i in range(lax.axis_size(axis...  29.5 us
    pallas_call x3, Pallas kernels, run_local(): pl.pallas_call(local_kernel(heads, with_trans), grid_spec=pltpu.PrefetchS...  26.3 us
    ppermute x41, waiting for transfers between devices, swapped(): lax.ppermute(block, axis, [(i, i ^ bit) for i in range(lax.axis_size(axis...  25.3 us
    dot_general x6, matrix products, grad_of(): lax.dot_general(left, right, (((0,), (0,)), ((), ())), preferred_element_...  22.3 us
    ppermute x10, starting transfers between devices, passed_along(): return lax.ppermute(block, axis, route)  21.8 us
    ppermute x10, waiting for transfers between devices, passed_along(): return lax.ppermute(block, axis, route)  20 us
  transfers between devices with their start and end apart: 75, of which 17 were waited for; matrix products, arithmetic and copies ran while one was open for 28% of the time, Pallas kernels for 27%

profile of v3, /device:TPU:0, one launch (start us, length us, event | category | flops | bytes accessed | tf_op | source)
XLA Modules:
  0.0 459.3 jit_solution(1337065529234779383)
XLA Ops:
  11.0 3.0 collective-permute-start
  14.0 2.6 collective-permute-start.1
  19.5 3.4 collective-permute-start.6
  31.6 2.8 fusion
  39.1 5.4 %collective-permute-done.3.refs_3_ = bf16[128,1152]{1,0:T(8,128)(2,1)S(1)} collective-permute-done((bf16[128,1152]{1,0:T(8,128)(2,1)S(1)}, bf16[128,1152]{1,0:T(8,128)(2,1)S(1)}, u32[]{:S(2)}, u32[]{:S(2)}) %collective-permute-start.3) | collective-permute-done | bytes 294944 | tf_op jit(solution)/shard_map/ppermute | solution.py:906
  50.8 4.0 collective-permute-done.5.refs_5_
  60.0 8.8 %mixer_local.3 = (bf16[1,2,512,128]{3,2,1,0:T(8,128)(2,1)S(1)}, f32[1,512,512]{2,1,0:T(8,128)S(1)}, bf16[1,2,512,128]{3,2,1,0:T(8,128)(2,1)S(1)}, f32[1,2,512,25...) custom-call(s32[1,9]{1,0:T(1,128)S(1)} %get-tuple-element.485.ends_r, ...), custom_call_target="tpu_custom_call" | custom-call | bytes 3300000 | tf_op jit(solution)/shard_map/mixer_local/pallas_call | solution.py:718
  74.3 3.6 fusion.83
  77.9 2.5 collective-permute-start.7
  84.2 8.8 %mixer_local.4 = (bf16[1,2,512,128]{3,2,1,0:T(8,128)(2,1)S(1)}, f32[1,512,512]{2,1,0:T(8,128)S(1)}, bf16[1,2,512,128]{3,2,1,0:T(8,128)(2,1)S(1)}, f32[1,2,512,25...) custom-call(s32[1,9]{1,0:T(1,128)S(1)} %get-tuple-element.483.ends_r, ...), custom_call_target="tpu_custom_call" | custom-call | bytes 3300000 | tf_op jit(solution)/shard_map/mixer_local/pallas_call | solution.py:718
  93.0 3.8 collective-permute-start.16
  96.9 2.6 collective-permute-done.11.refs_3_
  102.8 4.5 mixer_output.3
  109.0 8.8 %mixer_local.5 = (bf16[1,2,512,128]{3,2,1,0:T(8,128)(2,1)S(1)}, f32[1,512,512]{2,1,0:T(8,128)S(1)}, bf16[1,2,512,128]{3,2,1,0:T(8,128)(2,1)S(1)}, f32[1,2,512,25...) custom-call(s32[1,9]{1,0:T(1,128)S(1)} %get-tuple-element.484.ends_r, ...), custom_call_target="tpu_custom_call" | custom-call | bytes 3300000 | tf_op jit(solution)/shard_map/mixer_local/pallas_call | solution.py:718
  121.1 4.4 collective-permute-start.18
  125.6 4.5 mixer_output.4
  131.8 13.0 %mixer_output.5 = (bf16[3,512,512]{2,1,0:T(8,128)(2,1)}, f32[1,512,512]{2,1,0:T(8,128)S(1)}, bf16[1,2,512,256]{3,2,1,0:T(8,128)(2,1)S(1)}, bf16[1,256,1024]{2,1,0:T(8,128)(2,1)S(1)}, bf16[1,256,1024]{2,1,0:T(8,128)(2,1)S(1)}) custom-call(s32[4]{0:T(128)S(1)} %fusion.76.refs_0_, ...), custom_call_target="tpu_custom_call", output_to_operand_aliasing={{0}: (10, {})} | custom-call | bytes 1980000 | tf_op jit(solution)/shard_map/mixer_output/pallas_call | solution.py:650
  151.2 7.0 %all-gather.3.cloned.1.call-done = bf16[12,704,256]{2,1,0:T(8,128)(2,1)} async-done(((bf16[3,704,256]{2,1,0:T(8,128)(2,1)}), bf16[12,704,256]{2,1,0:T(8,128)(2,1)}) %all-gather.3.cloned.1.call-update) | async-done | bytes 4325392 | tf_op jit(solution)/shard_map/all_gather | solution.py:1316
  164.4 6.7 %feed_forward.3 = (bf16[1,256,1024]{2,1,0:T(8,128)(2,1)S(1)}, bf16[1,256,1024]{2,1,0:T(8,128)(2,1)S(1)}, bf16[3,256,1024]{2,1,0:T(8,128)(2,1)}, bf16[3,256,1024]...) custom-call(bf16[1,256,1024]{2,1,0:T(8,128)(2,1)S(1)} %copy-done.27,, ...), custom_call_target="tpu_custom_call" | custom-call | bytes 2970000 | tf_op jit(solution)/shard_map/feed_forward/pallas_call | solution.py:650
  178.2 3.0 collective-permute-done.25
  183.3 6.4 %feed_forward.4 = (bf16[1,256,1024]{2,1,0:T(8,128)(2,1)S(1)}, bf16[1,256,1024]{2,1,0:T(8,128)(2,1)}, bf16[3,256,1024]{2,1,0:T(8,128)(2,1)}, bf16[3,256,1024]{2,1...) custom-call(bf16[1,256,1024]{2,1,0:T(8,128)(2,1)S(1)} %pad_maximum_f, ...), custom_call_target="tpu_custom_call", output_to_operand_aliasing={{2}: (4, {}), {3}: (5, {}), {4}: (6, {}), {5}: (7, {}), {6}... | custom-call | bytes 2970000 | tf_op jit(solution)/shard_map/feed_forward/pallas_call | solution.py:650
  197.9 4.2 collective-permute-done.29
  207.1 6.6 %feed_forward.5 = (bf16[1,256,1024]{2,1,0:T(8,128)(2,1)S(1)}, bf16[1,256,1024]{2,1,0:T(8,128)(2,1)S(1)}, bf16[3,256,1024]{2,1,0:T(8,128)(2,1)}, bf16[3,256,1024]...) custom-call(bf16[1,256,1024]{2,1,0:T(8,128)(2,1)S(1)} %pad_maximum_f, ...), custom_call_target="tpu_custom_call", output_to_operand_aliasing={{2}: (4, {}), {3}: (5, {}), {4}: (6, {}), {5}: (7, {}), {6}... | custom-call | bytes 2970000 | tf_op jit(solution)/shard_map/feed_forward/pallas_call | solution.py:650
  213.7 5.2 %bitcast_convert_fusion.3 = bf16[704,1024]{1,0:T(8,128)(2,1)S(1)} fusion(bf16[3,512,704]{2,1,0:T(8,128)(2,1)} %get-tuple-element.263, bf16[3,512,1024]{2,1,0:T(8,128)(2,1)} %get-tuple-element.264), kind=kOutput, calls=%fused_computation.15 | convolution fusion | flops 2215313408 | bytes 6750208 | tf_op jit(solution)/shard_map/dot_general | solution.py:1144
  220.8 2.5 bitcast_convert_fusion.2
  225.9 3.0 bitcast_convert_fusion.1
  231.2 4.6 mixer_gate_back.3
  240.6 2.3 maximum_bitcast_fusion
  246.0 5.6 %mixer_gate_back.4 = (bf16[1,512,512]{2,1,0:T(8,128)(2,1)S(1)}, f32[1,2,512,256]{3,2,1,0:T(8,128)S(1)}, bf16[3,528,512]{2,1,0:T(8,128)(2,1)}, bf16[3,512,1024]{2...) custom-call(s32[4]{0:T(128)S(1)} %fusion.76.refs_0_, ...), custom_call_target="tpu_custom_call", output_to_operand_aliasing={{2}: (10, {}), {3}: (11, {})} | custom-call | bytes 1980000 | tf_op jit(solution)/shard_map/mixer_gate_back/pallas_call | solution.py:650
  259.3 4.7 %collective-permute-done.41.refs_12_ = bf16[1,2,128,256]{3,2,1,0:T(8,128)(2,1)S(1)} collective-permute-done((bf16[1,2,128,256]{3,2,1,0:T(8,128)(2,1)}, bf16[1,2,128,256]{3,2,1,0:T(8,128)(2,1)S(1)}, u32[]{:S(2)}, u32[]{:S(2)}) %collective-permute-start.41) | collective-permute-done | bytes 131104 | tf_op jit(solution)/shard_map/ppermute | solution.py:902
  270.9 12.9 %mixer_back.3 = (bf16[3,528,1152]{2,1,0:T(8,128)(2,1)}, bf16[1,528,1152]{2,1,0:T(8,128)(2,1)S(1)}, f32[1,8,1152]{2,1,0:T(8,128)S(1)}) custom-call(f32[1,528,1152]{2,1,0:T(8,128)S(1)} %copy-done.7, f32[1,528,1152]{2,1,0:T(8,128)S(1)} %copy-done.7, f32[1,528,1152]{2,1,0:T(8,128)S(1)} %copy-done.7, f32[1,2,8,512]{3,2,1,0:T(8,128)S(1)} %copy-done.81, ...), custom_call_target="tpu_custom_call" | custom-call | bytes 4620000 | tf_op jit(solution)/shard_map/mixer_back/pallas_call | solution.py:650
  285.1 5.7 %mixer_gate_back.5 = (bf16[1,512,512]{2,1,0:T(8,128)(2,1)S(1)}, f32[1,2,512,256]{3,2,1,0:T(8,128)S(1)}, bf16[3,528,512]{2,1,0:T(8,128)(2,1)}, bf16[3,512,1024]{2...) custom-call(s32[4]{0:T(128)S(1)} %fusion.76.refs_0_, ...), custom_call_target="tpu_custom_call", output_to_operand_aliasing={{2}: (10, {}), {3}: (11, {})} | custom-call | bytes 1980000 | tf_op jit(solution)/shard_map/mixer_gate_back/pallas_call | solution.py:650
  302.8 2.8 collective-permute-start.47
  305.6 4.4 collective-permute-done.43.refs_12_
  310.0 13.6 %mixer_back.4 = (bf16[3,528,1152]{2,1,0:T(8,128)(2,1)}, bf16[1,528,1152]{2,1,0:T(8,128)(2,1)S(1)}, f32[1,8,1152]{2,1,0:T(8,128)S(1)}) custom-call(f32[1,528,1152]{2,1,0:T(8,128)S(1)} %copy-done.5, f32[1,528,1152]{2,1,0:T(8,128)S(1)} %copy-done.5, f32[1,528,1152]{2,1,0:T(8,128)S(1)} %copy-done.5, ...), custom_call_target="tpu_custom_call", output_to_operand_aliasing={{0}: (14, {})} | custom-call | bytes 4620000 | tf_op jit(solution)/shard_map/mixer_back/pallas_call | solution.py:650
  325.6 3.0 fusion.89
  328.8 10.7 %collective-permute-done.44 = bf16[1,16,1152]{2,1,0:T(8,128)(2,1)S(1)} collective-permute-done((bf16[1,16,1152]{2,1,0:T(8,128)(2,1)S(1)}, bf16[1,16,1152]{2,1,0:T(8,128)(2,1)S(1)}, u32[]{:S(2)}, u32[]{:S(2)}) %collective-permute-start.44) | collective-permute-done | bytes 36896 | tf_op jit(solution)/shard_map/ppermute | solution.py:902
  340.2 4.3 fusion.8
  353.4 12.7 %mixer_back.5 = (bf16[3,528,1152]{2,1,0:T(8,128)(2,1)}, bf16[1,528,1152]{2,1,0:T(8,128)(2,1)S(1)}, f32[1,8,1152]{2,1,0:T(8,128)S(1)}) custom-call(f32[1,528,1152]{2,1,0:T(8,128)S(1)} %copy-done.3, f32[1,528,1152]{2,1,0:T(8,128)S(1)} %copy-done.3, f32[1,528,1152]{2,1,0:T(8,128)S(1)} %copy-done.3, ...), custom_call_target="tpu_custom_call", output_to_operand_aliasing={{0}: (14, {})} | custom-call | bytes 4620000 | tf_op jit(solution)/shard_map/mixer_back/pallas_call | solution.py:650
  366.1 7.7 %bitcast_convert_fusion = bf16[1024,1152]{1,0:T(8,128)(2,1)S(1)} fusion(bf16[3,528,1024]{2,1,0:T(8,128)(2,1)S(1)} %copy-done.115, bf16[3,528,1152]{2,1,0:T(8,128)(2,1)} %get-tuple-element.330), kind=kOutput, calls=%fused_computation.5 | convolution fusion | flops 3738304512 | bytes 9252864 | tf_op jit(solution)/shard_map/dot_general | solution.py:1144
  383.2 2.4 collective-permute-start.57
  386.3 4.0 fusion.5
  392.1 2.5 collective-permute-start.54
  412.6 2.8 collective-permute-start.65
  417.5 2.7 collective-permute-start.66
  426.9 3.6 collective-permute-done.61
  433.1 2.9 collective-permute-start.68
  445.3 3.5 collective-permute-done.68
  (615 shorter events, 192.3 us)
Async XLA Ops:
  7.2 151.0 %all-gather.3.cloned.1.call-start = ((), (), s32[]{:S(2)}) async-start(), calls=%async_computation.2 | async-start | bytes 5406720 | tf_op jit(solution)/shard_map/all_gather | solution.py:1316
  11.0 23.4 %collective-permute-start = (bf16[128,1152]{1,0:T(8,128)(2,1)}, bf16[128,1152]{1,0:T(8,128)(2,1)S(1)}, u32[]{:S(2)}, u32[]{:S(2)}) collective-permute-start(bf16[128,1152]{1,0:T(8,128)(2,1)} %constant_dynamic-slice_fusion.18), channel_id=1, source_target_pairs={{0,1},{1,2},{2,3},{3,0},{4,5},{5,6},{6,7},{7,4},{8,9},{9,10},{10,1... | collective-permute-start | bytes 884744 | tf_op jit(solution)/shard_map/ppermute | solution.py:995
  14.0 22.0 %collective-permute-start.1 = (bf16[128,1152]{1,0:T(8,128)(2,1)}, bf16[128,1152]{1,0:T(8,128)(2,1)S(1)}, u32[]{:S(2)}, u32[]{:S(2)}) collective-permute-start(bf16[128,1152]{1,0:T(8,128)(2,1)} %constant_dynamic-slice_fusion.18), channel_id=1, source_target_pairs={{0,2},{1,3},{2,0},{3,1},{4,6},{5,7},{6,4},{7,5},{8,10},{9,11},{10,... | collective-permute-start | bytes 884744 | tf_op jit(solution)/shard_map/ppermute | solution.py:995
  16.6 20.9 %collective-permute-start.2 = (bf16[128,1152]{1,0:T(8,128)(2,1)}, bf16[128,1152]{1,0:T(8,128)(2,1)S(1)}, u32[]{:S(2)}, u32[]{:S(2)}) collective-permute-start(bf16[128,1152]{1,0:T(8,128)(2,1)} %constant_dynamic-slice_fusion.18), channel_id=1, source_target_pairs={{0,3},{1,0},{2,1},{3,2},{4,7},{5,4},{6,5},{7,6},{8,11},{9,8},{10,9... | collective-permute-start | bytes 884744 | tf_op jit(solution)/shard_map/ppermute | solution.py:995
  36.0 14.8 %collective-permute-start.4 = (bf16[128,1152]{1,0:T(8,128)(2,1)S(1)}, bf16[128,1152]{1,0:T(8,128)(2,1)S(1)}, u32[]{:S(2)}, u32[]{:S(2)}) collective-permute-start(bf16[128,1152]{1,0:T(8,128)(2,1)S(1)} %collective-permute-done.1.refs_1_), channel_id=1, source_target_pairs={{0,16},{16,0},{1,17},{17,1},{2,18},{18,2},{3,19},{19,3},{4,20},{20... | collective-permute-start | bytes 884744 | tf_op jit(solution)/shard_map/ppermute | solution.py:906
  37.5 17.3 %collective-permute-start.5 = (bf16[128,1152]{1,0:T(8,128)(2,1)S(1)}, bf16[128,1152]{1,0:T(8,128)(2,1)S(1)}, u32[]{:S(2)}, u32[]{:S(2)}) collective-permute-start(bf16[128,1152]{1,0:T(8,128)(2,1)S(1)} %collective-permute-done.2.refs_2_), channel_id=1, source_target_pairs={{0,16},{16,0},{1,17},{17,1},{2,18},{18,2},{3,19},{19,3},{4,20},{20... | collective-permute-start | bytes 884744 | tf_op jit(solution)/shard_map/ppermute | solution.py:906
  44.5 29.0 %collective-permute-start.8 = (bf16[128,1024]{1,0:T(8,128)(2,1)S(1)}, bf16[128,1024]{1,0:T(8,128)(2,1)S(1)}, u32[]{:S(2)}, u32[]{:S(2)}) collective-permute-start(bf16[128,1024]{1,0:T(8,128)(2,1)S(1)} %constant_dynamic-slice_fusion.14), channel_id=1, source_target_pairs={{0,1},{1,2},{2,3},{3,0},{4,5},{5,6},{6,7},{7,4},{8,9},{9,10},{10,1... | collective-permute-start | bytes 786440 | tf_op jit(solution)/shard_map/ppermute | solution.py:995
  45.4 28.7 %collective-permute-start.9 = (bf16[128,1024]{1,0:T(8,128)(2,1)S(1)}, bf16[128,1024]{1,0:T(8,128)(2,1)}, u32[]{:S(2)}, u32[]{:S(2)}) collective-permute-start(bf16[128,1024]{1,0:T(8,128)(2,1)S(1)} %constant_dynamic-slice_fusion.14), channel_id=1, source_target_pairs={{0,2},{1,3},{2,0},{3,1},{4,6},{5,7},{6,4},{7,5},{8,10},{9,11},{10,... | collective-permute-start | bytes 786440 | tf_op jit(solution)/shard_map/ppermute | solution.py:995
  47.5 26.6 %collective-permute-start.10 = (bf16[128,1024]{1,0:T(8,128)(2,1)S(1)}, bf16[128,1024]{1,0:T(8,128)(2,1)}, u32[]{:S(2)}, u32[]{:S(2)}) collective-permute-start(bf16[128,1024]{1,0:T(8,128)(2,1)S(1)} %constant_dynamic-slice_fusion.14), channel_id=1, source_target_pairs={{0,3},{1,0},{2,1},{3,2},{4,7},{5,4},{6,5},{7,6},{8,11},{9,8},{10,9... | collective-permute-start | bytes 786440 | tf_op jit(solution)/shard_map/ppermute | solution.py:995
  74.2 346.3 %reduce-scatter.2.cloned.1.call-start = ((), (), s32[]{:S(2)}) async-start(), calls=%async_computation.1 | async-start | bytes 4866048 | tf_op jit(solution)/shard_map/reduce_scatter | solution.py:1149
  77.9 18.9 %collective-permute-start.7 = (bf16[1,2,128,256]{3,2,1,0:T(8,128)(2,1)S(1)}, bf16[1,2,128,256]{3,2,1,0:T(8,128)(2,1)S(1)}, u32[]{:S(2)}, u32[]{:S(2)}) collective-permute-start(bf16[1,2,128,256]{3,2,1,0:T(8,128)(2,1)S(1)} %copy-done.85), channel_id=1, source_target_pairs={{0,16},{1,17},{2,18},{3,19},{4,20},{5,21},{6,22},{7,23},{8,24},{9,... | collective-permute-start | bytes 393224 | tf_op jit(solution)/shard_map/ppermute | solution.py:902
  80.4 16.5 %collective-permute-start.13 = (bf16[128,1024]{1,0:T(8,128)(2,1)}, bf16[128,1024]{1,0:T(8,128)(2,1)S(1)}, u32[]{:S(2)}, u32[]{:S(2)}) collective-permute-start(bf16[128,1024]{1,0:T(8,128)(2,1)} %collective-permute-done.10.refs_2_), channel_id=1, source_target_pairs={{0,16},{16,0},{1,17},{17,1},{2,18},{18,2},{3,19},{19,3},{4,20},{20... | collective-permute-start | bytes 786440 | tf_op jit(solution)/shard_map/ppermute | solution.py:906
  80.4 16.4 %collective-permute-start.12 = (bf16[128,1024]{1,0:T(8,128)(2,1)}, bf16[128,1024]{1,0:T(8,128)(2,1)S(1)}, u32[]{:S(2)}, u32[]{:S(2)}) collective-permute-start(bf16[128,1024]{1,0:T(8,128)(2,1)} %collective-permute-done.9.refs_1_), channel_id=1, source_target_pairs={{0,16},{16,0},{1,17},{17,1},{2,18},{18,2},{3,19},{19,3},{4,20},{20... | collective-permute-start | bytes 786440 | tf_op jit(solution)/shard_map/ppermute | solution.py:906
  82.5 17.0 %collective-permute-start.11 = (bf16[128,1024]{1,0:T(8,128)(2,1)S(1)}, bf16[128,1024]{1,0:T(8,128)(2,1)S(1)}, u32[]{:S(2)}, u32[]{:S(2)}) collective-permute-start(bf16[128,1024]{1,0:T(8,128)(2,1)S(1)} %copy-done.75), channel_id=1, source_target_pairs={{0,16},{16,0},{1,17},{17,1},{2,18},{18,2},{3,19},{19,3},{4,20},{20... | collective-permute-start | bytes 786440 | tf_op jit(solution)/shard_map/ppermute | solution.py:906
  93.0 32.5 %collective-permute-start.16 = (bf16[1,2,128,256]{3,2,1,0:T(8,128)(2,1)S(1)}, bf16[1,2,128,256]{3,2,1,0:T(8,128)(2,1)S(1)}, u32[]{:S(2)}, u32[]{:S(2)}) collective-permute-start(bf16[1,2,128,256]{3,2,1,0:T(8,128)(2,1)S(1)} %get-tuple-element.209), channel_id=1, source_target_pairs={{0,16},{1,17},{2,18},{3,19},{4,20},{5,21},{6,22},{7,23},{8,24},{9,... | collective-permute-start | bytes 393224 | tf_op jit(solution)/shard_map/ppermute | solution.py:902
  130.1 14.9 %collective-permute-start.17 = (bf16[1,256,1024]{2,1,0:T(8,128)(2,1)S(1)}, bf16[1,256,1024]{2,1,0:T(8,128)(2,1)S(1)}, u32[]{:S(2)}, u32[]{:S(2)}) collective-permute-start(bf16[1,256,1024]{2,1,0:T(8,128)(2,1)S(1)} %get-tuple-element.218), channel_id=1, source_target_pairs={{0,4},{4,0},{8,12},{12,8},{1,5},{5,1},{9,13},{13,9},{2,6},{6,2},{1... | collective-permute-start | bytes 1572872 | tf_op jit(solution)/shard_map/ppermute | solution.py:906
  131.2 15.1 %collective-permute-start.20 = (bf16[1,128,1024]{2,1,0:T(8,128)(2,1)S(1)}, bf16[1,128,1024]{2,1,0:T(8,128)(2,1)S(1)}, u32[]{:S(2)}, u32[]{:S(2)}) collective-permute-start(bf16[1,128,1024]{2,1,0:T(8,128)(2,1)S(1)} %multiply_convert_fusion.2), channel_id=1, source_target_pairs={{0,8},{4,12},{8,0},{12,4},{1,9},{5,13},{9,1},{13,5},{2,10},{6,14},... | collective-permute-start | bytes 786440 | tf_op jit(solution)/shard_map/ppermute | solution.py:906
  147.4 23.7 %collective-permute-start.19 = (bf16[1,128,1024]{2,1,0:T(8,128)(2,1)}, bf16[1,128,1024]{2,1,0:T(8,128)(2,1)}, u32[]{:S(2)}, u32[]{:S(2)}) collective-permute-start(bf16[1,128,1024]{2,1,0:T(8,128)(2,1)} %slice.546), channel_id=1, source_target_pairs={{0,8},{4,12},{8,0},{12,4},{1,9},{5,13},{9,1},{13,5},{2,10},{6,14},... | collective-permute-start | bytes 786440 | tf_op jit(solution)/shard_map/ppermute | solution.py:906
  149.9 24.8 %collective-permute-start.23 = (bf16[1,128,1024]{2,1,0:T(8,128)(2,1)}, bf16[1,128,1024]{2,1,0:T(8,128)(2,1)}, u32[]{:S(2)}, u32[]{:S(2)}) collective-permute-start(bf16[1,128,1024]{2,1,0:T(8,128)(2,1)} %slice.545), channel_id=1, source_target_pairs={{0,8},{4,12},{8,0},{12,4},{1,9},{5,13},{9,1},{13,5},{2,10},{6,14},... | collective-permute-start | bytes 786440 | tf_op jit(solution)/shard_map/ppermute | solution.py:906
  181.4 12.9 %collective-permute-start.24 = (bf16[1,128,1024]{2,1,0:T(8,128)(2,1)}, bf16[1,128,1024]{2,1,0:T(8,128)(2,1)}, u32[]{:S(2)}, u32[]{:S(2)}) collective-permute-start(bf16[1,128,1024]{2,1,0:T(8,128)(2,1)} %multiply_convert_fusion), channel_id=1, source_target_pairs={{0,8},{4,12},{8,0},{12,4},{1,9},{5,13},{9,1},{13,5},{2,10},{6,14},... | collective-permute-start | bytes 786440 | tf_op jit(solution)/shard_map/ppermute | solution.py:906
  197.3 26.0 %collective-permute-start.33 = (bf16[1,128,1024]{2,1,0:T(8,128)(2,1)S(1)}, bf16[1,128,1024]{2,1,0:T(8,128)(2,1)S(1)}, u32[]{:S(2)}, u32[]{:S(2)}) collective-permute-start(bf16[1,128,1024]{2,1,0:T(8,128)(2,1)S(1)} %slice.543), channel_id=1, source_target_pairs={{0,8},{4,12},{8,0},{12,4},{1,9},{5,13},{9,1},{13,5},{2,10},{6,14},... | collective-permute-start | bytes 786440 | tf_op jit(solution)/shard_map/ppermute | solution.py:906
  203.4 16.3 %collective-permute-start.34 = (bf16[1,128,1024]{2,1,0:T(8,128)(2,1)S(1)}, bf16[1,128,1024]{2,1,0:T(8,128)(2,1)S(1)}, u32[]{:S(2)}, u32[]{:S(2)}) collective-permute-start(bf16[1,128,1024]{2,1,0:T(8,128)(2,1)S(1)} %get-tuple-element.427), channel_id=1, source_target_pairs={{0,8},{4,12},{8,0},{12,4},{1,9},{5,13},{9,1},{13,5},{2,10},{6,14},... | collective-permute-start | bytes 786440 | tf_op jit(solution)/shard_map/ppermute | solution.py:906
  219.1 17.5 %collective-permute-start.32 = (bf16[1,128,1024]{2,1,0:T(8,128)(2,1)S(1)}, bf16[1,128,1024]{2,1,0:T(8,128)(2,1)S(1)}, u32[]{:S(2)}, u32[]{:S(2)}) collective-permute-start(bf16[1,128,1024]{2,1,0:T(8,128)(2,1)S(1)} %slice.542), channel_id=1, source_target_pairs={{0,8},{4,12},{8,0},{12,4},{1,9},{5,13},{9,1},{13,5},{2,10},{6,14},... | collective-permute-start | bytes 786440 | tf_op jit(solution)/shard_map/ppermute | solution.py:906
  238.5 14.9 %collective-permute-start.37 = (bf16[1,128,1024]{2,1,0:T(8,128)(2,1)}, bf16[1,128,1024]{2,1,0:T(8,128)(2,1)}, u32[]{:S(2)}, u32[]{:S(2)}) collective-permute-start(bf16[1,128,1024]{2,1,0:T(8,128)(2,1)} %get-tuple-element.423), channel_id=1, source_target_pairs={{0,8},{4,12},{8,0},{12,4},{1,9},{5,13},{9,1},{13,5},{2,10},{6,14},... | collective-permute-start | bytes 786440 | tf_op jit(solution)/shard_map/ppermute | solution.py:906
  254.5 30.6 %collective-permute-start.40 = (bf16[1,256,1024]{2,1,0:T(8,128)(2,1)S(1)}, bf16[1,256,1024]{2,1,0:T(8,128)(2,1)}, u32[]{:S(2)}, u32[]{:S(2)}) collective-permute-start(bf16[1,256,1024]{2,1,0:T(8,128)(2,1)S(1)} %pad_maximum_fusion.10.refs_1_), channel_id=1, source_target_pairs={{0,4},{4,0},{8,12},{12,8},{1,5},{5,1},{9,13},{13,9},{2,6},{6,2},{1... | collective-permute-start | bytes 1572872 | tf_op jit(solution)/shard_map/ppermute | solution.py:906
  256.9 28.2 %collective-permute-start.39 = (bf16[1,2,128,256]{3,2,1,0:T(8,128)(2,1)}, bf16[1,2,128,256]{3,2,1,0:T(8,128)(2,1)}, u32[]{:S(2)}, u32[]{:S(2)}) collective-permute-start(bf16[1,2,128,256]{3,2,1,0:T(8,128)(2,1)} %get-tuple-element.284), channel_id=1, source_target_pairs={{16,0},{17,1},{18,2},{19,3},{20,4},{21,5},{22,6},{23,7},{24,8},{25... | collective-permute-start | bytes 393224 | tf_op jit(solution)/shard_map/ppermute | solution.py:902
  258.8 87.5 %collective-permute-start.42 = (bf16[3,256,1024]{2,1,0:T(8,128)(2,1)}, bf16[3,256,1024]{2,1,0:T(8,128)(2,1)}, u32[]{:S(2)}, u32[]{:S(2)}) collective-permute-start(bf16[3,256,1024]{2,1,0:T(8,128)(2,1)} %get-tuple-element.300), channel_id=1, source_target_pairs={{0,4},{4,0},{8,12},{12,8},{1,5},{5,1},{9,13},{13,9},{2,6},{6,2},{1... | collective-permute-start | bytes 4718600 | tf_op jit(solution)/shard_map/ppermute | solution.py:906
  283.8 39.8 %collective-permute-start.45 = (bf16[1,16,1152]{2,1,0:T(8,128)(2,1)S(1)}, bf16[1,16,1152]{2,1,0:T(8,128)(2,1)S(1)}, u32[]{:S(2)}, u32[]{:S(2)}) collective-permute-start(bf16[1,16,1152]{2,1,0:T(8,128)(2,1)S(1)} %slice.302), channel_id=1, source_target_pairs={{16,0},{17,1},{18,2},{19,3},{20,4},{21,5},{22,6},{23,7},{24,8},{25... | collective-permute-start | bytes 110600 | tf_op jit(solution)/shard_map/ppermute | solution.py:902
  302.8 46.8 %collective-permute-start.47 = (bf16[512,1024]{0,1:T(8,128)(2,1)S(1)}, bf16[512,1024]{0,1:T(8,128)(2,1)S(1)}, u32[]{:S(2)}, u32[]{:S(2)}) collective-permute-start(bf16[512,1024]{0,1:T(8,128)(2,1)S(1)} %fusion.27), channel_id=1, source_target_pairs={{0,16},{16,0},{1,17},{17,1},{2,18},{18,2},{3,19},{19,3},{4,20},{20... | collective-permute-start | bytes 3145736 | tf_op jit(solution)/shard_map/ppermute | solution.py:906
  324.3 15.2 %collective-permute-start.44 = (bf16[1,16,1152]{2,1,0:T(8,128)(2,1)S(1)}, bf16[1,16,1152]{2,1,0:T(8,128)(2,1)S(1)}, u32[]{:S(2)}, u32[]{:S(2)}) collective-permute-start(bf16[1,16,1152]{2,1,0:T(8,128)(2,1)S(1)} %slice.299), channel_id=1, source_target_pairs={{16,0},{17,1},{18,2},{19,3},{20,4},{21,5},{22,6},{23,7},{24,8},{25... | collective-permute-start | bytes 110600 | tf_op jit(solution)/shard_map/ppermute | solution.py:902
  328.7 22.3 %collective-permute-start.48 = (bf16[1,256,1024]{2,1,0:T(8,128)(2,1)S(1)}, bf16[1,256,1024]{2,1,0:T(8,128)(2,1)S(1)}, u32[]{:S(2)}, u32[]{:S(2)}) collective-permute-start(bf16[1,256,1024]{2,1,0:T(8,128)(2,1)S(1)} %pad_maximum_fusion.11), channel_id=1, source_target_pairs={{0,4},{4,0},{8,12},{12,8},{1,5},{5,1},{9,13},{13,9},{2,6},{6,2},{1... | collective-permute-start | bytes 1572872 | tf_op jit(solution)/shard_map/ppermute | solution.py:906
  346.3 45.8 %collective-permute-start.51 = (bf16[1,256,1024]{2,1,0:T(8,128)(2,1)}, bf16[1,256,1024]{2,1,0:T(8,128)(2,1)}, u32[]{:S(2)}, u32[]{:S(2)}) collective-permute-start(bf16[1,256,1024]{2,1,0:T(8,128)(2,1)} %pad_maximum_fusion.12), channel_id=1, source_target_pairs={{0,4},{4,0},{8,12},{12,8},{1,5},{5,1},{9,13},{13,9},{2,6},{6,2},{1... | collective-permute-start | bytes 1572872 | tf_op jit(solution)/shard_map/ppermute | solution.py:906
  348.5 28.9 %collective-permute-start.46 = (bf16[3,128,1024]{2,1,0:T(8,128)(2,1)S(1)}, bf16[3,128,1024]{2,1,0:T(8,128)(2,1)S(1)}, u32[]{:S(2)}, u32[]{:S(2)}) collective-permute-start(bf16[3,128,1024]{2,1,0:T(8,128)(2,1)S(1)} %slice.538), channel_id=1, source_target_pairs={{0,8},{4,12},{8,0},{12,4},{1,9},{5,13},{9,1},{13,5},{2,10},{6,14},... | collective-permute-start | bytes 2359304 | tf_op jit(solution)/shard_map/ppermute | solution.py:906
  374.1 23.3 %collective-permute-start.49 = (bf16[1,128,1024]{2,1,0:T(8,128)(2,1)}, bf16[1,128,1024]{2,1,0:T(8,128)(2,1)S(1)}, u32[]{:S(2)}, u32[]{:S(2)}) collective-permute-start(bf16[1,128,1024]{2,1,0:T(8,128)(2,1)} %slice.541), channel_id=1, source_target_pairs={{0,8},{4,12},{8,0},{12,4},{1,9},{5,13},{9,1},{13,5},{2,10},{6,14},... | collective-permute-start | bytes 786440 | tf_op jit(solution)/shard_map/ppermute | solution.py:906
  375.1 22.3 %collective-permute-start.55 = (bf16[128,1024]{0,1:T(8,128)(2,1)}, bf16[128,1024]{0,1:T(8,128)(2,1)}, u32[]{:S(2)}, u32[]{:S(2)}) collective-permute-start(bf16[128,1024]{0,1:T(8,128)(2,1)} %get-tuple-element.446), channel_id=1, source_target_pairs={{0,1},{1,2},{2,3},{3,0},{4,5},{5,6},{6,7},{7,4},{8,9},{9,10},{10,1... | collective-permute-start | bytes 786440 | tf_op jit(solution)/shard_map/ppermute | solution.py:1090
  375.1 22.3 %collective-permute-start.56 = (bf16[128,1024]{0,1:T(8,128)(2,1)}, bf16[128,1024]{0,1:T(8,128)(2,1)}, u32[]{:S(2)}, u32[]{:S(2)}) collective-permute-start(bf16[128,1024]{0,1:T(8,128)(2,1)} %get-tuple-element.445), channel_id=1, source_target_pairs={{0,2},{1,3},{2,0},{3,1},{4,6},{5,7},{6,4},{7,5},{8,10},{9,11},{10,... | collective-permute-start | bytes 786440 | tf_op jit(solution)/shard_map/ppermute | solution.py:1090
  383.2 14.6 %collective-permute-start.57 = (bf16[128,1024]{0,1:T(8,128)(2,1)S(1)}, bf16[128,1024]{0,1:T(8,128)(2,1)S(1)}, u32[]{:S(2)}, u32[]{:S(2)}) collective-permute-start(bf16[128,1024]{0,1:T(8,128)(2,1)S(1)} %copy-done.134), channel_id=1, source_target_pairs={{0,3},{1,0},{2,1},{3,2},{4,7},{5,4},{6,5},{7,6},{8,11},{9,8},{10,9... | collective-permute-start | bytes 786440 | tf_op jit(solution)/shard_map/ppermute | solution.py:1090
  392.1 15.6 %collective-permute-start.54 = (bf16[512,512]{1,0:T(8,128)(2,1)}, bf16[512,512]{1,0:T(8,128)(2,1)}, u32[]{:S(2)}, u32[]{:S(2)}) collective-permute-start(bf16[512,512]{1,0:T(8,128)(2,1)} %constant_dynamic-slice_fusion.7), channel_id=1, source_target_pairs={{0,16},{16,0},{1,17},{17,1},{2,18},{18,2},{3,19},{19,3},{4,20},{20... | collective-permute-start | bytes 1572872 | tf_op jit(solution)/shard_map/ppermute | solution.py:906
  397.4 25.3 %collective-permute-start.63 = (bf16[512,640]{1,0:T(8,128)(2,1)}, bf16[512,640]{1,0:T(8,128)(2,1)}, u32[]{:S(2)}, u32[]{:S(2)}) collective-permute-start(bf16[512,640]{1,0:T(8,128)(2,1)} %constant_dynamic-slice_fusion.6), channel_id=1, source_target_pairs={{0,16},{16,0},{1,17},{17,1},{2,18},{18,2},{3,19},{19,3},{4,20},{20... | collective-permute-start | bytes 1966088 | tf_op jit(solution)/shard_map/ppermute | solution.py:906
  397.4 13.1 %collective-permute-start.53 = (f32[152,128]{1,0:T(8,128)}, f32[152,128]{1,0:T(8,128)}, u32[]{:S(2)}, u32[]{:S(2)}) collective-permute-start(f32[152,128]{1,0:T(8,128)} %pad_bitcast_fusion), channel_id=1, source_target_pairs={{0,4},{4,8},{8,12},{12,0},{1,5},{5,9},{9,13},{13,1},{2,6},{6,10},{... | collective-permute-start | bytes 233480 | tf_op jit(solution)/shard_map/ppermute | solution.py:1051
  397.5 13.0 %collective-permute-start.58 = (f32[152,128]{1,0:T(8,128)}, f32[152,128]{1,0:T(8,128)}, u32[]{:S(2)}, u32[]{:S(2)}) collective-permute-start(f32[152,128]{1,0:T(8,128)} %pad_bitcast_fusion), channel_id=1, source_target_pairs={{0,8},{4,12},{8,0},{12,4},{1,9},{5,13},{9,1},{13,5},{2,10},{6,14},... | collective-permute-start | bytes 233480 | tf_op jit(solution)/shard_map/ppermute | solution.py:1051
  397.9 14.8 %collective-permute-start.59 = (f32[152,128]{1,0:T(8,128)}, f32[152,128]{1,0:T(8,128)}, u32[]{:S(2)}, u32[]{:S(2)}) collective-permute-start(f32[152,128]{1,0:T(8,128)} %pad_bitcast_fusion), channel_id=1, source_target_pairs={{0,12},{4,0},{8,4},{12,8},{1,13},{5,1},{9,5},{13,9},{2,14},{6,2},{... | collective-permute-start | bytes 233480 | tf_op jit(solution)/shard_map/ppermute | solution.py:1051
  410.5 20.5 %collective-permute-start.64 = (bf16[128,512]{1,0:T(8,128)(2,1)}, bf16[128,512]{1,0:T(8,128)(2,1)}, u32[]{:S(2)}, u32[]{:S(2)}) collective-permute-start(bf16[128,512]{1,0:T(8,128)(2,1)} %get-tuple-element.465), channel_id=1, source_target_pairs={{0,1},{1,2},{2,3},{3,0},{4,5},{5,6},{6,7},{7,4},{8,9},{9,10},{10,1... | collective-permute-start | bytes 393224 | tf_op jit(solution)/shard_map/ppermute | solution.py:1090
  412.6 19.6 %collective-permute-start.65 = (bf16[128,512]{1,0:T(8,128)(2,1)}, bf16[128,512]{1,0:T(8,128)(2,1)}, u32[]{:S(2)}, u32[]{:S(2)}) collective-permute-start(bf16[128,512]{1,0:T(8,128)(2,1)} %get-tuple-element.464), channel_id=1, source_target_pairs={{0,2},{1,3},{2,0},{3,1},{4,6},{5,7},{6,4},{7,5},{8,10},{9,11},{10,... | collective-permute-start | bytes 393224 | tf_op jit(solution)/shard_map/ppermute | solution.py:1090
  417.5 15.5 %collective-permute-start.66 = (bf16[128,512]{1,0:T(8,128)(2,1)}, bf16[128,512]{1,0:T(8,128)(2,1)S(1)}, u32[]{:S(2)}, u32[]{:S(2)}) collective-permute-start(bf16[128,512]{1,0:T(8,128)(2,1)} %get-tuple-element.463), channel_id=1, source_target_pairs={{0,3},{1,0},{2,1},{3,2},{4,7},{5,4},{6,5},{7,6},{8,11},{9,8},{10,9... | collective-permute-start | bytes 393224 | tf_op jit(solution)/shard_map/ppermute | solution.py:1090
  426.8 12.3 %collective-permute-start.70 = (f32[152,128]{1,0:T(8,128)S(1)}, f32[152,128]{1,0:T(8,128)S(1)}, u32[]{:S(2)}, u32[]{:S(2)}) collective-permute-start(f32[152,128]{1,0:T(8,128)S(1)} %add.550), channel_id=1, source_target_pairs={{0,1},{1,2},{2,3},{3,0},{4,5},{5,6},{6,7},{7,4},{8,9},{9,10},{10,1... | collective-permute-start | bytes 233480 | tf_op jit(solution)/shard_map/ppermute | solution.py:1051
  432.2 13.1 %collective-permute-start.67 = (bf16[128,640]{1,0:T(8,128)(2,1)S(1)}, bf16[128,640]{1,0:T(8,128)(2,1)S(1)}, u32[]{:S(2)}, u32[]{:S(2)}) collective-permute-start(bf16[128,640]{1,0:T(8,128)(2,1)S(1)} %get-tuple-element.449), channel_id=1, source_target_pairs={{0,1},{1,2},{2,3},{3,0},{4,5},{5,6},{6,7},{7,4},{8,9},{9,10},{10,1... | collective-permute-start | bytes 491528 | tf_op jit(solution)/shard_map/ppermute | solution.py:1090
  433.1 15.8 %collective-permute-start.68 = (bf16[128,640]{1,0:T(8,128)(2,1)S(1)}, bf16[128,640]{1,0:T(8,128)(2,1)S(1)}, u32[]{:S(2)}, u32[]{:S(2)}) collective-permute-start(bf16[128,640]{1,0:T(8,128)(2,1)S(1)} %get-tuple-element.448), channel_id=1, source_target_pairs={{0,2},{1,3},{2,0},{3,1},{4,6},{5,7},{6,4},{7,5},{8,10},{9,11},{10,... | collective-permute-start | bytes 491528 | tf_op jit(solution)/shard_map/ppermute | solution.py:1090
  (183 other events, 1245.6 us)
Sparse Core Ops, SparseCore 0:
  74.3 83.8 all-gather.2
  259.4 101.0 reduce-scatter.1
